TPU v7x, 256 devices: a whole 4x4x8 slice. The times are simulated.
256 devices in a mesh: row: 8 (over x_hi, y), col: 32 (over x_lo, z, core).
Axes of the slice: x: 4 (x_hi: 2, x_lo: 2; x = x_hi * 2 + x_lo), y: 4, z: 8, core: 2. Of those that a mesh axis runs over, the one named last changes fastest.
Arguments:
- orbitals: bfloat16 [16384, 1024], P('row', 'col'), may hold values from -0.1875 to 0.1875
- kernel: bfloat16 [16384, 16384], P('col', 'row'), may hold values from -6 to 6
- applied: bfloat16 [16384, 512], P('col', 'row'), may hold values from -1.5 to 1.5
- fit: bfloat16 [16384, 65536], P('row', 'col'), may hold values from -0.046875 to 0.046875
Outputs:
- exchange_term: bfloat16 [512, 65536], P('row', 'col')
All inputs are finite; a program needn't handle non-finite values.
Results may differ from a plain program's by a relative error of at most 0.0058.
Values may be sent and summed in bfloat16 or wider, within the bound.
No kernel may reach another device: no remote copies, remote signals or barrier semaphores. Data moves between devices by JAX's collectives and lax.ppermute only.
A program may use at most 64 MiB of HBM per device.

v0:
```python
import jax
import jax.numpy as jnp
from jax import lax
from jax.sharding import PartitionSpec as P


def per_device(orbitals, kernel, applied, fit):
    columns = lax.all_gather(orbitals, "row", axis=0, tiled=True)
    nearby = lax.all_to_all(columns, "col", split_axis=0, concat_axis=1, tiled=True)
    density = lax.dot_general(
        nearby,
        lax.all_gather(orbitals, "col", axis=1, tiled=True),
        (((1,), (1,)), ((), ())),
        preferred_element_type=jnp.float32,
    )
    weighted = (density * kernel.astype(jnp.float32)).astype(jnp.bfloat16)
    partial_sum = lax.dot_general(
        weighted,
        lax.all_gather(applied, "row", axis=1, tiled=True),
        (((0,), (0,)), ((), ())),
        preferred_element_type=jnp.float32,
    )
    projected = lax.psum(partial_sum, "col")
    projected_low = projected.astype(jnp.bfloat16)
    result = lax.psum_scatter(
        -lax.dot_general(
            projected_low, fit, (((0,), (0,)), ((), ())), preferred_element_type=jnp.float32
        ),
        "row",
        scatter_dimension=0,
        tiled=True,
    )
    return result.astype(jnp.bfloat16)


def solution(mesh):
    return jax.shard_map(
        per_device,
        mesh=mesh,
        in_specs=(P("row", "col"), P("col", "row"), P("col", "row"), P("row", "col")),
        out_specs=P("row", "col"),
        check_vma=False,
    )
```

profile of v0, /device:TPU:8, one launch (start us, length us, event | category | flops | bytes accessed | tf_op | source)
XLA Modules:
  0.0 383.5 jit_solution(3494709787726680160)
XLA Ops:
  6.5 0.0 copy-start
  6.5 0.0 all-gather.3.cloned.1.call-start
  6.5 0.7 all-gather.3.cloned.1.call-update
  7.3 0.0 all-gather.5.cloned.1.call-start
  7.3 0.7 all-gather.5.cloned.1.call-update
  8.0 55.9 %all-gather.3.cloned.1.call-done = bf16[16384,32]{0,1:T(8,128)(2,1)} async-done(((bf16[2048,32]{0,1:T(8,128)(2,1)}), bf16[16384,32]{0,1:T(8,128)(2,1)}) %all-gather.3.cloned.1.call-update) | async-done | bytes 1048592 | tf_op jit(solution)/shard_map/all_gather | solution.py:8
  63.9 2.4 copy.9
  66.3 7.4 %all-to-all-start = ((bf16[32,512,32]{1,2,0:T(8,128)(2,1)}), bf16[32,512,32]{1,2,0:T(8,128)(2,1)S(1)}, u32[]{:S(2)}, u32[]{:S(2)}) async-start(bf16[32,512,32]{1,2,0:T(8,128)(2,1)} %bitcast.11), calls=%async_computation | async-start | bytes 2097152 | tf_op jit(solution)/shard_map/all_to_all | solution.py:9
  73.7 0.0 reduce-scatter.2.cloned.1.call-start
  73.8 0.0 copy-done
  73.8 37.0 %all_gather.11 = bf16[512,512]{0,1:T(8,128)(2,1)S(1)} all-gather(bf16[512,64]{0,1:T(8,128)(2,1)S(1)} %copy-done), channel_id=1, replica_groups=mesh['row'=8,'col'=32] {'row'}, dimensions={1}, use_global_device_ids=true | all-gather | bytes 589824 | tf_op jit(solution)/shard_map/all_gather | solution.py:19
  110.8 0.0 all-to-all-done
  110.8 30.2 %all-gather.5.cloned.1.call-done = bf16[2048,1024]{0,1:T(8,128)(2,1)} async-done(((bf16[2048,32]{0,1:T(8,128)(2,1)}), bf16[2048,1024]{0,1:T(8,128)(2,1)}) %all-gather.5.cloned.1.call-update) | async-done | bytes 4194320 | tf_op jit(solution)/shard_map/all_gather | solution.py:12
  140.9 8.3 %fusion.1 = f32[2048,512]{1,0:T(8,128)} fusion(bf16[512,512]{0,1:T(8,128)(2,1)S(1)} %all_gather.11, bf16[512,2048]{1,0:T(8,128)(2,1)} %param.5, bf16[512,1024]{0,1:T(8,128)(2,1)S(1)} %bitcast.12, bf16[2048,1024]{0,1:T(8,128)(2,1)} %all-gather.5.cloned.1.call-done), kind=kOutput, calls=%fused_computation.3 | convolution fusion | flops 3224371200 | bytes 12058624 | tf_op jit(solution)/shard_map/dot_general | solution.py:17
  149.2 130.4 %all-reduce.1 = bf16[2048,512]{1,0:T(8,128)(2,1)S(1)} all-reduce(f32[2048,512]{1,0:T(8,128)} %fusion.1), channel_id=1, replica_groups=mesh['row'=8,'col'=32] {'col'}, use_global_device_ids=true, to_apply=%region_0.0 | all-reduce | flops 1048576 | bytes 6291456 | tf_op jit(solution)/shard_map/psum | solution.py:23
  279.7 9.5 %convolution_negate_fusion = f32[512,2048]{1,0:T(8,128)} fusion(bf16[2048,2048]{1,0:T(8,128)(2,1)} %param.7, bf16[2048,512]{1,0:T(8,128)(2,1)S(1)} %all-reduce.1), kind=kOutput, calls=%fused_computation.1 | convolution fusion | flops 4296015872 | bytes 14680064 | tf_op jit(solution)/shard_map/dot_general | solution.py:26
  289.1 0.0 reduce-scatter.2.cloned.1.call-update
  289.1 86.1 %reduce-scatter.2.cloned.1.call-done = f32[64,2048]{1,0:T(8,128)} async-done(((f32[512,2048]{1,0:T(8,128)}), f32[64,2048]{1,0:T(8,128)}) %reduce-scatter.2.cloned.1.call-update) | async-done | bytes 524304 | tf_op jit(solution)/shard_map/reduce_scatter | solution.py:25
  375.2 1.8 convert_element_type.15
Async XLA Ops:
  6.5 67.2 %copy-start = (bf16[512,64]{0,1:T(8,128)(2,1)S(1)}, bf16[512,64]{0,1:T(8,128)(2,1)}, u32[]{:S(2)}) copy-start(bf16[512,64]{0,1:T(8,128)(2,1)} %param.6) | copy-start | bytes 196612
  6.5 57.4 %all-gather.3.cloned.1.call-start = ((), (), s32[]{:S(2)}) async-start(), calls=%async_computation.2 | async-start | bytes 1179648 | tf_op jit(solution)/shard_map/all_gather | solution.py:8
  7.3 133.7 %all-gather.5.cloned.1.call-start = ((), (), s32[]{:S(2)}) async-start(), calls=%async_computation.3 | async-start | bytes 4325376 | tf_op jit(solution)/shard_map/all_gather | solution.py:12
  66.3 44.5 %all-to-all-start = ((bf16[32,512,32]{1,2,0:T(8,128)(2,1)}), bf16[32,512,32]{1,2,0:T(8,128)(2,1)S(1)}, u32[]{:S(2)}, u32[]{:S(2)}) async-start(bf16[32,512,32]{1,2,0:T(8,128)(2,1)} %bitcast.11), calls=%async_computation | async-start | bytes 2097152 | tf_op jit(solution)/shard_map/all_to_all | solution.py:9
  73.7 301.5 %reduce-scatter.2.cloned.1.call-start = ((), (), s32[]{:S(2)}) async-start(), calls=%async_computation.4 | async-start | bytes 4718592 | tf_op jit(solution)/shard_map/reduce_scatter | solution.py:25
Sparse Core Ops, SparseCore 0:
  9.9 53.9 all-gather.2
  65.8 75.0 all-gather.4
  289.3 85.8 reduce-scatter.1
where the time goes:
time: 384 us
  waiting for transfers between devices  174 us (45%)
  blocking collectives  167 us (43%)
  matrix products  17.8 us (5%)
  between operations  13.1 us (3%)
  starting transfers between devices  7.49 us (2%)
    psum x1, blocking collectives, per_device(): projected = lax.psum(partial_sum, 'col')  130 us
    reduce_scatter x1, waiting for transfers between devices, per_device(): lax.psum_scatter(-lax.dot_general(projected_low, fit, (((0,), (0,)), ((),...  86.1 us
    all_gather x1, waiting for transfers between devices, per_device(): columns = lax.all_gather(orbitals, 'row', axis=0, tiled=True)  55.9 us
    all_gather x1, blocking collectives, per_device(): lax.all_gather(applied, 'row', axis=1, tiled=True)  37 us
    all_gather x1, waiting for transfers between devices, per_device(): lax.all_gather(orbitals, 'col', axis=1, tiled=True)  30.2 us
    dot_general x1, matrix products, per_device(): lax.dot_general(projected_low, fit, (((0,), (0,)), ((), ())), preferred_e...  9.47 us
    dot_general x1, matrix products, per_device(): lax.dot_general(weighted, lax.all_gather(applied, 'row', axis=1, tiled=Tr...  8.31 us
  transfers between devices with their start and end apart: 4, of which 3 were waited for; matrix products, arithmetic and copies ran while one was open for 1% of the time, Pallas kernels for 0%

commit v1 on v0

v1 whole, which is shorter than its diff:
```python
import jax
import jax.numpy as jnp
from jax import lax
from jax.sharding import Mesh
from jax.sharding import PartitionSpec as P

BF = jnp.bfloat16
F32 = jnp.float32
ROW = ("xh", "y")
Z = ("zh", "zl")
SIZES = (("xh", 2), ("y", 4), ("xl", 2), ("zh", 4), ("zl", 2), ("core", 2))
NAMES = tuple(name for name, _ in SIZES)
PAIR = ((0, 1), (1, 0))
CHUNKS = 2


def flat(coords):
    index = 0
    for (_, size), value in zip(SIZES, coords):
        index = index * size + value
    return index


def swap_pairs():
    pairs = []
    for a in range(2):
        for b in range(4):
            for c in range(2):
                for d in range(4):
                    for e in range(2):
                        for f in range(2):
                            pairs.append((flat((a, b, c, d, e, f)), flat((c, d, a, b, e, f))))
    return pairs


def dot(a, b):
    return lax.dot_general(a, b, (((0,), (0,)), ((), ())), preferred_element_type=F32)


def swap(x, axis):
    return lax.ppermute(x, axis, PAIR)


def gather(x, axes, count):
    copies = jnp.broadcast_to(x[None], (count,) + x.shape)
    return lax.all_to_all(copies, axes, 0, 0, tiled=False)


def half(x, index, axis):
    size = x.shape[axis] // 2
    return lax.dynamic_slice_in_dim(x, index * size, size, axis)


def total(terms):
    parts = [terms[k].astype(F32) for k in range(terms.shape[0])]
    while len(parts) > 1:
        parts = [a + b for a, b in zip(parts[::2], parts[1::2])]
    return parts[0]


def ordered(index, own, other):
    first = jnp.where(index == 0, own, other)
    second = jnp.where(index == 0, other, own)
    return first, second


def per_device(orbitals, kernel, applied, fit):
    core = lax.axis_index("core")
    xl = lax.axis_index("xl")
    zl = lax.axis_index("zl")

    bands = orbitals.T
    with jax.named_scope("mu"):
        mu_own = half(bands, core, 1)
        mu_other = swap(half(bands, 1 - core, 1), "core")
        mu_a = gather(mu_own, Z, 8).reshape(256, 1024)
        mu_b = gather(mu_other, Z, 8).reshape(256, 1024)
        mu_ax = swap(mu_a, "xl")
        mu_bx = swap(mu_b, "xl")
    with jax.named_scope("nu"):
        low, high = ordered(zl, half(bands, zl, 1), swap(half(bands, 1 - zl, 1), "zl"))
        piece = jnp.concatenate([low, high], axis=0)
        piece = lax.ppermute(piece, NAMES, swap_pairs())
        both_a = gather(jnp.concatenate([piece, applied.T], axis=1), ROW, 8)
        both_b = swap(both_a, "core")
        nu_a = both_a[:, :, :1024].reshape(512, 1024)
        nu_b = both_b[:, :, :1024].reshape(512, 1024)
        blocks = jnp.concatenate(ordered(core, both_a[:, :, 1024:], both_b[:, :, 1024:]), axis=2)
    with jax.named_scope("kernel"):
        own = half(kernel, core, 1)
        other = swap(half(kernel, 1 - core, 1), "core")
        weights = jnp.concatenate(ordered(core, own, other), axis=0)
    with jax.named_scope("fit"):
        place = core * 2 + xl
        fits = [
            lax.dynamic_slice_in_dim(fit, jnp.bitwise_xor(place, k) * 512, 512, 0) for k in range(4)
        ]

    with jax.named_scope("density"):
        density = dot(half(nu_a, xl, 0), mu_a)
        density = density + dot(half(nu_b, xl, 0), mu_b)
        density = density + dot(half(nu_a, 1 - xl, 0), mu_ax)
        density = density + dot(half(nu_b, 1 - xl, 0), mu_bx)
        weighted = (density * weights.astype(F32)).astype(BF)
        weighted = lax.optimization_barrier(weighted)

    outs = []
    width = 64 // CHUNKS
    for h in range(CHUNKS):
        with jax.named_scope(f"projected{h}"):
            block = blocks[:, h * width : (h + 1) * width].reshape(8 * width, 1024)
            partial = lax.dot_general(
                weighted, block, (((0,), (1,)), ((), ())), preferred_element_type=F32
            )
            arrived = swap(half(partial, 1 - xl, 0).astype(BF), "xl")
            two = (half(partial, xl, 0) + arrived.astype(F32)).astype(BF)
            terms = lax.all_to_all(two.reshape(8, 64, 8 * width), Z, 0, 0, tiled=False)
            low = total(terms).astype(BF)
            p0 = gather(low, Z, 8).reshape(512, 8 * width)
            p1 = swap(p0, "xl")
            p2 = swap(p0, "core")
            p3 = swap(p1, "core")
        with jax.named_scope(f"exchange{h}"):
            result = dot(p0, fits[0])
            result = result + dot(p1, fits[1])
            result = result + dot(p2, fits[2])
            result = result + dot(p3, fits[3])
            terms = lax.all_to_all(
                (-result).astype(BF).reshape(8, width, 2048), ROW, 0, 0, tiled=False
            )
            outs.append(total(terms).astype(BF))
    return jnp.concatenate(outs, axis=0)


def solution(mesh):
    fine = Mesh(mesh.devices.reshape(tuple(size for _, size in SIZES)), NAMES)
    row, col = ROW, ("xl",) + Z + ("core",)
    return jax.shard_map(
        per_device,
        mesh=fine,
        in_specs=(P(row, col), P(col, row), P(col, row), P(row, col)),
        out_specs=P(row, col),
        check_vma=False,
    )
```

time: 384 us -> 233 us (0.61)
  blocking collectives: 167 us -> 0 us
  starting transfers between devices: 7.49 us -> 69.1 us
  waiting for transfers between devices: 174 us -> 124 us
  between operations: 13.1 us -> 0.37 us
  local copies, waits for them, and re-layouts: 2.37 us -> 9.23 us
  matrix products: 17.8 us -> 23.1 us
  other arithmetic: 1.77 us -> 5.97 us
    psum x1 -> x0, blocking collectives: 130 us -> none  [per_device(): projected = lax.psum(partial_sum, 'col')]
    all_to_all x1 -> x9, waiting for transfers between devices: 0.01 us -> 88.8 us  [the longest x5 47.1 us: gather(): return lax.all_to_all(copies, axes, 0, 0, tiled=False)]
    all_gather x2 -> x0, waiting for transfers between devices: 86.1 us -> none  [the longest x1 55.9 us: per_device(): columns = lax.all_gather(orbitals, 'row', axis=0, tiled=True)]
    reduce_scatter x1 -> x0, waiting for transfers between devices: 86.1 us -> none  [per_device(): lax.psum_scatter(-lax.dot_general(projected_low, fit, (((0,), (0,)), ((),...]
    all_to_all x1 -> x9, starting transfers between devices: 7.41 us -> 59.4 us  [the longest x5 33.5 us: gather(): return lax.all_to_all(copies, axes, 0, 0, tiled=False)]
    all_gather x1 -> x0, blocking collectives: 37 us -> none  [per_device(): lax.all_gather(applied, 'row', axis=1, tiled=True)]
    ppermute x0 -> x15, waiting for transfers between devices: none -> 35.7 us  [the longest x14 26.6 us: swap(): return lax.ppermute(x, axis, PAIR)]
    ppermute x0 -> x15, starting transfers between devices: none -> 9.79 us  [the longest x14 6.08 us: swap(): return lax.ppermute(x, axis, PAIR)]
  transfers between devices with their start and end apart: 4 -> 24, of which waited for: 3 -> 14; matrix products, arithmetic and copies ran while one was open for 1% -> 13% of each run, Pallas kernels for 0% -> 0%
where the time goes in v1:
time: 233 us; the launch traced here: 232 us
  waiting for transfers between devices  124 us (53%)
  starting transfers between devices  69.1 us (30%)
  matrix products  23.1 us (10%)
  local copies, waits for them, and re-layouts  9.23 us (4%)
  other arithmetic  5.97 us (3%)
    all_to_all x5, waiting for transfers between devices, gather(): return lax.all_to_all(copies, axes, 0, 0, tiled=False)  47.1 us
    all_to_all x5, starting transfers between devices, gather(): return lax.all_to_all(copies, axes, 0, 0, tiled=False)  33.5 us
    ppermute x14, waiting for transfers between devices, swap(): return lax.ppermute(x, axis, PAIR)  26.6 us
    all_to_all x2, waiting for transfers between devices, per_device(): lax.all_to_all((-result).astype(BF).reshape(8, width, 2048), ROW, 0, 0, t...  21.6 us
    dot_general x12, matrix products, dot(): lax.dot_general(a, b, (((0,), (0,)), ((), ())), preferred_element_type=F32)  21.5 us
    all_to_all x2, waiting for transfers between devices, per_device(): terms = lax.all_to_all(two.reshape(8, 64, 8 * width), Z, 0, 0, tiled=False)  20.1 us
    all_to_all x2, starting transfers between devices, per_device(): terms = lax.all_to_all(two.reshape(8, 64, 8 * width), Z, 0, 0, tiled=False)  13.1 us
    all_to_all x2, starting transfers between devices, per_device(): lax.all_to_all((-result).astype(BF).reshape(8, width, 2048), ROW, 0, 0, t...  12.8 us
  transfers between devices with their start and end apart: 24, of which 14 were waited for; matrix products, arithmetic and copies ran while one was open for 13% of the time, Pallas kernels for 0%

profile of v1, /device:TPU:8, one launch (start us, length us, event | category | flops | bytes accessed | tf_op | source)
XLA Modules:
  0.0 232.3 jit_solution(13465510634262078182)
XLA Ops:
  0.0 1.0 dynamic-slice_bitcast_fusion
  1.0 0.8 broadcast_in_dim.15
  1.8 8.5 %all-to-all-start.1 = ((bf16[8,32,1024]{2,1,0:T(8,128)(2,1)}), bf16[8,32,1024]{2,1,0:T(8,128)(2,1)S(1)}, u32[]{:S(2)}, u32[]{:S(2)}) async-start(bf16[8,32,1024]{2,1,0:T(8,128)(2,1)} %broadcast_in_dim.15), calls=%async_computation.1 | async-start | bytes 1048576 | tf_op jit(solution)/shard_map/mu/all_to_all | solution.py:46
  10.3 2.0 collective-permute-start
  12.3 12.7 %collective-permute-done = bf16[32,1024]{1,0:T(8,128)(2,1)S(1)} collective-permute-done((bf16[32,1024]{1,0:T(8,128)(2,1)S(1)}, bf16[32,1024]{1,0:T(8,128)(2,1)S(1)}, u32[]{:S(2)}, u32[]{:S(2)}) %collective-permute-start) | collective-permute-done | bytes 65568 | tf_op jit(solution)/shard_map/nu/ppermute | solution.py:41
  25.0 3.7 %collective-permute-start.1 = (bf16[64,1024]{1,0:T(8,128)(2,1)S(1)}, bf16[64,1024]{1,0:T(8,128)(2,1)S(1)}, u32[]{:S(2)}, u32[]{:S(2)}) collective-permute-start(bf16[64,1024]{1,0:T(8,128)(2,1)S(1)} %pad_maximum_fusion.3), channel_id=1, source_target_pairs={{0,0},{1,1},{2,2},{3,3},{4,32},{5,33},{6,34},{7,35},{8,64},{9,65},... | collective-permute-start | bytes 393224 | tf_op jit(solution)/shard_map/nu/ppermute | solution.py:83
  28.8 9.1 %collective-permute-done.1 = bf16[64,1024]{1,0:T(8,128)(2,1)S(1)} collective-permute-done((bf16[64,1024]{1,0:T(8,128)(2,1)S(1)}, bf16[64,1024]{1,0:T(8,128)(2,1)S(1)}, u32[]{:S(2)}, u32[]{:S(2)}) %collective-permute-start.1) | collective-permute-done | bytes 131104 | tf_op jit(solution)/shard_map/nu/ppermute | solution.py:83
  37.9 1.3 broadcast_in_dim.14
  39.2 9.4 %all-to-all-start = ((bf16[8,64,1536]{2,1,0:T(8,128)(2,1)}), bf16[8,64,1536]{2,1,0:T(8,128)(2,1)S(1)}, u32[]{:S(2)}, u32[]{:S(2)}) async-start(bf16[8,64,1536]{2,1,0:T(8,128)(2,1)} %broadcast_in_dim.14), calls=%async_computation | async-start | bytes 3145728 | tf_op jit(solution)/shard_map/nu/all_to_all | solution.py:46
  48.7 2.3 constant_dynamic-slice_fusion
  50.9 0.5 collective-permute-start.3
  51.5 2.5 %collective-permute-done.3 = bf16[32,1024]{1,0:T(8,128)(2,1)S(1)} collective-permute-done((bf16[32,1024]{1,0:T(8,128)(2,1)S(1)}, bf16[32,1024]{1,0:T(8,128)(2,1)S(1)}, u32[]{:S(2)}, u32[]{:S(2)}) %collective-permute-start.3) | collective-permute-done | bytes 65568 | tf_op jit(solution)/shard_map/mu/ppermute | solution.py:41
  53.9 12.0 %all-to-all-done = bf16[8,64,1536]{2,1,0:T(8,128)(2,1)S(1)} async-done(((bf16[8,64,1536]{2,1,0:T(8,128)(2,1)}), bf16[8,64,1536]{2,1,0:T(8,128)(2,1)S(1)}, u32[]{:S(2)}, u32[]{:S(2)}) %all-to-all-start) | async-done | bytes 1572896 | tf_op jit(solution)/shard_map/nu/all_to_all | solution.py:46
  65.9 0.9 broadcast_in_dim.16
  66.8 8.7 %all-to-all-start.2 = ((bf16[8,32,1024]{2,1,0:T(8,128)(2,1)}), bf16[8,32,1024]{2,1,0:T(8,128)(2,1)S(1)}, u32[]{:S(2)}, u32[]{:S(2)}) async-start(bf16[8,32,1024]{2,1,0:T(8,128)(2,1)} %broadcast_in_dim.16), calls=%async_computation.2 | async-start | bytes 1048576 | tf_op jit(solution)/shard_map/mu/all_to_all | solution.py:46
  75.5 0.1 collective-permute-start.4
  75.6 15.1 %all-to-all-done.2 = bf16[8,32,1024]{2,1,0:T(8,128)(2,1)S(1)} async-done(((bf16[8,32,1024]{2,1,0:T(8,128)(2,1)}), bf16[8,32,1024]{2,1,0:T(8,128)(2,1)S(1)}, u32[]{:S(2)}, u32[]{:S(2)}) %all-to-all-start.2) | async-done | bytes 524320 | tf_op jit(solution)/shard_map/mu/all_to_all | solution.py:46
  90.7 2.1 broadcast_select_fusion.1
  92.8 0.1 slice.152
  93.0 0.8 fusion.23
  93.7 0.8 fusion.19
  94.5 1.3 slice.153
  95.8 0.8 fusion.21
  96.6 4.5 %collective-permute-done.5 = bf16[256,1024]{1,0:T(8,128)(2,1)S(1)} collective-permute-done((bf16[256,1024]{1,0:T(8,128)(2,1)S(1)}, bf16[256,1024]{1,0:T(8,128)(2,1)S(1)}, u32[]{:S(2)}, u32[]{:S(2)}) %collective-permute-start.5) | collective-permute-done | bytes 524320 | tf_op jit(solution)/shard_map/mu/ppermute | solution.py:41
  101.1 1.2 multiply_convert_fusion
  102.3 1.1 broadcast_select_fusion.3
  103.4 0.1 fusion.14
  103.6 0.8 fusion.42
  104.4 0.4 collective-permute-start.11
  104.8 0.8 fusion.41
  105.6 1.8 collective-permute-start.7
  107.5 3.7 %collective-permute-done.11 = bf16[512,256]{1,0:T(8,128)(2,1)S(1)} collective-permute-done((bf16[512,256]{1,0:T(8,128)(2,1)S(1)}, bf16[512,256]{1,0:T(8,128)(2,1)S(1)}, u32[]{:S(2)}, u32[]{:S(2)}) %collective-permute-start.11) | collective-permute-done | bytes 262176 | tf_op jit(solution)/shard_map/projected1/ppermute | solution.py:41
  111.2 0.8 add_convert_fusion
  111.9 9.7 %all-to-all-start.6 = ((bf16[8,64,256]{2,1,0:T(8,128)(2,1)}), bf16[8,64,256]{2,1,0:T(8,128)(2,1)S(1)}, u32[]{:S(2)}, u32[]{:S(2)}) async-start(bf16[8,64,256]{2,1,0:T(8,128)(2,1)} %bitcast.16), calls=%async_computation.6 | async-start | bytes 524288 | tf_op jit(solution)/shard_map/projected1/all_to_all | solution.py:117
  121.6 0.8 add_convert_fusion.1
  122.4 9.7 %all-to-all-done.6 = bf16[8,64,256]{2,1,0:T(8,128)(2,1)S(1)} async-done(((bf16[8,64,256]{2,1,0:T(8,128)(2,1)}), bf16[8,64,256]{2,1,0:T(8,128)(2,1)S(1)}, u32[]{:S(2)}, u32[]{:S(2)}) %all-to-all-start.6) | async-done | bytes 262176 | tf_op jit(solution)/shard_map/projected1/all_to_all | solution.py:117
  132.1 3.4 %all-to-all-start.3 = ((bf16[8,64,256]{2,1,0:T(8,128)(2,1)}), bf16[8,64,256]{2,1,0:T(8,128)(2,1)S(1)}, u32[]{:S(2)}, u32[]{:S(2)}) async-start(bf16[8,64,256]{2,1,0:T(8,128)(2,1)} %bitcast.10), calls=%async_computation.3 | async-start | bytes 524288 | tf_op jit(solution)/shard_map/projected0/all_to_all | solution.py:117
  135.6 10.3 %all-to-all-done.3 = bf16[8,64,256]{2,1,0:T(8,128)(2,1)S(1)} async-done(((bf16[8,64,256]{2,1,0:T(8,128)(2,1)}), bf16[8,64,256]{2,1,0:T(8,128)(2,1)S(1)}, u32[]{:S(2)}, u32[]{:S(2)}) %all-to-all-start.3) | async-done | bytes 262176 | tf_op jit(solution)/shard_map/projected0/all_to_all | solution.py:117
  145.9 0.7 broadcast_in_dim.40
  146.7 3.4 %all-to-all-start.7 = ((bf16[8,64,256]{2,1,0:T(8,128)(2,1)}), bf16[8,64,256]{2,1,0:T(8,128)(2,1)S(1)}, u32[]{:S(2)}, u32[]{:S(2)}) async-start(bf16[8,64,256]{2,1,0:T(8,128)(2,1)} %broadcast_in_dim.40), calls=%async_computation.7 | async-start | bytes 524288 | tf_op jit(solution)/shard_map/projected1/all_to_all | solution.py:46
  150.1 10.3 %all-to-all-done.7 = bf16[8,64,256]{2,1,0:T(8,128)(2,1)S(1)} async-done(((bf16[8,64,256]{2,1,0:T(8,128)(2,1)}), bf16[8,64,256]{2,1,0:T(8,128)(2,1)S(1)}, u32[]{:S(2)}, u32[]{:S(2)}) %all-to-all-start.7) | async-done | bytes 262176 | tf_op jit(solution)/shard_map/projected1/all_to_all | solution.py:46
  160.5 0.7 broadcast_in_dim.18
  161.2 3.4 %all-to-all-start.4 = ((bf16[8,64,256]{2,1,0:T(8,128)(2,1)}), bf16[8,64,256]{2,1,0:T(8,128)(2,1)S(1)}, u32[]{:S(2)}, u32[]{:S(2)}) async-start(bf16[8,64,256]{2,1,0:T(8,128)(2,1)} %broadcast_in_dim.18), calls=%async_computation.4 | async-start | bytes 524288 | tf_op jit(solution)/shard_map/projected0/all_to_all | solution.py:46
  164.6 0.3 collective-permute-start.13
  164.9 0.4 collective-permute-start.12
  165.3 9.7 %all-to-all-done.4 = bf16[8,64,256]{2,1,0:T(8,128)(2,1)S(1)} async-done(((bf16[8,64,256]{2,1,0:T(8,128)(2,1)}), bf16[8,64,256]{2,1,0:T(8,128)(2,1)S(1)}, u32[]{:S(2)}, u32[]{:S(2)}) %all-to-all-start.4) | async-done | bytes 262176 | tf_op jit(solution)/shard_map/projected0/all_to_all | solution.py:46
  175.0 0.3 collective-permute-start.8
  175.3 2.5 %fusion.12 = f32[256,2048]{1,0:T(8,128)S(1)} fusion(bf16[512,256]{1,0:T(8,128)(2,1)S(1)} %bitcast.64, bf16[2048,2048]{1,0:T(8,128)(2,1)} %param.7, s32[]{:T(128)S(6)} %select_n.95), kind=kOutput, calls=%fused_computation.19 | convolution fusion | flops 536870912 | bytes 4456452 | tf_op jit(solution)/shard_map/exchange0/dot_general | solution.py:37
  177.8 2.5 %fusion.10 = f32[256,2048]{1,0:T(8,128)S(1)} fusion(bf16[512,256]{1,0:T(8,128)(2,1)S(1)} %bitcast.61, bf16[2048,2048]{1,0:T(8,128)(2,1)} %param.7, s32[]{:T(128)S(6)} %select_n.95), kind=kOutput, calls=%fused_computation.17 | convolution fusion | flops 536870912 | bytes 4456452 | tf_op jit(solution)/shard_map/exchange1/dot_general | solution.py:37
  180.3 0.3 collective-permute-start.14
  180.6 3.1 %collective-permute-done.8 = bf16[512,256]{1,0:T(8,128)(2,1)S(1)} collective-permute-done((bf16[512,256]{1,0:T(8,128)(2,1)S(1)}, bf16[512,256]{1,0:T(8,128)(2,1)S(1)}, u32[]{:S(2)}, u32[]{:S(2)}) %collective-permute-start.8) | collective-permute-done | bytes 262176 | tf_op jit(solution)/shard_map/projected0/ppermute | solution.py:41
  183.7 2.3 %convolution_add_fusion.5 = f32[256,2048]{1,0:T(8,128)S(1)} fusion(f32[256,2048]{1,0:T(8,128)S(1)} %fusion.12, bf16[512,256]{1,0:T(8,128)(2,1)S(1)} %collective-permute-done.8, bf16[2048,2048]{1,0:T(8,128)(2,1)} %param.7, s32[]{:T(128)S(6)} %select_n.96), kind=kOutput, calls=%fused_computation.8 | convolution fusion | flops 537395200 | bytes 6553604 | tf_op jit(solution)/shard_map/exchange0/dot_general | solution.py:37
  186.1 0.7 convolution_add_fusion.4
  186.9 1.7 fusion.2
  188.6 7.4 %all-to-all-start.5 = ((bf16[8,32,2048]{2,1,0:T(8,128)(2,1)}), bf16[8,32,2048]{2,1,0:T(8,128)(2,1)S(1)}, u32[]{:S(2)}, u32[]{:S(2)}) async-start(bf16[8,32,2048]{2,1,0:T(8,128)(2,1)} %bitcast.52), calls=%async_computation.5 | async-start | bytes 2097152 | tf_op jit(solution)/shard_map/exchange0/all_to_all | solution.py:128
  196.0 2.4 %convolution_add_fusion.2 = f32[256,2048]{1,0:T(8,128)S(1)} fusion(f32[256,2048]{1,0:T(8,128)S(1)} %fusion.10, bf16[512,256]{1,0:T(8,128)(2,1)} %collective-permute-done.12, bf16[2048,2048]{1,0:T(8,128)(2,1)} %param.7, s32[]{:T(128)S(6)} %select_n.96), kind=kOutput, calls=%fused_computation.4 | convolution fusion | flops 537395200 | bytes 6553604 | tf_op jit(solution)/shard_map/exchange1/dot_general | solution.py:37
  198.5 2.4 %convolution_add_fusion.1 = f32[256,2048]{1,0:T(8,128)S(1)} fusion(f32[256,2048]{1,0:T(8,128)S(1)} %convolution_add_fusion.2, bf16[512,256]{1,0:T(8,128)(2,1)} %collective-permute-done.13, bf16[2048,2048]{1,0:T(8,128)(2,1)} %param.7, s32[]{:T(128)S(6)} %select_n.97), kind=kOutput, calls=%fused_computation.3 | convolution fusion | flops 537395200 | bytes 6553604 | tf_op jit(solution)/shard_map/exchange1/dot_general | solution.py:37
  200.9 3.4 %fusion.3 = bf16[256,2048]{1,0:T(8,128)(2,1)} fusion(f32[256,2048]{1,0:T(8,128)S(1)} %convolution_add_fusion.1, bf16[512,256]{1,0:T(8,128)(2,1)} %collective-permute-done.14, bf16[2048,2048]{1,0:T(8,128)(2,1)} %param.7, s32[]{:T(128)S(6)} %select_n.98), kind=kOutput, calls=%fused_computation.10 | convolution fusion | flops 538443776 | bytes 5505028 | tf_op jit(solution)/shard_map/exchange1/dot_general | solution.py:37
  204.3 6.9 %all-to-all-done.5 = bf16[8,32,2048]{2,1,0:T(8,128)(2,1)S(1)} async-done(((bf16[8,32,2048]{2,1,0:T(8,128)(2,1)}), bf16[8,32,2048]{2,1,0:T(8,128)(2,1)S(1)}, u32[]{:S(2)}, u32[]{:S(2)}) %all-to-all-start.5) | async-done | bytes 1048608 | tf_op jit(solution)/shard_map/exchange0/all_to_all | solution.py:128
  211.3 5.4 %all-to-all-start.8 = ((bf16[8,32,2048]{2,1,0:T(8,128)(2,1)}), bf16[8,32,2048]{2,1,0:T(8,128)(2,1)S(1)}, u32[]{:S(2)}, u32[]{:S(2)}) async-start(bf16[8,32,2048]{2,1,0:T(8,128)(2,1)} %bitcast.19), calls=%async_computation.8 | async-start | bytes 2097152 | tf_op jit(solution)/shard_map/exchange1/all_to_all | solution.py:128
  216.6 0.1 fusion.25
  216.8 14.6 %all-to-all-done.8 = bf16[8,32,2048]{2,1,0:T(8,128)(2,1)S(1)} async-done(((bf16[8,32,2048]{2,1,0:T(8,128)(2,1)}), bf16[8,32,2048]{2,1,0:T(8,128)(2,1)S(1)}, u32[]{:S(2)}, u32[]{:S(2)}) %all-to-all-start.8) | async-done | bytes 1048608 | tf_op jit(solution)/shard_map/exchange1/all_to_all | solution.py:128
  231.4 0.1 fusion.26
  231.6 0.7 pad_maximum_fusion.1
  (31 shorter events, 0.3 us)
Async XLA Ops:
  0.0 25.0 %copy-start = (bf16[2048,32]{0,1:T(8,128)(2,1)S(1)}, bf16[2048,32]{0,1:T(8,128)(2,1)}, u32[]{:S(2)}) copy-start(bf16[2048,32]{0,1:T(8,128)(2,1)} %param.4) | copy-start | bytes 393220
  0.0 37.9 %copy-start.1 = (bf16[512,64]{0,1:T(8,128)(2,1)S(1)}, bf16[512,64]{0,1:T(8,128)(2,1)}, u32[]{:S(2)}) copy-start(bf16[512,64]{0,1:T(8,128)(2,1)} %param.6) | copy-start | bytes 196612
  1.8 36.1 %all-to-all-start.1 = ((bf16[8,32,1024]{2,1,0:T(8,128)(2,1)}), bf16[8,32,1024]{2,1,0:T(8,128)(2,1)S(1)}, u32[]{:S(2)}, u32[]{:S(2)}) async-start(bf16[8,32,1024]{2,1,0:T(8,128)(2,1)} %broadcast_in_dim.15), calls=%async_computation.1 | async-start | bytes 1048576 | tf_op jit(solution)/shard_map/mu/all_to_all | solution.py:46
  10.3 14.7 %collective-permute-start = (bf16[32,1024]{1,0:T(8,128)(2,1)S(1)}, bf16[32,1024]{1,0:T(8,128)(2,1)S(1)}, u32[]{:S(2)}, u32[]{:S(2)}) collective-permute-start(bf16[32,1024]{1,0:T(8,128)(2,1)S(1)} %get-tuple-element.14), channel_id=1, source_target_pairs={{0,2},{2,0},{1,3},{3,1},{4,6},{6,4},{5,7},{7,5},{8,10},{10,8},{9,1... | collective-permute-start | bytes 196616 | tf_op jit(solution)/shard_map/nu/ppermute | solution.py:41
  25.0 12.9 %collective-permute-start.1 = (bf16[64,1024]{1,0:T(8,128)(2,1)S(1)}, bf16[64,1024]{1,0:T(8,128)(2,1)S(1)}, u32[]{:S(2)}, u32[]{:S(2)}) collective-permute-start(bf16[64,1024]{1,0:T(8,128)(2,1)S(1)} %pad_maximum_fusion.3), channel_id=1, source_target_pairs={{0,0},{1,1},{2,2},{3,3},{4,32},{5,33},{6,34},{7,35},{8,64},{9,65},... | collective-permute-start | bytes 393224 | tf_op jit(solution)/shard_map/nu/ppermute | solution.py:83
  39.2 26.7 %all-to-all-start = ((bf16[8,64,1536]{2,1,0:T(8,128)(2,1)}), bf16[8,64,1536]{2,1,0:T(8,128)(2,1)S(1)}, u32[]{:S(2)}, u32[]{:S(2)}) async-start(bf16[8,64,1536]{2,1,0:T(8,128)(2,1)} %broadcast_in_dim.14), calls=%async_computation | async-start | bytes 3145728 | tf_op jit(solution)/shard_map/nu/all_to_all | solution.py:46
  50.9 39.8 %collective-permute-start.6 = (bf16[512,1024]{1,0:T(8,128)(2,1)}, bf16[512,1024]{1,0:T(8,128)(2,1)}, u32[]{:S(2)}, u32[]{:S(2)}) collective-permute-start(bf16[512,1024]{1,0:T(8,128)(2,1)} %constant_dynamic-slice_fusion), channel_id=1, source_target_pairs={{0,1},{1,0},{2,3},{3,2},{4,5},{5,4},{6,7},{7,6},{8,9},{9,8},{10,11... | collective-permute-start | bytes 3145736 | tf_op jit(solution)/shard_map/kernel/ppermute | solution.py:41
  50.9 3.0 %collective-permute-start.3 = (bf16[32,1024]{1,0:T(8,128)(2,1)S(1)}, bf16[32,1024]{1,0:T(8,128)(2,1)S(1)}, u32[]{:S(2)}, u32[]{:S(2)}) collective-permute-start(bf16[32,1024]{1,0:T(8,128)(2,1)S(1)} %get-tuple-element.13), channel_id=1, source_target_pairs={{0,1},{1,0},{2,3},{3,2},{4,5},{5,4},{6,7},{7,6},{8,9},{9,8},{10,11... | collective-permute-start | bytes 196616 | tf_op jit(solution)/shard_map/mu/ppermute | solution.py:41
  66.8 24.0 %all-to-all-start.2 = ((bf16[8,32,1024]{2,1,0:T(8,128)(2,1)}), bf16[8,32,1024]{2,1,0:T(8,128)(2,1)S(1)}, u32[]{:S(2)}, u32[]{:S(2)}) async-start(bf16[8,32,1024]{2,1,0:T(8,128)(2,1)} %broadcast_in_dim.16), calls=%async_computation.2 | async-start | bytes 1048576 | tf_op jit(solution)/shard_map/mu/all_to_all | solution.py:46
  75.5 19.0 %collective-permute-start.2 = (bf16[8,64,1536]{2,1,0:T(8,128)(2,1)S(1)}, bf16[8,64,1536]{2,1,0:T(8,128)(2,1)}, u32[]{:S(2)}, u32[]{:S(2)}) collective-permute-start(bf16[8,64,1536]{2,1,0:T(8,128)(2,1)S(1)} %all-to-all-done), channel_id=1, source_target_pairs={{0,1},{1,0},{2,3},{3,2},{4,5},{5,4},{6,7},{7,6},{8,9},{9,8},{10,11... | collective-permute-start | bytes 4718600 | tf_op jit(solution)/shard_map/nu/ppermute | solution.py:41
  75.5 18.2 %collective-permute-start.4 = (bf16[256,1024]{1,0:T(8,128)(2,1)S(1)}, bf16[256,1024]{1,0:T(8,128)(2,1)S(1)}, u32[]{:S(2)}, u32[]{:S(2)}) collective-permute-start(bf16[256,1024]{1,0:T(8,128)(2,1)S(1)} %bitcast.53), channel_id=1, source_target_pairs={{0,16},{16,0},{1,17},{17,1},{2,18},{18,2},{3,19},{19,3},{4,20},{20... | collective-permute-start | bytes 1572872 | tf_op jit(solution)/shard_map/mu/ppermute | solution.py:41
  90.7 10.3 %collective-permute-start.5 = (bf16[256,1024]{1,0:T(8,128)(2,1)S(1)}, bf16[256,1024]{1,0:T(8,128)(2,1)S(1)}, u32[]{:S(2)}, u32[]{:S(2)}) collective-permute-start(bf16[256,1024]{1,0:T(8,128)(2,1)S(1)} %bitcast.55), channel_id=1, source_target_pairs={{0,16},{16,0},{1,17},{17,1},{2,18},{18,2},{3,19},{19,3},{4,20},{20... | collective-permute-start | bytes 1572872 | tf_op jit(solution)/shard_map/mu/ppermute | solution.py:41
  104.4 6.8 %collective-permute-start.11 = (bf16[512,256]{1,0:T(8,128)(2,1)S(1)}, bf16[512,256]{1,0:T(8,128)(2,1)S(1)}, u32[]{:S(2)}, u32[]{:S(2)}) collective-permute-start(bf16[512,256]{1,0:T(8,128)(2,1)S(1)} %dynamic-slice_convert_fusion), channel_id=1, source_target_pairs={{0,16},{16,0},{1,17},{17,1},{2,18},{18,2},{3,19},{19,3},{4,20},{20... | collective-permute-start | bytes 786440 | tf_op jit(solution)/shard_map/projected1/ppermute | solution.py:41
  105.6 16.0 %collective-permute-start.7 = (bf16[512,256]{1,0:T(8,128)(2,1)S(1)}, bf16[512,256]{1,0:T(8,128)(2,1)S(1)}, u32[]{:S(2)}, u32[]{:S(2)}) collective-permute-start(bf16[512,256]{1,0:T(8,128)(2,1)S(1)} %dynamic-slice_convert_fusion.1), channel_id=1, source_target_pairs={{0,16},{16,0},{1,17},{17,1},{2,18},{18,2},{3,19},{19,3},{4,20},{20... | collective-permute-start | bytes 786440 | tf_op jit(solution)/shard_map/projected0/ppermute | solution.py:41
  111.9 20.2 %all-to-all-start.6 = ((bf16[8,64,256]{2,1,0:T(8,128)(2,1)}), bf16[8,64,256]{2,1,0:T(8,128)(2,1)S(1)}, u32[]{:S(2)}, u32[]{:S(2)}) async-start(bf16[8,64,256]{2,1,0:T(8,128)(2,1)} %bitcast.16), calls=%async_computation.6 | async-start | bytes 524288 | tf_op jit(solution)/shard_map/projected1/all_to_all | solution.py:117
  132.1 13.8 %all-to-all-start.3 = ((bf16[8,64,256]{2,1,0:T(8,128)(2,1)}), bf16[8,64,256]{2,1,0:T(8,128)(2,1)S(1)}, u32[]{:S(2)}, u32[]{:S(2)}) async-start(bf16[8,64,256]{2,1,0:T(8,128)(2,1)} %bitcast.10), calls=%async_computation.3 | async-start | bytes 524288 | tf_op jit(solution)/shard_map/projected0/all_to_all | solution.py:117
  146.7 13.8 %all-to-all-start.7 = ((bf16[8,64,256]{2,1,0:T(8,128)(2,1)}), bf16[8,64,256]{2,1,0:T(8,128)(2,1)S(1)}, u32[]{:S(2)}, u32[]{:S(2)}) async-start(bf16[8,64,256]{2,1,0:T(8,128)(2,1)} %broadcast_in_dim.40), calls=%async_computation.7 | async-start | bytes 524288 | tf_op jit(solution)/shard_map/projected1/all_to_all | solution.py:46
  161.2 13.8 %all-to-all-start.4 = ((bf16[8,64,256]{2,1,0:T(8,128)(2,1)}), bf16[8,64,256]{2,1,0:T(8,128)(2,1)S(1)}, u32[]{:S(2)}, u32[]{:S(2)}) async-start(bf16[8,64,256]{2,1,0:T(8,128)(2,1)} %broadcast_in_dim.18), calls=%async_computation.4 | async-start | bytes 524288 | tf_op jit(solution)/shard_map/projected0/all_to_all | solution.py:46
  164.6 33.8 %collective-permute-start.13 = (bf16[512,256]{1,0:T(8,128)(2,1)S(1)}, bf16[512,256]{1,0:T(8,128)(2,1)}, u32[]{:S(2)}, u32[]{:S(2)}) collective-permute-start(bf16[512,256]{1,0:T(8,128)(2,1)S(1)} %bitcast.59), channel_id=1, source_target_pairs={{0,1},{1,0},{2,3},{3,2},{4,5},{5,4},{6,7},{7,6},{8,9},{9,8},{10,11... | collective-permute-start | bytes 786440 | tf_op jit(solution)/shard_map/projected1/ppermute | solution.py:41
  164.9 15.3 %collective-permute-start.12 = (bf16[512,256]{1,0:T(8,128)(2,1)S(1)}, bf16[512,256]{1,0:T(8,128)(2,1)}, u32[]{:S(2)}, u32[]{:S(2)}) collective-permute-start(bf16[512,256]{1,0:T(8,128)(2,1)S(1)} %bitcast.60), channel_id=1, source_target_pairs={{0,16},{16,0},{1,17},{17,1},{2,18},{18,2},{3,19},{19,3},{4,20},{20... | collective-permute-start | bytes 786440 | tf_op jit(solution)/shard_map/projected1/ppermute | solution.py:41
  175.0 11.1 %collective-permute-start.9 = (bf16[512,256]{1,0:T(8,128)(2,1)S(1)}, bf16[512,256]{1,0:T(8,128)(2,1)S(1)}, u32[]{:S(2)}, u32[]{:S(2)}) collective-permute-start(bf16[512,256]{1,0:T(8,128)(2,1)S(1)} %bitcast.62), channel_id=1, source_target_pairs={{0,1},{1,0},{2,3},{3,2},{4,5},{5,4},{6,7},{7,6},{8,9},{9,8},{10,11... | collective-permute-start | bytes 786440 | tf_op jit(solution)/shard_map/projected0/ppermute | solution.py:41
  175.0 8.7 %collective-permute-start.8 = (bf16[512,256]{1,0:T(8,128)(2,1)S(1)}, bf16[512,256]{1,0:T(8,128)(2,1)S(1)}, u32[]{:S(2)}, u32[]{:S(2)}) collective-permute-start(bf16[512,256]{1,0:T(8,128)(2,1)S(1)} %bitcast.63), channel_id=1, source_target_pairs={{0,16},{16,0},{1,17},{17,1},{2,18},{18,2},{3,19},{19,3},{4,20},{20... | collective-permute-start | bytes 786440 | tf_op jit(solution)/shard_map/projected0/ppermute | solution.py:41
  175.3 10.8 %slice-start = ((s8[8388608]{0:T(1024)(128)(4,1)}), s8[4194304]{0:T(1024)(128)(4,1)S(1)}, s32[]{:S(2)}) async-start(s8[8388608]{0:T(1024)(128)(4,1)} %bitcast.46), calls=%async_computation.9 | async-start | bytes 8388608
  177.8 8.3 %slice-start.1 = ((s8[8388608]{0:T(1024)(128)(4,1)}), s8[4194304]{0:T(1024)(128)(4,1)S(1)}, s32[]{:S(2)}) async-start(s8[8388608]{0:T(1024)(128)(4,1)} %bitcast.46), calls=%async_computation.10 | async-start | bytes 8388608
  180.3 20.7 %collective-permute-start.14 = (bf16[512,256]{1,0:T(8,128)(2,1)}, bf16[512,256]{1,0:T(8,128)(2,1)}, u32[]{:S(2)}, u32[]{:S(2)}) collective-permute-start(bf16[512,256]{1,0:T(8,128)(2,1)} %collective-permute-done.12), channel_id=1, source_target_pairs={{0,1},{1,0},{2,3},{3,2},{4,5},{5,4},{6,7},{7,6},{8,9},{9,8},{10,11... | collective-permute-start | bytes 786440 | tf_op jit(solution)/shard_map/projected1/ppermute | solution.py:41
  183.7 3.1 %collective-permute-start.10 = (bf16[512,256]{1,0:T(8,128)(2,1)S(1)}, bf16[512,256]{1,0:T(8,128)(2,1)S(1)}, u32[]{:S(2)}, u32[]{:S(2)}) collective-permute-start(bf16[512,256]{1,0:T(8,128)(2,1)S(1)} %collective-permute-done.8), channel_id=1, source_target_pairs={{0,1},{1,0},{2,3},{3,2},{4,5},{5,4},{6,7},{7,6},{8,9},{9,8},{10,11... | collective-permute-start | bytes 786440 | tf_op jit(solution)/shard_map/projected0/ppermute | solution.py:41
  188.6 22.7 %all-to-all-start.5 = ((bf16[8,32,2048]{2,1,0:T(8,128)(2,1)}), bf16[8,32,2048]{2,1,0:T(8,128)(2,1)S(1)}, u32[]{:S(2)}, u32[]{:S(2)}) async-start(bf16[8,32,2048]{2,1,0:T(8,128)(2,1)} %bitcast.52), calls=%async_computation.5 | async-start | bytes 2097152 | tf_op jit(solution)/shard_map/exchange0/all_to_all | solution.py:128
  211.3 20.1 %all-to-all-start.8 = ((bf16[8,32,2048]{2,1,0:T(8,128)(2,1)}), bf16[8,32,2048]{2,1,0:T(8,128)(2,1)S(1)}, u32[]{:S(2)}, u32[]{:S(2)}) async-start(bf16[8,32,2048]{2,1,0:T(8,128)(2,1)} %bitcast.19), calls=%async_computation.8 | async-start | bytes 2097152 | tf_op jit(solution)/shard_map/exchange1/all_to_all | solution.py:128

commit v2 on v1

v2 whole, which is shorter than its diff:
```python
import jax
import jax.numpy as jnp
from jax import lax
from jax.sharding import Mesh
from jax.sharding import PartitionSpec as P


BF = jnp.bfloat16
F32 = jnp.float32
ROW = ("xh", "y")
Z = ("zh", "zl")
SIZES = (("xh", 2), ("y", 4), ("xl", 2), ("zh", 4), ("zl", 2), ("core", 2))
NAMES = tuple(name for name, _ in SIZES)
PAIR = ((0, 1), (1, 0))
MATE = tuple((z, z ^ 1) for z in range(8))
STEPS = (0, 3, 1, 2)
ORDER = (1, 0, 7, 6, 3, 2, 5, 4)
OUTER = tuple((z, (z - 1) % 8 if z % 2 == 0 else (z + 1) % 8) for z in range(8))


def flat(coords):
    index = 0
    for (_, size), value in zip(SIZES, coords):
        index = index * size + value
    return index


def nu_pairs(cross):
    pairs = []
    for xh in range(2):
        for y in range(4):
            for xl in range(2):
                for zh in range(4):
                    for zl in range(2):
                        for core in range(2):
                            away = STEPS[y] if zl == 0 else -STEPS[y]
                            source = (xl, zh, xl ^ xh, (zh + away) % 4, zl ^ cross, core)
                            pairs.append((flat(source), flat((xh, y, xl, zh, zl, core))))
    return pairs


def dot(a, b):
    return lax.dot_general(a, b, (((0,), (0,)), ((), ())), preferred_element_type=F32)


def swap(x, axis):
    return lax.ppermute(x, axis, PAIR)


def gather(x, axes, count):
    copies = jnp.broadcast_to(x[None], (count,) + x.shape)
    return lax.all_to_all(copies, axes, 0, 0, tiled=False)


def ring(x):
    near, far = [x], [x]
    for step in range(1, 5):
        near.append(lax.ppermute(far[step - 1], Z, MATE))
        if step < 4:
            far.append(lax.ppermute(near[step - 1], Z, OUTER))
    return near + far[:0:-1]


def half(x, index, axis):
    size = x.shape[axis] // 2
    return lax.dynamic_slice_in_dim(x, index * size, size, axis)


def total(terms):
    parts = [terms[k].astype(F32) for k in range(terms.shape[0])]
    while len(parts) > 1:
        parts = [a + b for a, b in zip(parts[::2], parts[1::2])]
    return parts[0]


def ordered(index, own, other):
    first = jnp.where(index == 0, own, other)
    second = jnp.where(index == 0, other, own)
    return first, second


def program(orbitals, kernel, applied, fit):
    core = lax.axis_index("core")
    xl = lax.axis_index("xl")
    zl = lax.axis_index("zl")

    bands = orbitals.T
    same = lax.ppermute(half(bands, zl, 1), NAMES, nu_pairs(0))
    cross = lax.ppermute(half(bands, 1 - zl, 1), NAMES, nu_pairs(1))
    piece = jnp.concatenate([cross, same], axis=0)
    both = gather(jnp.concatenate([piece, applied.T], axis=1), ROW, 8)
    nu_a = both[:, :, :1024].reshape(512, 1024)
    nu_b = swap(nu_a, "core")
    own = both[:, :, 1024:].reshape(512, 512)
    other = swap(own, "core")
    blocks = jnp.concatenate(ordered(core, own, other), axis=1)
    mu_own = half(bands, core, 1)
    mu_other = swap(half(bands, 1 - core, 1), "core")
    near = ring(jnp.concatenate([mu_own, mu_other], axis=0))
    away = [None] * 8
    away[0] = swap(near[0], "xl")
    for a, b in ((1, 7), (2, 6), (3, 5)):
        two = swap(jnp.concatenate([near[a], near[b]], axis=0), "xl")
        away[a], away[b] = two[:64], two[64:]
    away[4] = swap(near[4], "xl")
    mu = [
        jnp.concatenate([pieces[n][k * 32 : k * 32 + 32] for n in ORDER], axis=0)
        for pieces in (near, away)
        for k in range(2)
    ]
    own = half(kernel, core, 1)
    other = swap(half(kernel, 1 - core, 1), "core")
    weights = jnp.concatenate(ordered(core, own, other), axis=0)
    place = core * 2 + xl
    fits = [
        lax.dynamic_slice_in_dim(fit, jnp.bitwise_xor(place, k) * 512, 512, 0) for k in range(4)
    ]
    fits = lax.optimization_barrier(fits)

    density = dot(nu_a[:256], mu[0])
    density = density + dot(nu_b[:256], mu[1])
    density = density + dot(nu_a[256:], mu[2])
    density = density + dot(nu_b[256:], mu[3])
    weighted = (density * weights.astype(F32)).astype(BF)
    weighted = lax.optimization_barrier(weighted)

    partial = lax.dot_general(
        weighted, blocks, (((0,), (1,)), ((), ())), preferred_element_type=F32
    )
    arrived = swap(half(partial, 1 - xl, 0).astype(BF), "xl")
    two = (half(partial, xl, 0) + arrived.astype(F32)).astype(BF)
    terms = lax.all_to_all(two.reshape(8, 64, 512), Z, 0, 0, tiled=False)
    low = total(terms).astype(BF)
    p0 = gather(low, Z, 8).reshape(512, 512)
    p1 = swap(p0, "xl")
    p2 = swap(p0, "core")
    p3 = swap(p1, "core")
    result = dot(p0, fits[0])
    result = result + dot(p2, fits[2])
    result = result + dot(p1, fits[1])
    result = result + dot(p3, fits[3])
    terms = lax.all_to_all((-result).astype(BF).reshape(8, 64, 2048), ROW, 0, 0, tiled=False)
    return total(terms).astype(BF)


def solution(mesh):
    fine = Mesh(mesh.devices.reshape(tuple(size for _, size in SIZES)), NAMES)
    row, col = ROW, ("xl",) + Z + ("core",)
    return jax.shard_map(
        program,
        mesh=fine,
        in_specs=(P(row, col), P(col, row), P(col, row), P(row, col)),
        out_specs=P(row, col),
        check_vma=False,
    )
```

time: 233 us -> 186 us (0.80)
  waiting for transfers between devices: 124 us -> 53.6 us
  blocking collectives: 0 us -> 57.2 us
  starting transfers between devices: 69.1 us -> 42.2 us
  matrix products: 23.1 us -> 11.7 us
  local copies, waits for them, and re-layouts: 9.23 us -> 17.1 us
  other arithmetic: 5.97 us -> 2.02 us
    all_to_all x0 -> x2, blocking collectives: none -> 57.2 us  [the longest x1 35 us: program(): lax.all_to_all((-result).astype(BF).reshape(8, 64, 2048), ROW, 0, 0, tile...]
    all_to_all x4 -> x0, waiting for transfers between devices: 41.6 us -> none  [the longest x2 21.6 us: per_device(): lax.all_to_all((-result).astype(BF).reshape(8, width, 2048), ROW, 0, 0, t...]
    all_to_all x5 -> x2, waiting for transfers between devices: 47.1 us -> 15.3 us  [gather(): return lax.all_to_all(copies, axes, 0, 0, tiled=False)]
    all_to_all x4 -> x0, starting transfers between devices: 25.9 us -> none  [the longest x2 13.1 us: per_device(): terms = lax.all_to_all(two.reshape(8, 64, 8 * width), Z, 0, 0, tiled=False)]
    all_to_all x5 -> x2, starting transfers between devices: 33.5 us -> 9.9 us  [gather(): return lax.all_to_all(copies, axes, 0, 0, tiled=False)]
    ppermute x1 -> x9, starting transfers between devices: 3.71 us -> 22.5 us  [the longest x3 11.7 us: ring(): far.append(lax.ppermute(near[step - 1], Z, OUTER))]
    dot_general x12 -> x8, matrix products: 21.5 us -> 10.4 us  [dot(): lax.dot_general(a, b, (((0,), (0,)), ((), ())), preferred_element_type=F32)]
    unnamed x8 -> x27, local copies, waits for them, and re-layouts: 0.02 us -> 6.39 us
  transfers between devices with their start and end apart: 24 -> 24, of which waited for: 14 -> 11; matrix products, arithmetic and copies ran while one was open for 13% -> 10% of each run, Pallas kernels for 0% -> 0%
where the time goes in v2:
time: 186 us; the launch traced here: 184 us
  blocking collectives  57.2 us (31%)
  waiting for transfers between devices  53.6 us (29%)
  starting transfers between devices  42.2 us (23%)
  local copies, waits for them, and re-layouts  17.1 us (9%)
  matrix products  11.7 us (6%)
  other arithmetic  2.02 us (1%)
    all_to_all x1, blocking collectives, program(): lax.all_to_all((-result).astype(BF).reshape(8, 64, 2048), ROW, 0, 0, tile...  35 us
    ppermute x13, waiting for transfers between devices, swap(): return lax.ppermute(x, axis, PAIR)  31.2 us
    all_to_all x1, blocking collectives, program(): terms = lax.all_to_all(two.reshape(8, 64, 512), Z, 0, 0, tiled=False)  22.2 us
    all_to_all x2, waiting for transfers between devices, gather(): return lax.all_to_all(copies, axes, 0, 0, tiled=False)  15.3 us
    ppermute x3, starting transfers between devices, ring(): far.append(lax.ppermute(near[step - 1], Z, OUTER))  11.7 us
    dot_general x8, matrix products, dot(): lax.dot_general(a, b, (((0,), (0,)), ((), ())), preferred_element_type=F32)  10.4 us
    all_to_all x2, starting transfers between devices, gather(): return lax.all_to_all(copies, axes, 0, 0, tiled=False)  9.9 us
    ppermute x13, starting transfers between devices, swap(): return lax.ppermute(x, axis, PAIR)  9.81 us
  transfers between devices with their start and end apart: 24, of which 11 were waited for; matrix products, arithmetic and copies ran while one was open for 10% of the time, Pallas kernels for 0%

profile of v2, /device:TPU:8, one launch (start us, length us, event | category | flops | bytes accessed | tf_op | source)
XLA Modules:
  0.0 184.3 jit_solution(9440515881754859434)
XLA Ops:
  0.0 1.0 dynamic-slice_bitcast_fusion.3
  1.0 5.7 %collective-permute-start = (bf16[32,1024]{1,0:T(8,128)(2,1)S(1)}, bf16[32,1024]{1,0:T(8,128)(2,1)S(1)}, u32[]{:S(2)}, u32[]{:S(2)}) collective-permute-start(bf16[32,1024]{1,0:T(8,128)(2,1)S(1)} %get-tuple-element.53), channel_id=1, source_target_pairs={{2,0},{3,1},{0,2},{1,3},{38,4},{39,5},{36,6},{37,7},{74,8},{75,9},... | collective-permute-start | bytes 196616 | tf_op jit(solution)/shard_map/ppermute | solution.py:89
  6.7 1.9 %collective-permute-start.1 = (bf16[32,1024]{1,0:T(8,128)(2,1)S(1)}, bf16[32,1024]{1,0:T(8,128)(2,1)S(1)}, u32[]{:S(2)}, u32[]{:S(2)}) collective-permute-start(bf16[32,1024]{1,0:T(8,128)(2,1)S(1)} %get-tuple-element.54), channel_id=1, source_target_pairs={{0,0},{1,1},{2,2},{3,3},{36,4},{37,5},{38,6},{39,7},{72,8},{73,9},... | collective-permute-start | bytes 196616 | tf_op jit(solution)/shard_map/ppermute | solution.py:88
  8.6 0.1 collective-permute-start.2
  8.7 2.3 %constant_dynamic-slice_fusion.4 = bf16[512,1024]{1,0:T(8,128)(2,1)} fusion(bf16[512,2048]{1,0:T(8,128)(2,1)} %param.5, s32[]{:T(128)S(6)} %select_n.59), kind=kLoop, calls=%fused_computation.65 | loop fusion | bytes 2097156 | tf_op jit(solution)/shard_map/dynamic_slice | solution.py:66
  11.0 0.5 collective-permute-start.16
  11.5 2.6 %collective-permute-start.12 = (bf16[64,1024]{1,0:T(8,128)(2,1)S(1)}, bf16[64,1024]{1,0:T(8,128)(2,1)S(1)}, u32[]{:S(2)}, u32[]{:S(2)}) collective-permute-start(bf16[64,1024]{1,0:T(8,128)(2,1)S(1)} %pad_maximum_fusion.4), channel_id=1, source_target_pairs={{0,16},{16,0},{1,17},{17,1},{2,18},{18,2},{3,19},{19,3},{4,20},{20... | collective-permute-start | bytes 393224 | tf_op jit(solution)/shard_map/ppermute | solution.py:47
  14.1 8.0 %collective-permute-start.4 = (bf16[64,1024]{1,0:T(8,128)(2,1)S(1)}, bf16[64,1024]{1,0:T(8,128)(2,1)S(1)}, u32[]{:S(2)}, u32[]{:S(2)}) collective-permute-start(bf16[64,1024]{1,0:T(8,128)(2,1)S(1)} %pad_maximum_fusion.4), channel_id=1, source_target_pairs={{0,14},{2,4},{4,2},{6,8},{8,6},{10,12},{12,10},{14,0},{1,15},{3,5}... | collective-permute-start | bytes 393224 | tf_op jit(solution)/shard_map/ppermute | solution.py:60
  22.1 1.3 broadcast_in_dim.6
  23.4 6.4 %all-to-all-start = ((bf16[8,64,1536]{2,1,0:T(8,128)(2,1)}), bf16[8,64,1536]{2,1,0:T(8,128)(2,1)S(1)}, u32[]{:S(2)}, u32[]{:S(2)}) async-start(bf16[8,64,1536]{2,1,0:T(8,128)(2,1)} %broadcast_in_dim.6), calls=%async_computation | async-start | bytes 3145728 | tf_op jit(solution)/shard_map/all_to_all | solution.py:52
  29.9 0.9 collective-permute-start.11
  30.8 1.6 collective-permute-start.7
  32.4 1.7 collective-permute-start.5
  34.1 1.7 collective-permute-done.7
  35.9 2.0 %collective-permute-start.8 = (bf16[64,1024]{1,0:T(8,128)(2,1)S(1)}, bf16[64,1024]{1,0:T(8,128)(2,1)S(1)}, u32[]{:S(2)}, u32[]{:S(2)}) collective-permute-start(bf16[64,1024]{1,0:T(8,128)(2,1)S(1)} %collective-permute-done.7), channel_id=1, source_target_pairs={{0,14},{2,4},{4,2},{6,8},{8,6},{10,12},{12,10},{14,0},{1,15},{3,5}... | collective-permute-start | bytes 393224 | tf_op jit(solution)/shard_map/ppermute | solution.py:60
  37.9 1.7 collective-permute-done.5
  39.7 2.4 %collective-permute-done.8 = bf16[64,1024]{1,0:T(8,128)(2,1)S(1)} collective-permute-done((bf16[64,1024]{1,0:T(8,128)(2,1)S(1)}, bf16[64,1024]{1,0:T(8,128)(2,1)S(1)}, u32[]{:S(2)}, u32[]{:S(2)}) %collective-permute-start.8) | collective-permute-done | bytes 131104 | tf_op jit(solution)/shard_map/ppermute | solution.py:60
  42.0 1.2 collective-permute-start.13
  43.2 1.3 collective-permute-done.6
  44.6 1.2 collective-permute-start.14
  45.8 9.1 %collective-permute-done.11 = bf16[128,1024]{1,0:T(8,128)(2,1)S(1)} collective-permute-done((bf16[128,1024]{1,0:T(8,128)(2,1)S(1)}, bf16[128,1024]{1,0:T(8,128)(2,1)S(1)}, u32[]{:S(2)}, u32[]{:S(2)}) %collective-permute-start.11) | collective-permute-done | bytes 262176 | tf_op jit(solution)/shard_map/ppermute | solution.py:47
  54.9 1.5 collective-permute-start.9
  56.4 0.6 constant_dynamic-update-slice_fusion.23
  57.1 0.6 constant_dynamic-update-slice_fusion.22
  57.7 0.6 constant_dynamic-update-slice_fusion.21
  58.3 2.2 %collective-permute-done.13 = bf16[128,1024]{1,0:T(8,128)(2,1)S(1)} collective-permute-done((bf16[128,1024]{1,0:T(8,128)(2,1)S(1)}, bf16[128,1024]{1,0:T(8,128)(2,1)S(1)}, u32[]{:S(2)}, u32[]{:S(2)}) %collective-permute-start.13) | collective-permute-done | bytes 262176 | tf_op jit(solution)/shard_map/ppermute | solution.py:47
  60.5 0.6 constant_dynamic-update-slice_fusion.20
  61.1 1.2 collective-permute-start.15
  62.3 2.5 %collective-permute-done.14 = bf16[128,1024]{1,0:T(8,128)(2,1)S(1)} collective-permute-done((bf16[128,1024]{1,0:T(8,128)(2,1)S(1)}, bf16[128,1024]{1,0:T(8,128)(2,1)S(1)}, u32[]{:S(2)}, u32[]{:S(2)}) %collective-permute-start.14) | collective-permute-done | bytes 262176 | tf_op jit(solution)/shard_map/ppermute | solution.py:47
  64.9 0.6 constant_dynamic-update-slice_fusion.19
  65.5 0.6 constant_dynamic-update-slice_fusion.18
  66.1 0.6 constant_dynamic-update-slice_fusion.17
  66.8 0.6 constant_dynamic-update-slice_fusion.16
  67.4 0.1 slice.244
  67.5 0.1 collective-permute-start.10
  67.6 1.3 copy-done
  69.0 0.6 broadcast_select_fusion.1
  69.6 0.3 collective-permute-start.17
  69.9 0.1 fusion.11
  70.0 0.6 copy-done.4
  70.6 0.7 fusion.12
  71.4 0.4 collective-permute-done.17
  71.8 0.1 broadcast_select_fusion.3
  71.9 1.8 %fusion.4 = f32[1024,1024]{1,0:T(8,128)S(1)} fusion(bf16[256,1024]{1,0:T(8,128)(2,1)} %get-tuple-element.36, bf16[512,1024]{1,0:T(8,128)(2,1)S(1)} %collective-permute-done.10), kind=kOutput, calls=%fused_computation.10 | convolution fusion | flops 536870912 | bytes 5242880 | tf_op jit(solution)/shard_map/dot_general | solution.py:43
  73.8 0.7 fusion.6
  74.5 1.3 multiply_convert_fusion
  75.8 1.3 fusion
  77.2 1.4 collective-permute-start.18
  78.6 12.7 %collective-permute-done.18 = bf16[512,512]{1,0:T(8,128)(2,1)S(1)} collective-permute-done((bf16[512,512]{1,0:T(8,128)(2,1)S(1)}, bf16[512,512]{1,0:T(8,128)(2,1)S(1)}, u32[]{:S(2)}, u32[]{:S(2)}) %collective-permute-start.18) | collective-permute-done | bytes 524320 | tf_op jit(solution)/shard_map/ppermute | solution.py:47
  91.3 0.2 add_convert_fusion
  91.4 22.2 %all_to_all.20 = bf16[8,64,512]{2,1,0:T(8,128)(2,1)S(1)} all-to-all(bf16[8,64,512]{2,1,0:T(8,128)(2,1)S(1)} %bitcast.40), channel_id=1, replica_groups=mesh['xh'=2,'y'=4,'xl'=2,'zh'=4,'zl'=2,'core'=2] {'zh','zl'}, dimensions={0} | all-to-all | bytes 1048576 | tf_op jit(solution)/shard_map/all_to_all | solution.py:132
  113.8 0.8 broadcast_in_dim.16
  114.6 3.5 %all-to-all-start.2 = ((bf16[8,64,512]{2,1,0:T(8,128)(2,1)}), bf16[8,64,512]{2,1,0:T(8,128)(2,1)S(1)}, u32[]{:S(2)}, u32[]{:S(2)}) async-start(bf16[8,64,512]{2,1,0:T(8,128)(2,1)} %broadcast_in_dim.16), calls=%async_computation.2 | async-start | bytes 1048576 | tf_op jit(solution)/shard_map/all_to_all | solution.py:52
  118.1 15.2 %all-to-all-done.2 = bf16[8,64,512]{2,1,0:T(8,128)(2,1)S(1)} async-done(((bf16[8,64,512]{2,1,0:T(8,128)(2,1)}), bf16[8,64,512]{2,1,0:T(8,128)(2,1)S(1)}, u32[]{:S(2)}, u32[]{:S(2)}) %all-to-all-start.2) | async-done | bytes 524320 | tf_op jit(solution)/shard_map/all_to_all | solution.py:52
  133.4 0.4 collective-permute-start.20
  133.7 4.3 %constant_dynamic-slice_fusion = (bf16[512,2048]{1,0:T(8,128)(2,1)S(1)}, bf16[512,2048]{1,0:T(8,128)(2,1)S(1)}, bf16[512,2048]{1,0:T(8,128)(2,1)S(1)}, bf16[512,2048]{1,0:T(8,128)(2,1)S(1)}) fusion(bf16[2048,2048]{1,0:T(8,128)(2,1)} %param.7, s32[]{:T(128)S(6)} %select_n.71, s32[]{:T(128)S(6)} %select_n.69, s32[]{:T(128)S(6)} %select_n.68, s32[]{:T(128)S(6)} %select_n.70), kind=kLoop, calls=%fused_computation.61 | loop fusion | bytes 16777232 | tf_op jit(solution)/shard_map/dynamic_slice | solution.py:116
  138.1 0.1 collective-permute-start.19
  138.2 1.3 fusion.13
  139.4 4.3 %collective-permute-done.20 = bf16[512,512]{1,0:T(8,128)(2,1)S(1)} collective-permute-done((bf16[512,512]{1,0:T(8,128)(2,1)S(1)}, bf16[512,512]{1,0:T(8,128)(2,1)S(1)}, u32[]{:S(2)}, u32[]{:S(2)}) %collective-permute-start.20) | collective-permute-done | bytes 524320 | tf_op jit(solution)/shard_map/ppermute | solution.py:47
  143.7 1.3 fusion.15
  145.0 1.3 fusion.14
  146.3 1.9 %negate_convert_fusion = bf16[512,2048]{1,0:T(8,128)(2,1)S(1)} fusion(f32[512,2048]{1,0:T(8,128)S(1)} %fusion.15, f32[512,2048]{1,0:T(8,128)S(1)} %fusion.13, f32[512,2048]{1,0:T(8,128)S(1)} %fusion.14, bf16[512,512]{1,0:T(8,128)(2,1)S(1)} %collective-permute-done.21, bf16[512,2048]{1,0:T(8,128)(2,1)S(1)} %get-tuple-element.12), kind=kOutput, calls=%fused_computation | convolution fusion | flops 1078984704 | bytes 17301504 | tf_op jit(solution)/shard_map/dot_general | solution.py:43
  148.2 35.0 %all_to_all.21 = bf16[8,64,2048]{2,1,0:T(8,128)(2,1)S(1)} all-to-all(bf16[8,64,2048]{2,1,0:T(8,128)(2,1)S(1)} %bitcast.37), channel_id=1, replica_groups=mesh['xh'=2,'y'=4,'xl'=2,'zh'=4,'zl'=2,'core'=2] {'xh','y'}, dimensions={0} | all-to-all | bytes 4194304 | tf_op jit(solution)/shard_map/all_to_all | solution.py:142
  183.2 1.0 fusion.8
  (43 shorter events, 0.4 us)
Async XLA Ops:
  0.0 22.1 %copy-start.5 = (bf16[512,64]{0,1:T(8,128)(2,1)S(1)}, bf16[512,64]{0,1:T(8,128)(2,1)}, u32[]{:S(2)}) copy-start(bf16[512,64]{0,1:T(8,128)(2,1)} %param.6) | copy-start | bytes 196612
  1.0 21.1 %collective-permute-start = (bf16[32,1024]{1,0:T(8,128)(2,1)S(1)}, bf16[32,1024]{1,0:T(8,128)(2,1)S(1)}, u32[]{:S(2)}, u32[]{:S(2)}) collective-permute-start(bf16[32,1024]{1,0:T(8,128)(2,1)S(1)} %get-tuple-element.53), channel_id=1, source_target_pairs={{2,0},{3,1},{0,2},{1,3},{38,4},{39,5},{36,6},{37,7},{74,8},{75,9},... | collective-permute-start | bytes 196616 | tf_op jit(solution)/shard_map/ppermute | solution.py:89
  6.7 15.4 %collective-permute-start.1 = (bf16[32,1024]{1,0:T(8,128)(2,1)S(1)}, bf16[32,1024]{1,0:T(8,128)(2,1)S(1)}, u32[]{:S(2)}, u32[]{:S(2)}) collective-permute-start(bf16[32,1024]{1,0:T(8,128)(2,1)S(1)} %get-tuple-element.54), channel_id=1, source_target_pairs={{0,0},{1,1},{2,2},{3,3},{36,4},{37,5},{38,6},{39,7},{72,8},{73,9},... | collective-permute-start | bytes 196616 | tf_op jit(solution)/shard_map/ppermute | solution.py:88
  8.6 2.9 %collective-permute-start.2 = (bf16[32,1024]{1,0:T(8,128)(2,1)S(1)}, bf16[32,1024]{1,0:T(8,128)(2,1)S(1)}, u32[]{:S(2)}, u32[]{:S(2)}) collective-permute-start(bf16[32,1024]{1,0:T(8,128)(2,1)S(1)} %get-tuple-element.55), channel_id=1, source_target_pairs={{0,1},{1,0},{2,3},{3,2},{4,5},{5,4},{6,7},{7,6},{8,9},{9,8},{10,11... | collective-permute-start | bytes 196616 | tf_op jit(solution)/shard_map/ppermute | solution.py:47
  11.0 56.6 %collective-permute-start.16 = (bf16[512,1024]{1,0:T(8,128)(2,1)}, bf16[512,1024]{1,0:T(8,128)(2,1)S(1)}, u32[]{:S(2)}, u32[]{:S(2)}) collective-permute-start(bf16[512,1024]{1,0:T(8,128)(2,1)} %constant_dynamic-slice_fusion.4), channel_id=1, source_target_pairs={{0,1},{1,0},{2,3},{3,2},{4,5},{5,4},{6,7},{7,6},{8,9},{9,8},{10,11... | collective-permute-start | bytes 3145736 | tf_op jit(solution)/shard_map/ppermute | solution.py:47
  11.5 45.6 %collective-permute-start.12 = (bf16[64,1024]{1,0:T(8,128)(2,1)S(1)}, bf16[64,1024]{1,0:T(8,128)(2,1)S(1)}, u32[]{:S(2)}, u32[]{:S(2)}) collective-permute-start(bf16[64,1024]{1,0:T(8,128)(2,1)S(1)} %pad_maximum_fusion.4), channel_id=1, source_target_pairs={{0,16},{16,0},{1,17},{17,1},{2,18},{18,2},{3,19},{19,3},{4,20},{20... | collective-permute-start | bytes 393224 | tf_op jit(solution)/shard_map/ppermute | solution.py:47
  14.1 15.8 %collective-permute-start.4 = (bf16[64,1024]{1,0:T(8,128)(2,1)S(1)}, bf16[64,1024]{1,0:T(8,128)(2,1)S(1)}, u32[]{:S(2)}, u32[]{:S(2)}) collective-permute-start(bf16[64,1024]{1,0:T(8,128)(2,1)S(1)} %pad_maximum_fusion.4), channel_id=1, source_target_pairs={{0,14},{2,4},{4,2},{6,8},{8,6},{10,12},{12,10},{14,0},{1,15},{3,5}... | collective-permute-start | bytes 393224 | tf_op jit(solution)/shard_map/ppermute | solution.py:60
  22.1 7.8 %collective-permute-start.3 = (bf16[64,1024]{1,0:T(8,128)(2,1)S(1)}, bf16[64,1024]{1,0:T(8,128)(2,1)S(1)}, u32[]{:S(2)}, u32[]{:S(2)}) collective-permute-start(bf16[64,1024]{1,0:T(8,128)(2,1)S(1)} %pad_maximum_fusion.4), channel_id=1, source_target_pairs={{0,2},{2,0},{4,6},{6,4},{8,10},{10,8},{12,14},{14,12},{1,3},{3,1},... | collective-permute-start | bytes 393224 | tf_op jit(solution)/shard_map/ppermute | solution.py:58
  23.4 44.0 %all-to-all-start = ((bf16[8,64,1536]{2,1,0:T(8,128)(2,1)}), bf16[8,64,1536]{2,1,0:T(8,128)(2,1)S(1)}, u32[]{:S(2)}, u32[]{:S(2)}) async-start(bf16[8,64,1536]{2,1,0:T(8,128)(2,1)} %broadcast_in_dim.6), calls=%async_computation | async-start | bytes 3145728 | tf_op jit(solution)/shard_map/all_to_all | solution.py:52
  29.9 25.0 %collective-permute-start.11 = (bf16[128,1024]{1,0:T(8,128)(2,1)S(1)}, bf16[128,1024]{1,0:T(8,128)(2,1)S(1)}, u32[]{:S(2)}, u32[]{:S(2)}) collective-permute-start(bf16[128,1024]{1,0:T(8,128)(2,1)S(1)} %pad_maximum_fusion), channel_id=1, source_target_pairs={{0,16},{16,0},{1,17},{17,1},{2,18},{18,2},{3,19},{19,3},{4,20},{20... | collective-permute-start | bytes 786440 | tf_op jit(solution)/shard_map/ppermute | solution.py:47
  30.8 5.1 %collective-permute-start.7 = (bf16[64,1024]{1,0:T(8,128)(2,1)S(1)}, bf16[64,1024]{1,0:T(8,128)(2,1)S(1)}, u32[]{:S(2)}, u32[]{:S(2)}) collective-permute-start(bf16[64,1024]{1,0:T(8,128)(2,1)S(1)} %collective-permute-done.4), channel_id=1, source_target_pairs={{0,2},{2,0},{4,6},{6,4},{8,10},{10,8},{12,14},{14,12},{1,3},{3,1},... | collective-permute-start | bytes 393224 | tf_op jit(solution)/shard_map/ppermute | solution.py:58
  32.4 7.2 %collective-permute-start.5 = (bf16[64,1024]{1,0:T(8,128)(2,1)S(1)}, bf16[64,1024]{1,0:T(8,128)(2,1)S(1)}, u32[]{:S(2)}, u32[]{:S(2)}) collective-permute-start(bf16[64,1024]{1,0:T(8,128)(2,1)S(1)} %collective-permute-done.3), channel_id=1, source_target_pairs={{0,14},{2,4},{4,2},{6,8},{8,6},{10,12},{12,10},{14,0},{1,15},{3,5}... | collective-permute-start | bytes 393224 | tf_op jit(solution)/shard_map/ppermute | solution.py:60
  35.9 6.2 %collective-permute-start.8 = (bf16[64,1024]{1,0:T(8,128)(2,1)S(1)}, bf16[64,1024]{1,0:T(8,128)(2,1)S(1)}, u32[]{:S(2)}, u32[]{:S(2)}) collective-permute-start(bf16[64,1024]{1,0:T(8,128)(2,1)S(1)} %collective-permute-done.7), channel_id=1, source_target_pairs={{0,14},{2,4},{4,2},{6,8},{8,6},{10,12},{12,10},{14,0},{1,15},{3,5}... | collective-permute-start | bytes 393224 | tf_op jit(solution)/shard_map/ppermute | solution.py:60
  39.6 5.0 %collective-permute-start.6 = (bf16[64,1024]{1,0:T(8,128)(2,1)S(1)}, bf16[64,1024]{1,0:T(8,128)(2,1)S(1)}, u32[]{:S(2)}, u32[]{:S(2)}) collective-permute-start(bf16[64,1024]{1,0:T(8,128)(2,1)S(1)} %collective-permute-done.5), channel_id=1, source_target_pairs={{0,2},{2,0},{4,6},{6,4},{8,10},{10,8},{12,14},{14,12},{1,3},{3,1},... | collective-permute-start | bytes 393224 | tf_op jit(solution)/shard_map/ppermute | solution.py:58
  42.0 18.4 %collective-permute-start.13 = (bf16[128,1024]{1,0:T(8,128)(2,1)S(1)}, bf16[128,1024]{1,0:T(8,128)(2,1)S(1)}, u32[]{:S(2)}, u32[]{:S(2)}) collective-permute-start(bf16[128,1024]{1,0:T(8,128)(2,1)S(1)} %pad_maximum_fusion.1), channel_id=1, source_target_pairs={{0,16},{16,0},{1,17},{17,1},{2,18},{18,2},{3,19},{19,3},{4,20},{20... | collective-permute-start | bytes 786440 | tf_op jit(solution)/shard_map/ppermute | solution.py:47
  44.6 20.3 %collective-permute-start.14 = (bf16[128,1024]{1,0:T(8,128)(2,1)S(1)}, bf16[128,1024]{1,0:T(8,128)(2,1)S(1)}, u32[]{:S(2)}, u32[]{:S(2)}) collective-permute-start(bf16[128,1024]{1,0:T(8,128)(2,1)S(1)} %pad_maximum_fusion.2), channel_id=1, source_target_pairs={{0,16},{16,0},{1,17},{17,1},{2,18},{18,2},{3,19},{19,3},{4,20},{20... | collective-permute-start | bytes 786440 | tf_op jit(solution)/shard_map/ppermute | solution.py:47
  54.9 6.2 %collective-permute-start.9 = (bf16[64,1024]{1,0:T(8,128)(2,1)S(1)}, bf16[64,1024]{1,0:T(8,128)(2,1)S(1)}, u32[]{:S(2)}, u32[]{:S(2)}) collective-permute-start(bf16[64,1024]{1,0:T(8,128)(2,1)S(1)} %collective-permute-done.8), channel_id=1, source_target_pairs={{0,2},{2,0},{4,6},{6,4},{8,10},{10,8},{12,14},{14,12},{1,3},{3,1},... | collective-permute-start | bytes 393224 | tf_op jit(solution)/shard_map/ppermute | solution.py:58
  61.1 5.7 %collective-permute-start.15 = (bf16[64,1024]{1,0:T(8,128)(2,1)S(1)}, bf16[64,1024]{1,0:T(8,128)(2,1)S(1)}, u32[]{:S(2)}, u32[]{:S(2)}) collective-permute-start(bf16[64,1024]{1,0:T(8,128)(2,1)S(1)} %collective-permute-done.9), channel_id=1, source_target_pairs={{0,16},{16,0},{1,17},{17,1},{2,18},{18,2},{3,19},{19,3},{4,20},{20... | collective-permute-start | bytes 393224 | tf_op jit(solution)/shard_map/ppermute | solution.py:47
  62.3 4.5 %copy-start.1 = (bf16[256,1024]{1,0:T(8,128)(2,1)}, bf16[256,1024]{1,0:T(8,128)(2,1)S(1)}, u32[]{:S(2)}) copy-start(bf16[256,1024]{1,0:T(8,128)(2,1)S(1)} %get-tuple-element.39) | copy-start | bytes 1572868
  62.3 4.4 %copy-start.3 = (bf16[256,1024]{1,0:T(8,128)(2,1)}, bf16[256,1024]{1,0:T(8,128)(2,1)S(1)}, u32[]{:S(2)}) copy-start(bf16[256,1024]{1,0:T(8,128)(2,1)S(1)} %get-tuple-element.40) | copy-start | bytes 1572868
  67.4 1.6 copy-start
  67.5 4.4 %collective-permute-start.10 = (bf16[512,1024]{1,0:T(8,128)(2,1)S(1)}, bf16[512,1024]{1,0:T(8,128)(2,1)S(1)}, u32[]{:S(2)}, u32[]{:S(2)}) collective-permute-start(bf16[512,1024]{1,0:T(8,128)(2,1)S(1)} %bitcast.45), channel_id=1, source_target_pairs={{0,1},{1,0},{2,3},{3,2},{4,5},{5,4},{6,7},{7,6},{8,9},{9,8},{10,11... | collective-permute-start | bytes 3145736 | tf_op jit(solution)/shard_map/ppermute | solution.py:47
  69.6 1.0 copy-start.4
  69.6 2.2 %collective-permute-start.17 = (bf16[512,512]{1,0:T(8,128)(2,1)S(1)}, bf16[512,512]{1,0:T(8,128)(2,1)S(1)}, u32[]{:S(2)}, u32[]{:S(2)}) collective-permute-start(bf16[512,512]{1,0:T(8,128)(2,1)S(1)} %bitcast.39), channel_id=1, source_target_pairs={{0,1},{1,0},{2,3},{3,2},{4,5},{5,4},{6,7},{7,6},{8,9},{9,8},{10,11... | collective-permute-start | bytes 1572872 | tf_op jit(solution)/shard_map/ppermute | solution.py:47
  71.9 1.9 %copy-start.2 = (bf16[256,1024]{1,0:T(8,128)(2,1)S(1)}, bf16[256,1024]{1,0:T(8,128)(2,1)}, u32[]{:S(2)}) copy-start(bf16[256,1024]{1,0:T(8,128)(2,1)} %copy-done.1) | copy-start | bytes 1572868
  77.2 14.0 %collective-permute-start.18 = (bf16[512,512]{1,0:T(8,128)(2,1)S(1)}, bf16[512,512]{1,0:T(8,128)(2,1)S(1)}, u32[]{:S(2)}, u32[]{:S(2)}) collective-permute-start(bf16[512,512]{1,0:T(8,128)(2,1)S(1)} %dynamic-slice_convert_fusion), channel_id=1, source_target_pairs={{0,16},{16,0},{1,17},{17,1},{2,18},{18,2},{3,19},{19,3},{4,20},{20... | collective-permute-start | bytes 1572872 | tf_op jit(solution)/shard_map/ppermute | solution.py:47
  114.6 18.8 %all-to-all-start.2 = ((bf16[8,64,512]{2,1,0:T(8,128)(2,1)}), bf16[8,64,512]{2,1,0:T(8,128)(2,1)S(1)}, u32[]{:S(2)}, u32[]{:S(2)}) async-start(bf16[8,64,512]{2,1,0:T(8,128)(2,1)} %broadcast_in_dim.16), calls=%async_computation.2 | async-start | bytes 1048576 | tf_op jit(solution)/shard_map/all_to_all | solution.py:52
  133.4 10.3 %collective-permute-start.20 = (bf16[512,512]{1,0:T(8,128)(2,1)S(1)}, bf16[512,512]{1,0:T(8,128)(2,1)S(1)}, u32[]{:S(2)}, u32[]{:S(2)}) collective-permute-start(bf16[512,512]{1,0:T(8,128)(2,1)S(1)} %bitcast.42), channel_id=1, source_target_pairs={{0,16},{16,0},{1,17},{17,1},{2,18},{18,2},{3,19},{19,3},{4,20},{20... | collective-permute-start | bytes 1572872 | tf_op jit(solution)/shard_map/ppermute | solution.py:47
  138.1 6.9 %collective-permute-start.19 = (bf16[512,512]{1,0:T(8,128)(2,1)S(1)}, bf16[512,512]{1,0:T(8,128)(2,1)S(1)}, u32[]{:S(2)}, u32[]{:S(2)}) collective-permute-start(bf16[512,512]{1,0:T(8,128)(2,1)S(1)} %bitcast.43), channel_id=1, source_target_pairs={{0,1},{1,0},{2,3},{3,2},{4,5},{5,4},{6,7},{7,6},{8,9},{9,8},{10,11... | collective-permute-start | bytes 1572872 | tf_op jit(solution)/shard_map/ppermute | solution.py:47
  143.7 2.6 %collective-permute-start.21 = (bf16[512,512]{1,0:T(8,128)(2,1)S(1)}, bf16[512,512]{1,0:T(8,128)(2,1)S(1)}, u32[]{:S(2)}, u32[]{:S(2)}) collective-permute-start(bf16[512,512]{1,0:T(8,128)(2,1)S(1)} %collective-permute-done.20), channel_id=1, source_target_pairs={{0,1},{1,0},{2,3},{3,2},{4,5},{5,4},{6,7},{7,6},{8,9},{9,8},{10,11... | collective-permute-start | bytes 1572872 | tf_op jit(solution)/shard_map/ppermute | solution.py:47

commit v3 on v2

--- a/solution.py
+++ b/solution.py
@@ -25,7 +25,7 @@
     return index
 
 
-def nu_pairs(cross):
+def nu_pairs():
     pairs = []
     for xh in range(2):
         for y in range(4):
@@ -34,7 +34,7 @@
                     for zl in range(2):
                         for core in range(2):
                             away = STEPS[y] if zl == 0 else -STEPS[y]
-                            source = (xl, zh, xl ^ xh, (zh + away) % 4, zl ^ cross, core)
+                            source = (xl, zh, xl ^ xh, (zh + away) % 4, zl, core)
                             pairs.append((flat(source), flat((xh, y, xl, zh, zl, core))))
     return pairs
 
@@ -85,13 +85,15 @@
     zl = lax.axis_index("zl")
 
     bands = orbitals.T
-    same = lax.ppermute(half(bands, zl, 1), NAMES, nu_pairs(0))
-    cross = lax.ppermute(half(bands, 1 - zl, 1), NAMES, nu_pairs(1))
-    piece = jnp.concatenate([cross, same], axis=0)
-    both = gather(jnp.concatenate([piece, applied.T], axis=1), ROW, 8)
-    nu_a = both[:, :, :1024].reshape(512, 1024)
+    cross = swap(half(bands, 1 - zl, 1), "zl")
+    piece = jnp.concatenate([cross, half(bands, zl, 1)], axis=0)
+    piece = lax.ppermute(piece, NAMES, nu_pairs())
+    piece = jnp.concatenate([piece, applied.T], axis=1)
+    other = swap(piece, "xh")
+    both = gather(jnp.stack(ordered(lax.axis_index("xh"), piece, other)), "y", 4)
+    nu_a = jnp.transpose(both[:, :, :, :1024], (1, 0, 2, 3)).reshape(512, 1024)
     nu_b = swap(nu_a, "core")
-    own = both[:, :, 1024:].reshape(512, 512)
+    own = both[:, :, :, 1024:].reshape(512, 512)
     other = swap(own, "core")
     blocks = jnp.concatenate(ordered(core, own, other), axis=1)
     mu_own = half(bands, core, 1)
@@ -139,7 +141,7 @@
     result = result + dot(p2, fits[2])
     result = result + dot(p1, fits[1])
     result = result + dot(p3, fits[3])
-    terms = lax.all_to_all((-result).astype(BF).reshape(8, 64, 2048), ROW, 0, 0, tiled=False)
+    terms = lax.all_to_all((-result).astype(BF).reshape(8, 64, 2048), ("y", "xh"), 0, 0, tiled=False)
     return total(terms).astype(BF)
 
 

time: 186 us -> 182 us (0.978)
  waiting for transfers between devices: 53.6 us -> 44.3 us
  local copies, waits for them, and re-layouts: 17.1 us -> 23.2 us
  starting transfers between devices: 42.2 us -> 39 us
  other arithmetic: 2.02 us -> 4.21 us
    ppermute x13 -> x15, waiting for transfers between devices: 31.2 us -> 22 us  [swap(): return lax.ppermute(x, axis, PAIR)]
    unnamed x27, local copies, waits for them, and re-layouts: 6.39 us -> 11.7 us
    ppermute x3, waiting for transfers between devices: 4.11 us -> 0.01 us  [ring(): far.append(lax.ppermute(near[step - 1], Z, OUTER))]
    ppermute x4, waiting for transfers between devices: 3.09 us -> 7 us  [ring(): near.append(lax.ppermute(far[step - 1], Z, MATE))]
    ppermute x3, starting transfers between devices: 11.7 us -> 9.07 us  [ring(): far.append(lax.ppermute(near[step - 1], Z, OUTER))]
    ppermute x2 -> x1, starting transfers between devices: 7.62 us -> 5.18 us  [program(): piece = lax.ppermute(piece, NAMES, nu_pairs())]
    ppermute x13 -> x15, starting transfers between devices: 9.81 us -> 12.1 us  [swap(): return lax.ppermute(x, axis, PAIR)]
  transfers between devices with their start and end apart: 24 -> 25, of which waited for: 11 -> 8; matrix products, arithmetic and copies ran while one was open for 10% -> 15% of each run, Pallas kernels for 0% -> 0%
where the time goes in v3:
time: 182 us; the launch traced here: 180 us
  blocking collectives  57 us (31%)
  waiting for transfers between devices  44.3 us (24%)
  starting transfers between devices  39 us (21%)
  local copies, waits for them, and re-layouts  23.2 us (13%)
  matrix products  11.8 us (6%)
  other arithmetic  4.21 us (2%)
    all_to_all x1, blocking collectives, program(): lax.all_to_all((-result).astype(BF).reshape(8, 64, 2048), ('y', 'xh'), 0,...  34.3 us
    all_to_all x1, blocking collectives, program(): terms = lax.all_to_all(two.reshape(8, 64, 512), Z, 0, 0, tiled=False)  22.7 us
    ppermute x15, waiting for transfers between devices, swap(): return lax.ppermute(x, axis, PAIR)  22 us
    all_to_all x2, waiting for transfers between devices, gather(): return lax.all_to_all(copies, axes, 0, 0, tiled=False)  15.3 us
    ppermute x15, starting transfers between devices, swap(): return lax.ppermute(x, axis, PAIR)  12.1 us
    unnamed x27, local copies, waits for them, and re-layouts  11.7 us
    all_to_all x2, starting transfers between devices, gather(): return lax.all_to_all(copies, axes, 0, 0, tiled=False)  11.3 us
    dot_general x8, matrix products, dot(): lax.dot_general(a, b, (((0,), (0,)), ((), ())), preferred_element_type=F32)  10.5 us
  transfers between devices with their start and end apart: 25, of which 8 were waited for; matrix products, arithmetic and copies ran while one was open for 15% of the time, Pallas kernels for 0%

profile of v3, /device:TPU:8, one launch (start us, length us, event | category | flops | bytes accessed | tf_op | source)
XLA Modules:
  0.0 179.9 jit_solution(16787217552480142818)
XLA Ops:
  0.0 1.0 dynamic-slice_bitcast_fusion.3
  1.0 2.0 %collective-permute-start = (bf16[32,1024]{1,0:T(8,128)(2,1)S(1)}, bf16[32,1024]{1,0:T(8,128)(2,1)S(1)}, u32[]{:S(2)}, u32[]{:S(2)}) collective-permute-start(bf16[32,1024]{1,0:T(8,128)(2,1)S(1)} %get-tuple-element.57), channel_id=1, source_target_pairs={{0,2},{2,0},{1,3},{3,1},{4,6},{6,4},{5,7},{7,5},{8,10},{10,8},{9,1... | collective-permute-start | bytes 196616 | tf_op jit(solution)/shard_map/ppermute | solution.py:47
  3.0 2.3 %collective-permute-done = bf16[32,1024]{1,0:T(8,128)(2,1)S(1)} collective-permute-done((bf16[32,1024]{1,0:T(8,128)(2,1)S(1)}, bf16[32,1024]{1,0:T(8,128)(2,1)S(1)}, u32[]{:S(2)}, u32[]{:S(2)}) %collective-permute-start) | collective-permute-done | bytes 65568 | tf_op jit(solution)/shard_map/ppermute | solution.py:47
  5.4 5.2 %collective-permute-start.1 = (bf16[64,1024]{1,0:T(8,128)(2,1)S(1)}, bf16[64,1024]{1,0:T(8,128)(2,1)S(1)}, u32[]{:S(2)}, u32[]{:S(2)}) collective-permute-start(bf16[64,1024]{1,0:T(8,128)(2,1)S(1)} %pad_maximum_fusion.5), channel_id=1, source_target_pairs={{0,0},{1,1},{2,2},{3,3},{36,4},{37,5},{38,6},{39,7},{72,8},{73,9},... | collective-permute-start | bytes 393224 | tf_op jit(solution)/shard_map/ppermute | solution.py:90
  10.5 2.3 %constant_dynamic-slice_fusion.4 = bf16[512,1024]{1,0:T(8,128)(2,1)} fusion(bf16[512,2048]{1,0:T(8,128)(2,1)} %param.5, s32[]{:T(128)S(6)} %select_n.74), kind=kLoop, calls=%fused_computation.69 | loop fusion | bytes 2097156 | tf_op jit(solution)/shard_map/dynamic_slice | solution.py:66
  12.8 0.7 pad_maximum_fusion.6
  13.5 2.4 %collective-permute-start.13 = (bf16[64,1024]{1,0:T(8,128)(2,1)}, bf16[64,1024]{1,0:T(8,128)(2,1)}, u32[]{:S(2)}, u32[]{:S(2)}) collective-permute-start(bf16[64,1024]{1,0:T(8,128)(2,1)} %pad_maximum_fusion.6), channel_id=1, source_target_pairs={{0,16},{16,0},{1,17},{17,1},{2,18},{18,2},{3,19},{19,3},{4,20},{20... | collective-permute-start | bytes 393224 | tf_op jit(solution)/shard_map/ppermute | solution.py:47
  15.9 5.8 %collective-permute-start.5 = (bf16[64,1024]{1,0:T(8,128)(2,1)}, bf16[64,1024]{1,0:T(8,128)(2,1)S(1)}, u32[]{:S(2)}, u32[]{:S(2)}) collective-permute-start(bf16[64,1024]{1,0:T(8,128)(2,1)} %pad_maximum_fusion.6), channel_id=1, source_target_pairs={{0,14},{2,4},{4,2},{6,8},{8,6},{10,12},{12,10},{14,0},{1,15},{3,5}... | collective-permute-start | bytes 393224 | tf_op jit(solution)/shard_map/ppermute | solution.py:60
  21.7 2.7 %collective-permute-start.2 = (bf16[64,1536]{1,0:T(8,128)(2,1)S(1)}, bf16[64,1536]{1,0:T(8,128)(2,1)S(1)}, u32[]{:S(2)}, u32[]{:S(2)}) collective-permute-start(bf16[64,1536]{1,0:T(8,128)(2,1)S(1)} %pad_maximum_fusion.4), channel_id=1, source_target_pairs={{0,128},{128,0},{1,129},{129,1},{2,130},{130,2},{3,131},{131,3},{4... | collective-permute-start | bytes 589832 | tf_op jit(solution)/shard_map/ppermute | solution.py:47
  24.5 2.8 %collective-permute-done.4 = bf16[64,1024]{1,0:T(8,128)(2,1)S(1)} collective-permute-done((bf16[64,1024]{1,0:T(8,128)(2,1)}, bf16[64,1024]{1,0:T(8,128)(2,1)S(1)}, u32[]{:S(2)}, u32[]{:S(2)}) %collective-permute-start.4) | collective-permute-done | bytes 131104 | tf_op jit(solution)/shard_map/ppermute | solution.py:58
  27.2 2.8 %collective-permute-start.6 = (bf16[64,1024]{1,0:T(8,128)(2,1)S(1)}, bf16[64,1024]{1,0:T(8,128)(2,1)S(1)}, u32[]{:S(2)}, u32[]{:S(2)}) collective-permute-start(bf16[64,1024]{1,0:T(8,128)(2,1)S(1)} %collective-permute-done.4), channel_id=1, source_target_pairs={{0,14},{2,4},{4,2},{6,8},{8,6},{10,12},{12,10},{14,0},{1,15},{3,5}... | collective-permute-start | bytes 393224 | tf_op jit(solution)/shard_map/ppermute | solution.py:60
  30.2 0.7 pad_maximum_fusion.1
  30.9 4.2 %collective-permute-done.8 = bf16[64,1024]{1,0:T(8,128)(2,1)S(1)} collective-permute-done((bf16[64,1024]{1,0:T(8,128)(2,1)S(1)}, bf16[64,1024]{1,0:T(8,128)(2,1)S(1)}, u32[]{:S(2)}, u32[]{:S(2)}) %collective-permute-start.8) | collective-permute-done | bytes 131104 | tf_op jit(solution)/shard_map/ppermute | solution.py:58
  35.1 0.5 collective-permute-start.12
  35.6 0.6 collective-permute-start.9
  36.2 0.7 pad_maximum_fusion.2
  37.0 0.8 copy-done.1
  37.9 1.3 broadcast_in_dim.6
  39.2 7.8 %all-to-all-start = ((bf16[4,2,64,1536]{3,2,1,0:T(8,128)(2,1)}), bf16[4,2,64,1536]{3,2,1,0:T(8,128)(2,1)S(1)}, u32[]{:S(2)}, u32[]{:S(2)}) async-start(bf16[4,2,64,1536]{3,2,1,0:T(8,128)(2,1)} %broadcast_in_dim.6), calls=%async_computation | async-start | bytes 3145728 | tf_op jit(solution)/shard_map/all_to_all | solution.py:52
  47.0 0.5 collective-permute-start.14
  47.6 1.6 collective-permute-start.15
  49.2 1.2 collective-permute-start.10
  50.4 1.5 constant_dynamic-update-slice_fusion.23
  51.9 0.7 constant_dynamic-update-slice_fusion.11
  52.5 0.7 constant_dynamic-update-slice_fusion.10
  53.2 0.7 constant_dynamic-update-slice_fusion.9
  53.9 1.5 constant_dynamic-update-slice_fusion.22
  55.4 1.5 constant_dynamic-update-slice_fusion.21
  56.9 0.6 constant_dynamic-update-slice_fusion.20
  57.5 0.5 collective-permute-start.16
  58.0 0.7 constant_dynamic-update-slice_fusion.8
  58.7 0.6 constant_dynamic-update-slice_fusion.19
  59.4 0.6 constant_dynamic-update-slice_fusion.18
  60.0 0.6 constant_dynamic-update-slice_fusion.17
  60.6 1.9 %collective-permute-done.16 = bf16[64,1024]{1,0:T(8,128)(2,1)S(1)} collective-permute-done((bf16[64,1024]{1,0:T(8,128)(2,1)S(1)}, bf16[64,1024]{1,0:T(8,128)(2,1)S(1)}, u32[]{:S(2)}, u32[]{:S(2)}) %collective-permute-start.16) | collective-permute-done | bytes 131104 | tf_op jit(solution)/shard_map/ppermute | solution.py:47
  62.5 0.6 constant_dynamic-update-slice_fusion.16
  63.1 0.3 copy_bitcast_fusion
  63.5 1.2 copy-done
  64.7 0.6 broadcast_select_fusion.1
  65.3 0.3 collective-permute-start.18
  65.6 0.1 fusion.11
  65.7 0.6 copy-done.4
  66.3 0.7 fusion.12
  67.1 0.5 collective-permute-done.18
  67.6 1.9 %fusion.4 = f32[1024,1024]{1,0:T(8,128)S(1)} fusion(bf16[256,1024]{1,0:T(8,128)(2,1)} %get-tuple-element.40, bf16[512,1024]{1,0:T(8,128)(2,1)S(1)} %collective-permute-done.11), kind=kOutput, calls=%fused_computation.10 | convolution fusion | flops 536870912 | bytes 5242880 | tf_op jit(solution)/shard_map/dot_general | solution.py:43
  69.5 0.8 fusion.6
  70.3 1.3 multiply_convert_fusion
  71.6 1.3 fusion
  72.9 0.6 collective-permute-start.19
  73.6 13.4 %collective-permute-done.19 = bf16[512,512]{1,0:T(8,128)(2,1)S(1)} collective-permute-done((bf16[512,512]{1,0:T(8,128)(2,1)S(1)}, bf16[512,512]{1,0:T(8,128)(2,1)S(1)}, u32[]{:S(2)}, u32[]{:S(2)}) %collective-permute-start.19) | collective-permute-done | bytes 524320 | tf_op jit(solution)/shard_map/ppermute | solution.py:47
  87.0 0.2 add_convert_fusion
  87.2 22.7 %all_to_all.20 = bf16[8,64,512]{2,1,0:T(8,128)(2,1)S(1)} all-to-all(bf16[8,64,512]{2,1,0:T(8,128)(2,1)S(1)} %bitcast.47), channel_id=1, replica_groups=mesh['xh'=2,'y'=4,'xl'=2,'zh'=4,'zl'=2,'core'=2] {'zh','zl'}, dimensions={0} | all-to-all | bytes 1048576 | tf_op jit(solution)/shard_map/all_to_all | solution.py:134
  109.9 0.8 broadcast_in_dim.16
  110.7 3.5 %all-to-all-start.2 = ((bf16[8,64,512]{2,1,0:T(8,128)(2,1)}), bf16[8,64,512]{2,1,0:T(8,128)(2,1)S(1)}, u32[]{:S(2)}, u32[]{:S(2)}) async-start(bf16[8,64,512]{2,1,0:T(8,128)(2,1)} %broadcast_in_dim.16), calls=%async_computation.2 | async-start | bytes 1048576 | tf_op jit(solution)/shard_map/all_to_all | solution.py:52
  114.3 15.3 %all-to-all-done.2 = bf16[8,64,512]{2,1,0:T(8,128)(2,1)S(1)} async-done(((bf16[8,64,512]{2,1,0:T(8,128)(2,1)}), bf16[8,64,512]{2,1,0:T(8,128)(2,1)S(1)}, u32[]{:S(2)}, u32[]{:S(2)}) %all-to-all-start.2) | async-done | bytes 524320 | tf_op jit(solution)/shard_map/all_to_all | solution.py:52
  129.5 0.7 collective-permute-start.21
  130.3 4.3 %constant_dynamic-slice_fusion = (bf16[512,2048]{1,0:T(8,128)(2,1)S(1)}, bf16[512,2048]{1,0:T(8,128)(2,1)S(1)}, bf16[512,2048]{1,0:T(8,128)(2,1)S(1)}, bf16[512,2048]{1,0:T(8,128)(2,1)S(1)}) fusion(bf16[2048,2048]{1,0:T(8,128)(2,1)} %param.7, s32[]{:T(128)S(6)} %select_n.86, s32[]{:T(128)S(6)} %select_n.84, s32[]{:T(128)S(6)} %select_n.83, s32[]{:T(128)S(6)} %select_n.85), kind=kLoop, calls=%fused_computation.65 | loop fusion | bytes 16777232 | tf_op jit(solution)/shard_map/dynamic_slice | solution.py:118
  134.7 1.3 fusion.13
  136.0 3.9 %collective-permute-done.21 = bf16[512,512]{1,0:T(8,128)(2,1)S(1)} collective-permute-done((bf16[512,512]{1,0:T(8,128)(2,1)S(1)}, bf16[512,512]{1,0:T(8,128)(2,1)S(1)}, u32[]{:S(2)}, u32[]{:S(2)}) %collective-permute-start.21) | collective-permute-done | bytes 524320 | tf_op jit(solution)/shard_map/ppermute | solution.py:47
  139.9 1.3 fusion.15
  141.2 1.3 fusion.14
  142.5 2.0 %negate_convert_fusion = bf16[512,2048]{1,0:T(8,128)(2,1)S(1)} fusion(f32[512,2048]{1,0:T(8,128)S(1)} %fusion.15, f32[512,2048]{1,0:T(8,128)S(1)} %fusion.13, f32[512,2048]{1,0:T(8,128)S(1)} %fusion.14, bf16[512,512]{1,0:T(8,128)(2,1)S(1)} %collective-permute-done.22, bf16[512,2048]{1,0:T(8,128)(2,1)S(1)} %get-tuple-element.12), kind=kOutput, calls=%fused_computation | convolution fusion | flops 1078984704 | bytes 17301504 | tf_op jit(solution)/shard_map/dot_general | solution.py:43
  144.5 34.3 %all_to_all.21 = bf16[8,64,2048]{2,1,0:T(8,128)(2,1)S(1)} all-to-all(bf16[8,64,2048]{2,1,0:T(8,128)(2,1)S(1)} %bitcast.44), channel_id=1, replica_groups=mesh['xh'=2,'y'=4,'xl'=2,'zh'=4,'zl'=2,'core'=2] {'y','xh'}, dimensions={0} | all-to-all | bytes 4194304 | tf_op jit(solution)/shard_map/all_to_all | solution.py:144
  178.8 1.0 fusion.8
  (48 shorter events, 0.9 us)
Async XLA Ops:
  0.0 21.7 %copy-start.5 = (bf16[512,64]{0,1:T(8,128)(2,1)S(1)}, bf16[512,64]{0,1:T(8,128)(2,1)}, u32[]{:S(2)}) copy-start(bf16[512,64]{0,1:T(8,128)(2,1)} %param.6) | copy-start | bytes 196612
  1.0 4.4 %collective-permute-start = (bf16[32,1024]{1,0:T(8,128)(2,1)S(1)}, bf16[32,1024]{1,0:T(8,128)(2,1)S(1)}, u32[]{:S(2)}, u32[]{:S(2)}) collective-permute-start(bf16[32,1024]{1,0:T(8,128)(2,1)S(1)} %get-tuple-element.57), channel_id=1, source_target_pairs={{0,2},{2,0},{1,3},{3,1},{4,6},{6,4},{5,7},{7,5},{8,10},{10,8},{9,1... | collective-permute-start | bytes 196616 | tf_op jit(solution)/shard_map/ppermute | solution.py:47
  3.0 9.8 %collective-permute-start.3 = (bf16[32,1024]{1,0:T(8,128)(2,1)S(1)}, bf16[32,1024]{1,0:T(8,128)(2,1)S(1)}, u32[]{:S(2)}, u32[]{:S(2)}) collective-permute-start(bf16[32,1024]{1,0:T(8,128)(2,1)S(1)} %get-tuple-element.59), channel_id=1, source_target_pairs={{0,1},{1,0},{2,3},{3,2},{4,5},{5,4},{6,7},{7,6},{8,9},{9,8},{10,11... | collective-permute-start | bytes 196616 | tf_op jit(solution)/shard_map/ppermute | solution.py:47
  5.4 16.3 %collective-permute-start.1 = (bf16[64,1024]{1,0:T(8,128)(2,1)S(1)}, bf16[64,1024]{1,0:T(8,128)(2,1)S(1)}, u32[]{:S(2)}, u32[]{:S(2)}) collective-permute-start(bf16[64,1024]{1,0:T(8,128)(2,1)S(1)} %pad_maximum_fusion.5), channel_id=1, source_target_pairs={{0,0},{1,1},{2,2},{3,3},{36,4},{37,5},{38,6},{39,7},{72,8},{73,9},... | collective-permute-start | bytes 393224 | tf_op jit(solution)/shard_map/ppermute | solution.py:90
  12.8 50.7 %collective-permute-start.17 = (bf16[512,1024]{1,0:T(8,128)(2,1)}, bf16[512,1024]{1,0:T(8,128)(2,1)S(1)}, u32[]{:S(2)}, u32[]{:S(2)}) collective-permute-start(bf16[512,1024]{1,0:T(8,128)(2,1)} %constant_dynamic-slice_fusion.4), channel_id=1, source_target_pairs={{0,1},{1,0},{2,3},{3,2},{4,5},{5,4},{6,7},{7,6},{8,9},{9,8},{10,11... | collective-permute-start | bytes 3145736 | tf_op jit(solution)/shard_map/ppermute | solution.py:47
  13.5 40.4 %collective-permute-start.13 = (bf16[64,1024]{1,0:T(8,128)(2,1)}, bf16[64,1024]{1,0:T(8,128)(2,1)}, u32[]{:S(2)}, u32[]{:S(2)}) collective-permute-start(bf16[64,1024]{1,0:T(8,128)(2,1)} %pad_maximum_fusion.6), channel_id=1, source_target_pairs={{0,16},{16,0},{1,17},{17,1},{2,18},{18,2},{3,19},{19,3},{4,20},{20... | collective-permute-start | bytes 393224 | tf_op jit(solution)/shard_map/ppermute | solution.py:47
  15.9 14.1 %collective-permute-start.5 = (bf16[64,1024]{1,0:T(8,128)(2,1)}, bf16[64,1024]{1,0:T(8,128)(2,1)S(1)}, u32[]{:S(2)}, u32[]{:S(2)}) collective-permute-start(bf16[64,1024]{1,0:T(8,128)(2,1)} %pad_maximum_fusion.6), channel_id=1, source_target_pairs={{0,14},{2,4},{4,2},{6,8},{8,6},{10,12},{12,10},{14,0},{1,15},{3,5}... | collective-permute-start | bytes 393224 | tf_op jit(solution)/shard_map/ppermute | solution.py:60
  21.7 5.6 %collective-permute-start.4 = (bf16[64,1024]{1,0:T(8,128)(2,1)}, bf16[64,1024]{1,0:T(8,128)(2,1)S(1)}, u32[]{:S(2)}, u32[]{:S(2)}) collective-permute-start(bf16[64,1024]{1,0:T(8,128)(2,1)} %pad_maximum_fusion.6), channel_id=1, source_target_pairs={{0,2},{2,0},{4,6},{6,4},{8,10},{10,8},{12,14},{14,12},{1,3},{3,1},... | collective-permute-start | bytes 393224 | tf_op jit(solution)/shard_map/ppermute | solution.py:58
  21.7 15.2 %collective-permute-start.2 = (bf16[64,1536]{1,0:T(8,128)(2,1)S(1)}, bf16[64,1536]{1,0:T(8,128)(2,1)S(1)}, u32[]{:S(2)}, u32[]{:S(2)}) collective-permute-start(bf16[64,1536]{1,0:T(8,128)(2,1)S(1)} %pad_maximum_fusion.4), channel_id=1, source_target_pairs={{0,128},{128,0},{1,129},{129,1},{2,130},{130,2},{3,131},{131,3},{4... | collective-permute-start | bytes 589832 | tf_op jit(solution)/shard_map/ppermute | solution.py:47
  27.2 8.4 %collective-permute-start.6 = (bf16[64,1024]{1,0:T(8,128)(2,1)S(1)}, bf16[64,1024]{1,0:T(8,128)(2,1)S(1)}, u32[]{:S(2)}, u32[]{:S(2)}) collective-permute-start(bf16[64,1024]{1,0:T(8,128)(2,1)S(1)} %collective-permute-done.4), channel_id=1, source_target_pairs={{0,14},{2,4},{4,2},{6,8},{8,6},{10,12},{12,10},{14,0},{1,15},{3,5}... | collective-permute-start | bytes 393224 | tf_op jit(solution)/shard_map/ppermute | solution.py:60
  30.0 5.1 %collective-permute-start.8 = (bf16[64,1024]{1,0:T(8,128)(2,1)S(1)}, bf16[64,1024]{1,0:T(8,128)(2,1)S(1)}, u32[]{:S(2)}, u32[]{:S(2)}) collective-permute-start(bf16[64,1024]{1,0:T(8,128)(2,1)S(1)} %collective-permute-done.5), channel_id=1, source_target_pairs={{0,2},{2,0},{4,6},{6,4},{8,10},{10,8},{12,14},{14,12},{1,3},{3,1},... | collective-permute-start | bytes 393224 | tf_op jit(solution)/shard_map/ppermute | solution.py:58
  35.1 14.1 %collective-permute-start.12 = (bf16[128,1024]{1,0:T(8,128)(2,1)}, bf16[128,1024]{1,0:T(8,128)(2,1)}, u32[]{:S(2)}, u32[]{:S(2)}) collective-permute-start(bf16[128,1024]{1,0:T(8,128)(2,1)} %pad_maximum_fusion.1), channel_id=1, source_target_pairs={{0,16},{16,0},{1,17},{17,1},{2,18},{18,2},{3,19},{19,3},{4,20},{20... | collective-permute-start | bytes 786440 | tf_op jit(solution)/shard_map/ppermute | solution.py:47
  35.6 11.4 %collective-permute-start.9 = (bf16[64,1024]{1,0:T(8,128)(2,1)S(1)}, bf16[64,1024]{1,0:T(8,128)(2,1)S(1)}, u32[]{:S(2)}, u32[]{:S(2)}) collective-permute-start(bf16[64,1024]{1,0:T(8,128)(2,1)S(1)} %collective-permute-done.8), channel_id=1, source_target_pairs={{0,14},{2,4},{4,2},{6,8},{8,6},{10,12},{12,10},{14,0},{1,15},{3,5}... | collective-permute-start | bytes 393224 | tf_op jit(solution)/shard_map/ppermute | solution.py:60
  36.9 0.8 copy-start.1
  36.9 1.0 copy-start.3
  37.7 9.8 %collective-permute-start.7 = (bf16[64,1024]{1,0:T(8,128)(2,1)S(1)}, bf16[64,1024]{1,0:T(8,128)(2,1)S(1)}, u32[]{:S(2)}, u32[]{:S(2)}) collective-permute-start(bf16[64,1024]{1,0:T(8,128)(2,1)S(1)} %collective-permute-done.6), channel_id=1, source_target_pairs={{0,2},{2,0},{4,6},{6,4},{8,10},{10,8},{12,14},{14,12},{1,3},{3,1},... | collective-permute-start | bytes 393224 | tf_op jit(solution)/shard_map/ppermute | solution.py:58
  39.2 23.9 %all-to-all-start = ((bf16[4,2,64,1536]{3,2,1,0:T(8,128)(2,1)}), bf16[4,2,64,1536]{3,2,1,0:T(8,128)(2,1)S(1)}, u32[]{:S(2)}, u32[]{:S(2)}) async-start(bf16[4,2,64,1536]{3,2,1,0:T(8,128)(2,1)} %broadcast_in_dim.6), calls=%async_computation | async-start | bytes 3145728 | tf_op jit(solution)/shard_map/all_to_all | solution.py:52
  47.0 9.8 %collective-permute-start.14 = (bf16[128,1024]{1,0:T(8,128)(2,1)}, bf16[128,1024]{1,0:T(8,128)(2,1)S(1)}, u32[]{:S(2)}, u32[]{:S(2)}) collective-permute-start(bf16[128,1024]{1,0:T(8,128)(2,1)} %pad_maximum_fusion.2), channel_id=1, source_target_pairs={{0,16},{16,0},{1,17},{17,1},{2,18},{18,2},{3,19},{19,3},{4,20},{20... | collective-permute-start | bytes 786440 | tf_op jit(solution)/shard_map/ppermute | solution.py:47
  47.6 11.1 %collective-permute-start.15 = (bf16[128,1024]{1,0:T(8,128)(2,1)S(1)}, bf16[128,1024]{1,0:T(8,128)(2,1)S(1)}, u32[]{:S(2)}, u32[]{:S(2)}) collective-permute-start(bf16[128,1024]{1,0:T(8,128)(2,1)S(1)} %pad_maximum_fusion.3), channel_id=1, source_target_pairs={{0,16},{16,0},{1,17},{17,1},{2,18},{18,2},{3,19},{19,3},{4,20},{20... | collective-permute-start | bytes 786440 | tf_op jit(solution)/shard_map/ppermute | solution.py:47
  49.2 8.3 %collective-permute-start.10 = (bf16[64,1024]{1,0:T(8,128)(2,1)S(1)}, bf16[64,1024]{1,0:T(8,128)(2,1)S(1)}, u32[]{:S(2)}, u32[]{:S(2)}) collective-permute-start(bf16[64,1024]{1,0:T(8,128)(2,1)S(1)} %collective-permute-done.9), channel_id=1, source_target_pairs={{0,2},{2,0},{4,6},{6,4},{8,10},{10,8},{12,14},{14,12},{1,3},{3,1},... | collective-permute-start | bytes 393224 | tf_op jit(solution)/shard_map/ppermute | solution.py:58
  57.5 5.0 %collective-permute-start.16 = (bf16[64,1024]{1,0:T(8,128)(2,1)S(1)}, bf16[64,1024]{1,0:T(8,128)(2,1)S(1)}, u32[]{:S(2)}, u32[]{:S(2)}) collective-permute-start(bf16[64,1024]{1,0:T(8,128)(2,1)S(1)} %collective-permute-done.10), channel_id=1, source_target_pairs={{0,16},{16,0},{1,17},{17,1},{2,18},{18,2},{3,19},{19,3},{4,20},{20... | collective-permute-start | bytes 393224 | tf_op jit(solution)/shard_map/ppermute | solution.py:47
  63.1 1.6 copy-start
  63.4 4.2 %collective-permute-start.11 = (bf16[512,1024]{1,0:T(8,128)(2,1)S(1)}, bf16[512,1024]{1,0:T(8,128)(2,1)S(1)}, u32[]{:S(2)}, u32[]{:S(2)}) collective-permute-start(bf16[512,1024]{1,0:T(8,128)(2,1)S(1)} %bitcast.52), channel_id=1, source_target_pairs={{0,1},{1,0},{2,3},{3,2},{4,5},{5,4},{6,7},{7,6},{8,9},{9,8},{10,11... | collective-permute-start | bytes 3145736 | tf_op jit(solution)/shard_map/ppermute | solution.py:47
  65.3 1.0 copy-start.4
  65.3 2.2 %collective-permute-start.18 = (bf16[512,512]{1,0:T(8,128)(2,1)S(1)}, bf16[512,512]{1,0:T(8,128)(2,1)S(1)}, u32[]{:S(2)}, u32[]{:S(2)}) collective-permute-start(bf16[512,512]{1,0:T(8,128)(2,1)S(1)} %bitcast.46), channel_id=1, source_target_pairs={{0,1},{1,0},{2,3},{3,2},{4,5},{5,4},{6,7},{7,6},{8,9},{9,8},{10,11... | collective-permute-start | bytes 1572872 | tf_op jit(solution)/shard_map/ppermute | solution.py:47
  67.6 1.9 %copy-start.2 = (bf16[256,1024]{1,0:T(8,128)(2,1)S(1)}, bf16[256,1024]{1,0:T(8,128)(2,1)}, u32[]{:S(2)}) copy-start(bf16[256,1024]{1,0:T(8,128)(2,1)} %get-tuple-element.43) | copy-start | bytes 1572868
  72.9 14.1 %collective-permute-start.19 = (bf16[512,512]{1,0:T(8,128)(2,1)S(1)}, bf16[512,512]{1,0:T(8,128)(2,1)S(1)}, u32[]{:S(2)}, u32[]{:S(2)}) collective-permute-start(bf16[512,512]{1,0:T(8,128)(2,1)S(1)} %dynamic-slice_convert_fusion), channel_id=1, source_target_pairs={{0,16},{16,0},{1,17},{17,1},{2,18},{18,2},{3,19},{19,3},{4,20},{20... | collective-permute-start | bytes 1572872 | tf_op jit(solution)/shard_map/ppermute | solution.py:47
  110.7 18.8 %all-to-all-start.2 = ((bf16[8,64,512]{2,1,0:T(8,128)(2,1)}), bf16[8,64,512]{2,1,0:T(8,128)(2,1)S(1)}, u32[]{:S(2)}, u32[]{:S(2)}) async-start(bf16[8,64,512]{2,1,0:T(8,128)(2,1)} %broadcast_in_dim.16), calls=%async_computation.2 | async-start | bytes 1048576 | tf_op jit(solution)/shard_map/all_to_all | solution.py:52
  129.5 10.4 %collective-permute-start.21 = (bf16[512,512]{1,0:T(8,128)(2,1)S(1)}, bf16[512,512]{1,0:T(8,128)(2,1)S(1)}, u32[]{:S(2)}, u32[]{:S(2)}) collective-permute-start(bf16[512,512]{1,0:T(8,128)(2,1)S(1)} %bitcast.49), channel_id=1, source_target_pairs={{0,16},{16,0},{1,17},{17,1},{2,18},{18,2},{3,19},{19,3},{4,20},{20... | collective-permute-start | bytes 1572872 | tf_op jit(solution)/shard_map/ppermute | solution.py:47
  134.6 6.6 %collective-permute-start.20 = (bf16[512,512]{1,0:T(8,128)(2,1)S(1)}, bf16[512,512]{1,0:T(8,128)(2,1)S(1)}, u32[]{:S(2)}, u32[]{:S(2)}) collective-permute-start(bf16[512,512]{1,0:T(8,128)(2,1)S(1)} %bitcast.50), channel_id=1, source_target_pairs={{0,1},{1,0},{2,3},{3,2},{4,5},{5,4},{6,7},{7,6},{8,9},{9,8},{10,11... | collective-permute-start | bytes 1572872 | tf_op jit(solution)/shard_map/ppermute | solution.py:47
  139.9 2.6 %collective-permute-start.22 = (bf16[512,512]{1,0:T(8,128)(2,1)S(1)}, bf16[512,512]{1,0:T(8,128)(2,1)S(1)}, u32[]{:S(2)}, u32[]{:S(2)}) collective-permute-start(bf16[512,512]{1,0:T(8,128)(2,1)S(1)} %collective-permute-done.21), channel_id=1, source_target_pairs={{0,1},{1,0},{2,3},{3,2},{4,5},{5,4},{6,7},{7,6},{8,9},{9,8},{10,11... | collective-permute-start | bytes 1572872 | tf_op jit(solution)/shard_map/ppermute | solution.py:47

commit v4 on v3

--- a/solution.py
+++ b/solution.py
@@ -1,6 +1,8 @@
 import jax
 import jax.numpy as jnp
 from jax import lax
+from jax.experimental import pallas as pl
+from jax.experimental.pallas import tpu as pltpu
 from jax.sharding import Mesh
 from jax.sharding import PartitionSpec as P
 
@@ -79,6 +81,58 @@
     return first, second
 
 
+def weigh(core, nu_a, nu_b, near, away, own, other):
+    def body(core_ref, nu_a_ref, nu_b_ref, *refs):
+        near_refs, away_refs = refs[:8], refs[8:13]
+        own_ref, other_ref, out_ref, mu_a, mu_b = refs[13:]
+        across = {
+            0: (away_refs[0], 0),
+            1: (away_refs[1], 0),
+            7: (away_refs[1], 64),
+            2: (away_refs[2], 0),
+            6: (away_refs[2], 64),
+            3: (away_refs[3], 0),
+            5: (away_refs[3], 64),
+            4: (away_refs[4], 0),
+        }
+        for y in range(4):
+            for o in range(2):
+                n = ORDER[y * 2 + o]
+                for x, (ref, start) in enumerate(((near_refs[n], 0), across[n])):
+                    row = (y * 2 + x) * 64 + o * 32
+                    mu_a[row : row + 32, :] = ref[start : start + 32, :]
+                    mu_b[row : row + 32, :] = ref[start + 32 : start + 64, :]
+
+        mine = core_ref[0]
+
+        def tile(t, carry):
+            start = pl.multiple_of(t * 256, 256)
+            part_a = nu_a_ref[:, :, :, pl.ds(start, 256)].reshape(512, 256)
+            part_b = nu_b_ref[:, :, :, pl.ds(start, 256)].reshape(512, 256)
+            density = dot(part_a, mu_a[...]) + dot(part_b, mu_b[...])
+            row = pl.multiple_of((t % 2) * 256, 256)
+            ours = own_ref[pl.ds(row, 256), :]
+            theirs = other_ref[pl.ds(row, 256), :]
+            factor = jnp.where(t // 2 == mine, ours.astype(F32), theirs.astype(F32))
+            out_ref[pl.ds(start, 256), :] = (density * factor).astype(BF)
+            return carry
+
+        lax.fori_loop(0, 4, tile, 0)
+
+    vmem = pl.BlockSpec(memory_space=pltpu.VMEM)
+    return pl.pallas_call(
+        body,
+        out_shape=jax.ShapeDtypeStruct((1024, 1024), BF),
+        in_specs=[pl.BlockSpec(memory_space=pltpu.SMEM)] + [vmem] * 17,
+        out_specs=vmem,
+        scratch_shapes=[pltpu.VMEM((512, 1024), BF), pltpu.VMEM((512, 1024), BF)],
+        compiler_params=pltpu.CompilerParams(vmem_limit_bytes=32 << 20),
+        cost_estimate=pl.CostEstimate(
+            flops=2 * 1024**3, bytes_accessed=10 << 20, transcendentals=0
+        ),
+    )(core.reshape(1), nu_a, nu_b, *near, *away, own, other)
+
+
 def program(orbitals, kernel, applied, fit):
     core = lax.axis_index("core")
     xl = lax.axis_index("xl")
@@ -91,40 +145,25 @@
     piece = jnp.concatenate([piece, applied.T], axis=1)
     other = swap(piece, "xh")
     both = gather(jnp.stack(ordered(lax.axis_index("xh"), piece, other)), "y", 4)
-    nu_a = jnp.transpose(both[:, :, :, :1024], (1, 0, 2, 3)).reshape(512, 1024)
-    nu_b = swap(nu_a, "core")
-    own = both[:, :, :, 1024:].reshape(512, 512)
-    other = swap(own, "core")
-    blocks = jnp.concatenate(ordered(core, own, other), axis=1)
+    partner = swap(both, "core")
+    sides = ordered(core, both[:, :, :, 1024:], partner[:, :, :, 1024:])
+    blocks = jnp.concatenate(sides, axis=3).reshape(512, 1024)
     mu_own = half(bands, core, 1)
     mu_other = swap(half(bands, 1 - core, 1), "core")
     near = ring(jnp.concatenate([mu_own, mu_other], axis=0))
-    away = [None] * 8
-    away[0] = swap(near[0], "xl")
-    for a, b in ((1, 7), (2, 6), (3, 5)):
-        two = swap(jnp.concatenate([near[a], near[b]], axis=0), "xl")
-        away[a], away[b] = two[:64], two[64:]
-    away[4] = swap(near[4], "xl")
-    mu = [
-        jnp.concatenate([pieces[n][k * 32 : k * 32 + 32] for n in ORDER], axis=0)
-        for pieces in (near, away)
-        for k in range(2)
-    ]
+    away = []
+    for a, b in ((0, 0), (1, 7), (2, 6), (3, 5), (4, 4)):
+        piece = near[a] if a == b else jnp.concatenate([near[a], near[b]], axis=0)
+        away.append(swap(piece, "xl"))
     own = half(kernel, core, 1)
     other = swap(half(kernel, 1 - core, 1), "core")
-    weights = jnp.concatenate(ordered(core, own, other), axis=0)
     place = core * 2 + xl
     fits = [
         lax.dynamic_slice_in_dim(fit, jnp.bitwise_xor(place, k) * 512, 512, 0) for k in range(4)
     ]
     fits = lax.optimization_barrier(fits)
 
-    density = dot(nu_a[:256], mu[0])
-    density = density + dot(nu_b[:256], mu[1])
-    density = density + dot(nu_a[256:], mu[2])
-    density = density + dot(nu_b[256:], mu[3])
-    weighted = (density * weights.astype(F32)).astype(BF)
-    weighted = lax.optimization_barrier(weighted)
+    weighted = weigh(core, both, partner, near, away, own, other)
 
     partial = lax.dot_general(
         weighted, blocks, (((0,), (1,)), ((), ())), preferred_element_type=F32

time: 182 us -> 201 us (1.10)
  waiting for transfers between devices: 44.3 us -> 64.5 us
  blocking collectives: 57 us -> 74.8 us
  local copies, waits for them, and re-layouts: 23.2 us -> 7.49 us
  Pallas kernels: 0 us -> 4.85 us
  matrix products: 11.8 us -> 7.1 us
  starting transfers between devices: 39 us -> 34.8 us
    all_to_all x0 -> x1, blocking collectives: none -> 22.9 us  [gather(): return lax.all_to_all(copies, axes, 0, 0, tiled=False)]
    unnamed x27 -> x2, local copies, waits for them, and re-layouts: 11.7 us -> 0.01 us
    ppermute x15 -> x14, waiting for transfers between devices: 22 us -> 30.7 us  [swap(): return lax.ppermute(x, axis, PAIR)]
    ppermute x1, waiting for transfers between devices: 0.01 us -> 8.62 us  [program(): piece = lax.ppermute(piece, NAMES, nu_pairs())]
    all_to_all x2 -> x1, starting transfers between devices: 11.3 us -> 3.49 us  [gather(): return lax.all_to_all(copies, axes, 0, 0, tiled=False)]
    ppermute x3, waiting for transfers between devices: 0.01 us -> 7.59 us  [ring(): far.append(lax.ppermute(near[step - 1], Z, OUTER))]
    pallas_call x0 -> x1, Pallas kernels: none -> 4.85 us  [weigh(): pl.pallas_call(body, out_shape=jax.ShapeDtypeStruct((1024, 1024), BF), in...]
    dot_general x8 -> x4, matrix products: 10.5 us -> 5.79 us  [dot(): lax.dot_general(a, b, (((0,), (0,)), ((), ())), preferred_element_type=F32)]
  transfers between devices with their start and end apart: 25 -> 23, of which waited for: 8 -> 14; matrix products, arithmetic and copies ran while one was open for 15% -> 5% of each run, Pallas kernels for 0% -> 0%
where the time goes in v4:
time: 201 us; the launch traced here: 198 us
  blocking collectives  74.8 us (37%)
  waiting for transfers between devices  64.5 us (32%)
  starting transfers between devices  34.8 us (17%)
  local copies, waits for them, and re-layouts  7.49 us (4%)
  matrix products  7.1 us (4%)
  Pallas kernels  4.85 us (2%)
  other arithmetic  4.38 us (2%)
    all_to_all x1, blocking collectives, program(): lax.all_to_all((-result).astype(BF).reshape(8, 64, 2048), ('y', 'xh'), 0,...  31.3 us
    ppermute x14, waiting for transfers between devices, swap(): return lax.ppermute(x, axis, PAIR)  30.7 us
    all_to_all x1, blocking collectives, gather(): return lax.all_to_all(copies, axes, 0, 0, tiled=False)  22.9 us
    all_to_all x1, blocking collectives, program(): terms = lax.all_to_all(two.reshape(8, 64, 512), Z, 0, 0, tiled=False)  20.6 us
    ppermute x14, starting transfers between devices, swap(): return lax.ppermute(x, axis, PAIR)  15.9 us
    all_to_all x1, waiting for transfers between devices, gather(): return lax.all_to_all(copies, axes, 0, 0, tiled=False)  13.5 us
    ppermute x1, waiting for transfers between devices, program(): piece = lax.ppermute(piece, NAMES, nu_pairs())  8.62 us
    ppermute x3, waiting for transfers between devices, ring(): far.append(lax.ppermute(near[step - 1], Z, OUTER))  7.59 us
  transfers between devices with their start and end apart: 23, of which 14 were waited for; matrix products, arithmetic and copies ran while one was open for 5% of the time, Pallas kernels for 0%

profile of v4, /device:TPU:8, one launch (start us, length us, event | category | flops | bytes accessed | tf_op | source)
XLA Modules:
  0.0 198.2 jit_solution(4374871116285563048)
XLA Ops:
  0.0 1.0 dynamic-slice_bitcast_fusion.1
  1.0 2.0 %collective-permute-start = (bf16[32,1024]{1,0:T(8,128)(2,1)S(1)}, bf16[32,1024]{1,0:T(8,128)(2,1)S(1)}, u32[]{:S(2)}, u32[]{:S(2)}) collective-permute-start(bf16[32,1024]{1,0:T(8,128)(2,1)S(1)} %get-tuple-element.25), channel_id=1, source_target_pairs={{0,2},{2,0},{1,3},{3,1},{4,6},{6,4},{5,7},{7,5},{8,10},{10,8},{9,1... | collective-permute-start | bytes 196616 | tf_op jit(solution)/shard_map/ppermute | solution.py:49
  3.0 2.3 %collective-permute-done = bf16[32,1024]{1,0:T(8,128)(2,1)S(1)} collective-permute-done((bf16[32,1024]{1,0:T(8,128)(2,1)S(1)}, bf16[32,1024]{1,0:T(8,128)(2,1)S(1)}, u32[]{:S(2)}, u32[]{:S(2)}) %collective-permute-start) | collective-permute-done | bytes 65568 | tf_op jit(solution)/shard_map/ppermute | solution.py:49
  5.3 5.2 %collective-permute-start.1 = (bf16[64,1024]{1,0:T(8,128)(2,1)S(1)}, bf16[64,1024]{1,0:T(8,128)(2,1)S(1)}, u32[]{:S(2)}, u32[]{:S(2)}) collective-permute-start(bf16[64,1024]{1,0:T(8,128)(2,1)S(1)} %pad_maximum_fusion.6), channel_id=1, source_target_pairs={{0,0},{1,1},{2,2},{3,3},{36,4},{37,5},{38,6},{39,7},{72,8},{73,9},... | collective-permute-start | bytes 393224 | tf_op jit(solution)/shard_map/ppermute | solution.py:144
  10.5 8.6 %collective-permute-done.1 = bf16[64,1024]{1,0:T(8,128)(2,1)S(1)} collective-permute-done((bf16[64,1024]{1,0:T(8,128)(2,1)S(1)}, bf16[64,1024]{1,0:T(8,128)(2,1)S(1)}, u32[]{:S(2)}, u32[]{:S(2)}) %collective-permute-start.1) | collective-permute-done | bytes 131104 | tf_op jit(solution)/shard_map/ppermute | solution.py:144
  19.1 0.9 pad_maximum_fusion.5
  20.0 5.0 %collective-permute-start.2 = (bf16[64,1536]{1,0:T(8,128)(2,1)S(1)}, bf16[64,1536]{1,0:T(8,128)(2,1)S(1)}, u32[]{:S(2)}, u32[]{:S(2)}) collective-permute-start(bf16[64,1536]{1,0:T(8,128)(2,1)S(1)} %pad_maximum_fusion.5), channel_id=1, source_target_pairs={{0,128},{128,0},{1,129},{129,1},{2,130},{130,2},{3,131},{131,3},{4... | collective-permute-start | bytes 589832 | tf_op jit(solution)/shard_map/ppermute | solution.py:49
  24.9 3.6 %collective-permute-done.2 = bf16[64,1536]{1,0:T(8,128)(2,1)S(1)} collective-permute-done((bf16[64,1536]{1,0:T(8,128)(2,1)S(1)}, bf16[64,1536]{1,0:T(8,128)(2,1)S(1)}, u32[]{:S(2)}, u32[]{:S(2)}) %collective-permute-start.2) | collective-permute-done | bytes 196640 | tf_op jit(solution)/shard_map/ppermute | solution.py:49
  28.6 0.9 select_bitcast_fusion.1
  29.6 0.0 copy-start
  29.6 0.1 broadcast_in_dim.6
  29.7 22.9 %all_to_all.20.nu_a_ref = bf16[4,2,64,1536]{3,2,1,0:T(8,128)(2,1)S(1)} all-to-all(bf16[4,2,64,1536]{3,2,1,0:T(8,128)(2,1)S(1)} %broadcast_in_dim.6), channel_id=1, replica_groups=mesh['xh'=2,'y'=4,'xl'=2,'zh'=4,'zl'=2,'core'=2] {'y'}, dimensions={0} | all-to-all | bytes 3145728 | tf_op jit(solution)/shard_map/all_to_all | solution.py:54
  52.6 0.0 collective-permute-start.3
  52.6 0.5 collective-permute-start.4
  53.1 1.2 constant_dynamic-slice_fusion.4
  54.2 0.0 collective-permute-start.17
  54.2 1.9 collective-permute-done.4
  56.1 3.0 %collective-permute-start.6 = (bf16[64,1024]{1,0:T(8,128)(2,1)S(1)}, bf16[64,1024]{1,0:T(8,128)(2,1)S(1)}, u32[]{:S(2)}, u32[]{:S(2)}) collective-permute-start(bf16[64,1024]{1,0:T(8,128)(2,1)S(1)} %pad_maximum_fusion.7.refs_0_), channel_id=1, source_target_pairs={{0,14},{2,4},{4,2},{6,8},{8,6},{10,12},{12,10},{14,0},{1,15},{3,5}... | collective-permute-start | bytes 393224 | tf_op jit(solution)/shard_map/ppermute | solution.py:62
  59.1 2.1 %collective-permute-start.5 = (bf16[64,1024]{1,0:T(8,128)(2,1)S(1)}, bf16[64,1024]{1,0:T(8,128)(2,1)S(1)}, u32[]{:S(2)}, u32[]{:S(2)}) collective-permute-start(bf16[64,1024]{1,0:T(8,128)(2,1)S(1)} %pad_maximum_fusion.7.refs_0_), channel_id=1, source_target_pairs={{0,2},{2,0},{4,6},{6,4},{8,10},{10,8},{12,14},{14,12},{1,3},{3,1},... | collective-permute-start | bytes 393224 | tf_op jit(solution)/shard_map/ppermute | solution.py:60
  61.2 1.8 collective-permute-done.6.refs_7_
  63.0 3.0 %collective-permute-start.7 = (bf16[64,1024]{1,0:T(8,128)(2,1)S(1)}, bf16[64,1024]{1,0:T(8,128)(2,1)S(1)}, u32[]{:S(2)}, u32[]{:S(2)}) collective-permute-start(bf16[64,1024]{1,0:T(8,128)(2,1)S(1)} %collective-permute-done.6.refs_7_), channel_id=1, source_target_pairs={{0,2},{2,0},{4,6},{6,4},{8,10},{10,8},{12,14},{14,12},{1,3},{3,1},... | collective-permute-start | bytes 393224 | tf_op jit(solution)/shard_map/ppermute | solution.py:60
  66.0 1.5 collective-permute-start.8
  67.5 2.9 %collective-permute-start.12 = (bf16[64,1024]{1,0:T(8,128)(2,1)S(1)}, bf16[64,1024]{1,0:T(8,128)(2,1)S(1)}, u32[]{:S(2)}, u32[]{:S(2)}) collective-permute-start(bf16[64,1024]{1,0:T(8,128)(2,1)S(1)} %pad_maximum_fusion.7.refs_0_), channel_id=1, source_target_pairs={{0,16},{16,0},{1,17},{17,1},{2,18},{18,2},{3,19},{19,3},{4,20},{20... | collective-permute-start | bytes 393224 | tf_op jit(solution)/shard_map/ppermute | solution.py:49
  70.5 0.3 collective-permute-start.10
  70.8 1.4 collective-permute-done.8.refs_6_
  72.2 0.0 collective-permute-start.9
  72.2 4.4 %collective-permute-done.10.refs_5_ = bf16[64,1024]{1,0:T(8,128)(2,1)S(1)} collective-permute-done((bf16[64,1024]{1,0:T(8,128)(2,1)S(1)}, bf16[64,1024]{1,0:T(8,128)(2,1)S(1)}, u32[]{:S(2)}, u32[]{:S(2)}) %collective-permute-start.10) | collective-permute-done | bytes 131104 | tf_op jit(solution)/shard_map/ppermute | solution.py:62
  76.6 0.0 collective-permute-start.13
  76.7 0.5 collective-permute-done.9.refs_3_
  77.2 1.7 collective-permute-start.14
  78.8 0.0 collective-permute-done.12.refs_8_
  78.9 0.4 collective-permute-start.15
  79.3 0.0 collective-permute-done.3.nu_b_ref
  79.3 0.3 collective-permute-start.11
  79.6 1.1 broadcast_select_fusion.1
  80.7 3.6 %collective-permute-done.11.refs_4_ = bf16[64,1024]{1,0:T(8,128)(2,1)S(1)} collective-permute-done((bf16[64,1024]{1,0:T(8,128)(2,1)S(1)}, bf16[64,1024]{1,0:T(8,128)(2,1)S(1)}, u32[]{:S(2)}, u32[]{:S(2)}) %collective-permute-start.11) | collective-permute-done | bytes 131104 | tf_op jit(solution)/shard_map/ppermute | solution.py:60
  84.3 1.7 collective-permute-start.16
  85.9 0.1 pad_maximum_fusion
  86.1 0.0 collective-permute-done.13.refs_9_
  86.1 5.4 %collective-permute-done.14.refs_10_ = bf16[128,1024]{1,0:T(8,128)(2,1)S(1)} collective-permute-done((bf16[128,1024]{1,0:T(8,128)(2,1)S(1)}, bf16[128,1024]{1,0:T(8,128)(2,1)S(1)}, u32[]{:S(2)}, u32[]{:S(2)}) %collective-permute-start.14) | collective-permute-done | bytes 262176 | tf_op jit(solution)/shard_map/ppermute | solution.py:49
  91.4 5.0 %collective-permute-done.16.refs_12_ = bf16[64,1024]{1,0:T(8,128)(2,1)S(1)} collective-permute-done((bf16[64,1024]{1,0:T(8,128)(2,1)S(1)}, bf16[64,1024]{1,0:T(8,128)(2,1)S(1)}, u32[]{:S(2)}, u32[]{:S(2)}) %collective-permute-start.16) | collective-permute-done | bytes 131104 | tf_op jit(solution)/shard_map/ppermute | solution.py:49
  96.5 0.0 collective-permute-done.15.refs_11_
  96.5 0.0 collective-permute-done.17.refs_14_
  96.5 4.8 %shard_map.46 = bf16[1024,1024]{1,0:T(8,128)(2,1)S(1)} custom-call(s32[1]{0:T(128)} %bitcast.core_ref, bf16[4,2,64,1536]{3,2,1,0:T(8,128)(2,1)S(1)} %all_to_all.20.nu_a_ref, bf16[4,2,64,1536]{3,2,1,0:T(8,128)(2,1)} %collective-permute-done.3.nu_b_ref, bf16[64,1024]{1,0:T(8,128)(2,1)S(1)} %pad_maximum_fusion.7.refs_0_, ...), custom_call_target="tpu_custom_call" | custom-call | flops 2147483648 | bytes 10485760 | tf_op jit(solution)/shard_map/pallas_call | solution.py:123
  101.3 1.3 fusion.2
  102.6 0.1 dynamic-slice_convert_fusion
  102.7 0.8 collective-permute-start.18
  103.5 9.8 %collective-permute-done.18 = bf16[512,512]{1,0:T(8,128)(2,1)S(1)} collective-permute-done((bf16[512,512]{1,0:T(8,128)(2,1)S(1)}, bf16[512,512]{1,0:T(8,128)(2,1)S(1)}, u32[]{:S(2)}, u32[]{:S(2)}) %collective-permute-start.18) | collective-permute-done | bytes 524320 | tf_op jit(solution)/shard_map/ppermute | solution.py:49
  113.4 0.2 add_convert_fusion
  113.5 20.6 %all_to_all.21 = bf16[8,64,512]{2,1,0:T(8,128)(2,1)S(1)} all-to-all(bf16[8,64,512]{2,1,0:T(8,128)(2,1)S(1)} %bitcast.33), channel_id=1, replica_groups=mesh['xh'=2,'y'=4,'xl'=2,'zh'=4,'zl'=2,'core'=2] {'zh','zl'}, dimensions={0} | all-to-all | bytes 1048576 | tf_op jit(solution)/shard_map/all_to_all | solution.py:173
  134.1 0.1 fusion.1
  134.2 0.9 broadcast_in_dim.16
  135.0 3.5 %all-to-all-start.2 = ((bf16[8,64,512]{2,1,0:T(8,128)(2,1)}), bf16[8,64,512]{2,1,0:T(8,128)(2,1)S(1)}, u32[]{:S(2)}, u32[]{:S(2)}) async-start(bf16[8,64,512]{2,1,0:T(8,128)(2,1)} %broadcast_in_dim.16), calls=%async_computation.2 | async-start | bytes 1048576 | tf_op jit(solution)/shard_map/all_to_all | solution.py:54
  138.5 13.5 %all-to-all-done.2 = bf16[8,64,512]{2,1,0:T(8,128)(2,1)S(1)} async-done(((bf16[8,64,512]{2,1,0:T(8,128)(2,1)}), bf16[8,64,512]{2,1,0:T(8,128)(2,1)S(1)}, u32[]{:S(2)}, u32[]{:S(2)}) %all-to-all-start.2) | async-done | bytes 524320 | tf_op jit(solution)/shard_map/all_to_all | solution.py:54
  152.0 0.9 collective-permute-start.20
  152.9 4.3 %constant_dynamic-slice_fusion = (bf16[512,2048]{1,0:T(8,128)(2,1)S(1)}, bf16[512,2048]{1,0:T(8,128)(2,1)S(1)}, bf16[512,2048]{1,0:T(8,128)(2,1)S(1)}, bf16[512,2048]{1,0:T(8,128)(2,1)S(1)}) fusion(bf16[2048,2048]{1,0:T(8,128)(2,1)} %param.7, s32[]{:T(128)S(6)} %select_n.71, s32[]{:T(128)S(6)} %select_n.69, s32[]{:T(128)S(6)} %select_n.68, s32[]{:T(128)S(6)} %select_n.70), kind=kLoop, calls=%fused_computation.23 | loop fusion | bytes 16777232 | tf_op jit(solution)/shard_map/dynamic_slice | solution.py:162
  157.2 0.1 collective-permute-start.19
  157.3 1.3 fusion.3
  158.6 2.6 %collective-permute-done.20 = bf16[512,512]{1,0:T(8,128)(2,1)S(1)} collective-permute-done((bf16[512,512]{1,0:T(8,128)(2,1)S(1)}, bf16[512,512]{1,0:T(8,128)(2,1)S(1)}, u32[]{:S(2)}, u32[]{:S(2)}) %collective-permute-start.20) | collective-permute-done | bytes 524320 | tf_op jit(solution)/shard_map/ppermute | solution.py:49
  161.2 1.3 fusion.5
  162.5 1.3 fusion.4
  163.9 1.9 negate_convert_fusion
  165.8 31.3 %all_to_all.22 = bf16[8,64,2048]{2,1,0:T(8,128)(2,1)S(1)} all-to-all(bf16[8,64,2048]{2,1,0:T(8,128)(2,1)S(1)} %bitcast.32), channel_id=1, replica_groups=mesh['xh'=2,'y'=4,'xl'=2,'zh'=4,'zl'=2,'core'=2] {'y','xh'}, dimensions={0} | all-to-all | bytes 4194304 | tf_op jit(solution)/shard_map/all_to_all | solution.py:183
  197.1 1.0 fusion
  (12 shorter events, 0.1 us)
Async XLA Ops:
  1.0 4.4 %collective-permute-start = (bf16[32,1024]{1,0:T(8,128)(2,1)S(1)}, bf16[32,1024]{1,0:T(8,128)(2,1)S(1)}, u32[]{:S(2)}, u32[]{:S(2)}) collective-permute-start(bf16[32,1024]{1,0:T(8,128)(2,1)S(1)} %get-tuple-element.25), channel_id=1, source_target_pairs={{0,2},{2,0},{1,3},{3,1},{4,6},{6,4},{5,7},{7,5},{8,10},{10,8},{9,1... | collective-permute-start | bytes 196616 | tf_op jit(solution)/shard_map/ppermute | solution.py:49
  5.3 13.8 %collective-permute-start.1 = (bf16[64,1024]{1,0:T(8,128)(2,1)S(1)}, bf16[64,1024]{1,0:T(8,128)(2,1)S(1)}, u32[]{:S(2)}, u32[]{:S(2)}) collective-permute-start(bf16[64,1024]{1,0:T(8,128)(2,1)S(1)} %pad_maximum_fusion.6), channel_id=1, source_target_pairs={{0,0},{1,1},{2,2},{3,3},{36,4},{37,5},{38,6},{39,7},{72,8},{73,9},... | collective-permute-start | bytes 393224 | tf_op jit(solution)/shard_map/ppermute | solution.py:144
  20.0 8.6 %collective-permute-start.2 = (bf16[64,1536]{1,0:T(8,128)(2,1)S(1)}, bf16[64,1536]{1,0:T(8,128)(2,1)S(1)}, u32[]{:S(2)}, u32[]{:S(2)}) collective-permute-start(bf16[64,1536]{1,0:T(8,128)(2,1)S(1)} %pad_maximum_fusion.5), channel_id=1, source_target_pairs={{0,128},{128,0},{1,129},{129,1},{2,130},{130,2},{3,131},{131,3},{4... | collective-permute-start | bytes 589832 | tf_op jit(solution)/shard_map/ppermute | solution.py:49
  29.6 23.5 %copy-start = (bf16[512,2048]{1,0:T(8,128)(2,1)S(1)}, bf16[512,2048]{1,0:T(8,128)(2,1)}, u32[]{:S(2)}) copy-start(bf16[512,2048]{1,0:T(8,128)(2,1)} %param.5) | copy-start | bytes 6291460
  52.6 26.7 %collective-permute-start.3 = (bf16[4,2,64,1536]{3,2,1,0:T(8,128)(2,1)S(1)}, bf16[4,2,64,1536]{3,2,1,0:T(8,128)(2,1)}, u32[]{:S(2)}, u32[]{:S(2)}) collective-permute-start(bf16[4,2,64,1536]{3,2,1,0:T(8,128)(2,1)S(1)} %all_to_all.20.nu_a_ref), channel_id=1, source_target_pairs={{0,1},{1,0},{2,3},{3,2},{4,5},{5,4},{6,7},{7,6},{8,9},{9,8},{10,11... | collective-permute-start | bytes 4718600 | tf_op jit(solution)/shard_map/ppermute | solution.py:49
  52.6 3.5 %collective-permute-start.4 = (bf16[32,1024]{1,0:T(8,128)(2,1)S(1)}, bf16[32,1024]{1,0:T(8,128)(2,1)S(1)}, u32[]{:S(2)}, u32[]{:S(2)}) collective-permute-start(bf16[32,1024]{1,0:T(8,128)(2,1)S(1)} %get-tuple-element.26), channel_id=1, source_target_pairs={{0,1},{1,0},{2,3},{3,2},{4,5},{5,4},{6,7},{7,6},{8,9},{9,8},{10,11... | collective-permute-start | bytes 196616 | tf_op jit(solution)/shard_map/ppermute | solution.py:49
  54.2 42.2 %collective-permute-start.17 = (bf16[512,1024]{1,0:T(8,128)(2,1)}, bf16[512,1024]{1,0:T(8,128)(2,1)}, u32[]{:S(2)}, u32[]{:S(2)}) collective-permute-start(bf16[512,1024]{1,0:T(8,128)(2,1)} %get-tuple-element.19), channel_id=1, source_target_pairs={{0,1},{1,0},{2,3},{3,2},{4,5},{5,4},{6,7},{7,6},{8,9},{9,8},{10,11... | collective-permute-start | bytes 3145736 | tf_op jit(solution)/shard_map/ppermute | solution.py:49
  56.1 6.8 %collective-permute-start.6 = (bf16[64,1024]{1,0:T(8,128)(2,1)S(1)}, bf16[64,1024]{1,0:T(8,128)(2,1)S(1)}, u32[]{:S(2)}, u32[]{:S(2)}) collective-permute-start(bf16[64,1024]{1,0:T(8,128)(2,1)S(1)} %pad_maximum_fusion.7.refs_0_), channel_id=1, source_target_pairs={{0,14},{2,4},{4,2},{6,8},{8,6},{10,12},{12,10},{14,0},{1,15},{3,5}... | collective-permute-start | bytes 393224 | tf_op jit(solution)/shard_map/ppermute | solution.py:62
  59.1 6.9 %collective-permute-start.5 = (bf16[64,1024]{1,0:T(8,128)(2,1)S(1)}, bf16[64,1024]{1,0:T(8,128)(2,1)S(1)}, u32[]{:S(2)}, u32[]{:S(2)}) collective-permute-start(bf16[64,1024]{1,0:T(8,128)(2,1)S(1)} %pad_maximum_fusion.7.refs_0_), channel_id=1, source_target_pairs={{0,2},{2,0},{4,6},{6,4},{8,10},{10,8},{12,14},{14,12},{1,3},{3,1},... | collective-permute-start | bytes 393224 | tf_op jit(solution)/shard_map/ppermute | solution.py:60
  63.0 7.5 %collective-permute-start.7 = (bf16[64,1024]{1,0:T(8,128)(2,1)S(1)}, bf16[64,1024]{1,0:T(8,128)(2,1)S(1)}, u32[]{:S(2)}, u32[]{:S(2)}) collective-permute-start(bf16[64,1024]{1,0:T(8,128)(2,1)S(1)} %collective-permute-done.6.refs_7_), channel_id=1, source_target_pairs={{0,2},{2,0},{4,6},{6,4},{8,10},{10,8},{12,14},{14,12},{1,3},{3,1},... | collective-permute-start | bytes 393224 | tf_op jit(solution)/shard_map/ppermute | solution.py:60
  66.0 6.2 %collective-permute-start.8 = (bf16[64,1024]{1,0:T(8,128)(2,1)S(1)}, bf16[64,1024]{1,0:T(8,128)(2,1)S(1)}, u32[]{:S(2)}, u32[]{:S(2)}) collective-permute-start(bf16[64,1024]{1,0:T(8,128)(2,1)S(1)} %collective-permute-done.5.refs_1_), channel_id=1, source_target_pairs={{0,14},{2,4},{4,2},{6,8},{8,6},{10,12},{12,10},{14,0},{1,15},{3,5}... | collective-permute-start | bytes 393224 | tf_op jit(solution)/shard_map/ppermute | solution.py:62
  67.5 11.3 %collective-permute-start.12 = (bf16[64,1024]{1,0:T(8,128)(2,1)S(1)}, bf16[64,1024]{1,0:T(8,128)(2,1)S(1)}, u32[]{:S(2)}, u32[]{:S(2)}) collective-permute-start(bf16[64,1024]{1,0:T(8,128)(2,1)S(1)} %pad_maximum_fusion.7.refs_0_), channel_id=1, source_target_pairs={{0,16},{16,0},{1,17},{17,1},{2,18},{18,2},{3,19},{19,3},{4,20},{20... | collective-permute-start | bytes 393224 | tf_op jit(solution)/shard_map/ppermute | solution.py:49
  70.5 6.2 %collective-permute-start.10 = (bf16[64,1024]{1,0:T(8,128)(2,1)S(1)}, bf16[64,1024]{1,0:T(8,128)(2,1)S(1)}, u32[]{:S(2)}, u32[]{:S(2)}) collective-permute-start(bf16[64,1024]{1,0:T(8,128)(2,1)S(1)} %collective-permute-done.7.refs_2_), channel_id=1, source_target_pairs={{0,14},{2,4},{4,2},{6,8},{8,6},{10,12},{12,10},{14,0},{1,15},{3,5}... | collective-permute-start | bytes 393224 | tf_op jit(solution)/shard_map/ppermute | solution.py:62
  72.2 5.0 %collective-permute-start.9 = (bf16[64,1024]{1,0:T(8,128)(2,1)S(1)}, bf16[64,1024]{1,0:T(8,128)(2,1)S(1)}, u32[]{:S(2)}, u32[]{:S(2)}) collective-permute-start(bf16[64,1024]{1,0:T(8,128)(2,1)S(1)} %collective-permute-done.8.refs_6_), channel_id=1, source_target_pairs={{0,2},{2,0},{4,6},{6,4},{8,10},{10,8},{12,14},{14,12},{1,3},{3,1},... | collective-permute-start | bytes 393224 | tf_op jit(solution)/shard_map/ppermute | solution.py:60
  76.6 9.4 %collective-permute-start.13 = (bf16[128,1024]{1,0:T(8,128)(2,1)S(1)}, bf16[128,1024]{1,0:T(8,128)(2,1)S(1)}, u32[]{:S(2)}, u32[]{:S(2)}) collective-permute-start(bf16[128,1024]{1,0:T(8,128)(2,1)S(1)} %pad_maximum_fusion.2), channel_id=1, source_target_pairs={{0,16},{16,0},{1,17},{17,1},{2,18},{18,2},{3,19},{19,3},{4,20},{20... | collective-permute-start | bytes 786440 | tf_op jit(solution)/shard_map/ppermute | solution.py:49
  77.2 14.3 %collective-permute-start.14 = (bf16[128,1024]{1,0:T(8,128)(2,1)S(1)}, bf16[128,1024]{1,0:T(8,128)(2,1)S(1)}, u32[]{:S(2)}, u32[]{:S(2)}) collective-permute-start(bf16[128,1024]{1,0:T(8,128)(2,1)S(1)} %pad_maximum_fusion.3), channel_id=1, source_target_pairs={{0,16},{16,0},{1,17},{17,1},{2,18},{18,2},{3,19},{19,3},{4,20},{20... | collective-permute-start | bytes 786440 | tf_op jit(solution)/shard_map/ppermute | solution.py:49
  78.9 17.6 %collective-permute-start.15 = (bf16[128,1024]{1,0:T(8,128)(2,1)S(1)}, bf16[128,1024]{1,0:T(8,128)(2,1)S(1)}, u32[]{:S(2)}, u32[]{:S(2)}) collective-permute-start(bf16[128,1024]{1,0:T(8,128)(2,1)S(1)} %pad_maximum_fusion.4), channel_id=1, source_target_pairs={{0,16},{16,0},{1,17},{17,1},{2,18},{18,2},{3,19},{19,3},{4,20},{20... | collective-permute-start | bytes 786440 | tf_op jit(solution)/shard_map/ppermute | solution.py:49
  79.3 5.0 %collective-permute-start.11 = (bf16[64,1024]{1,0:T(8,128)(2,1)S(1)}, bf16[64,1024]{1,0:T(8,128)(2,1)S(1)}, u32[]{:S(2)}, u32[]{:S(2)}) collective-permute-start(bf16[64,1024]{1,0:T(8,128)(2,1)S(1)} %collective-permute-done.10.refs_5_), channel_id=1, source_target_pairs={{0,2},{2,0},{4,6},{6,4},{8,10},{10,8},{12,14},{14,12},{1,3},{3,1},... | collective-permute-start | bytes 393224 | tf_op jit(solution)/shard_map/ppermute | solution.py:60
  84.3 12.2 %collective-permute-start.16 = (bf16[64,1024]{1,0:T(8,128)(2,1)S(1)}, bf16[64,1024]{1,0:T(8,128)(2,1)S(1)}, u32[]{:S(2)}, u32[]{:S(2)}) collective-permute-start(bf16[64,1024]{1,0:T(8,128)(2,1)S(1)} %collective-permute-done.11.refs_4_), channel_id=1, source_target_pairs={{0,16},{16,0},{1,17},{17,1},{2,18},{18,2},{3,19},{19,3},{4,20},{20... | collective-permute-start | bytes 393224 | tf_op jit(solution)/shard_map/ppermute | solution.py:49
  102.7 10.6 %collective-permute-start.18 = (bf16[512,512]{1,0:T(8,128)(2,1)S(1)}, bf16[512,512]{1,0:T(8,128)(2,1)S(1)}, u32[]{:S(2)}, u32[]{:S(2)}) collective-permute-start(bf16[512,512]{1,0:T(8,128)(2,1)S(1)} %dynamic-slice_convert_fusion), channel_id=1, source_target_pairs={{0,16},{16,0},{1,17},{17,1},{2,18},{18,2},{3,19},{19,3},{4,20},{20... | collective-permute-start | bytes 1572872 | tf_op jit(solution)/shard_map/ppermute | solution.py:49
  135.0 17.0 %all-to-all-start.2 = ((bf16[8,64,512]{2,1,0:T(8,128)(2,1)}), bf16[8,64,512]{2,1,0:T(8,128)(2,1)S(1)}, u32[]{:S(2)}, u32[]{:S(2)}) async-start(bf16[8,64,512]{2,1,0:T(8,128)(2,1)} %broadcast_in_dim.16), calls=%async_computation.2 | async-start | bytes 1048576 | tf_op jit(solution)/shard_map/all_to_all | solution.py:54
  152.0 9.2 %collective-permute-start.20 = (bf16[512,512]{1,0:T(8,128)(2,1)S(1)}, bf16[512,512]{1,0:T(8,128)(2,1)S(1)}, u32[]{:S(2)}, u32[]{:S(2)}) collective-permute-start(bf16[512,512]{1,0:T(8,128)(2,1)S(1)} %bitcast.34), channel_id=1, source_target_pairs={{0,16},{16,0},{1,17},{17,1},{2,18},{18,2},{3,19},{19,3},{4,20},{20... | collective-permute-start | bytes 1572872 | tf_op jit(solution)/shard_map/ppermute | solution.py:49
  157.2 5.3 %collective-permute-start.19 = (bf16[512,512]{1,0:T(8,128)(2,1)S(1)}, bf16[512,512]{1,0:T(8,128)(2,1)S(1)}, u32[]{:S(2)}, u32[]{:S(2)}) collective-permute-start(bf16[512,512]{1,0:T(8,128)(2,1)S(1)} %bitcast.35), channel_id=1, source_target_pairs={{0,1},{1,0},{2,3},{3,2},{4,5},{5,4},{6,7},{7,6},{8,9},{9,8},{10,11... | collective-permute-start | bytes 1572872 | tf_op jit(solution)/shard_map/ppermute | solution.py:49
  161.2 2.6 %collective-permute-start.21 = (bf16[512,512]{1,0:T(8,128)(2,1)S(1)}, bf16[512,512]{1,0:T(8,128)(2,1)S(1)}, u32[]{:S(2)}, u32[]{:S(2)}) collective-permute-start(bf16[512,512]{1,0:T(8,128)(2,1)S(1)} %collective-permute-done.20), channel_id=1, source_target_pairs={{0,1},{1,0},{2,3},{3,2},{4,5},{5,4},{6,7},{7,6},{8,9},{9,8},{10,11... | collective-permute-start | bytes 1572872 | tf_op jit(solution)/shard_map/ppermute | solution.py:49

commit v5 on v4

--- a/solution.py
+++ b/solution.py
@@ -27,7 +27,7 @@
     return index
 
 
-def nu_pairs():
+def nu_pairs(flip):
     pairs = []
     for xh in range(2):
         for y in range(4):
@@ -36,7 +36,7 @@
                     for zl in range(2):
                         for core in range(2):
                             away = STEPS[y] if zl == 0 else -STEPS[y]
-                            source = (xl, zh, xl ^ xh, (zh + away) % 4, zl, core)
+                            source = (xl, zh, xl ^ xh ^ flip, (zh + away) % 4, zl, core)
                             pairs.append((flat(source), flat((xh, y, xl, zh, zl, core))))
     return pairs
 
@@ -81,8 +81,8 @@
     return first, second
 
 
-def weigh(core, nu_a, nu_b, near, away, own, other):
-    def body(core_ref, nu_a_ref, nu_b_ref, *refs):
+def weigh(places, nu_a, nu_b, near, away, own, other):
+    def body(place_ref, nu_a_ref, nu_b_ref, *refs):
         near_refs, away_refs = refs[:8], refs[8:13]
         own_ref, other_ref, out_ref, mu_a, mu_b = refs[13:]
         across = {
@@ -95,15 +95,16 @@
             5: (away_refs[3], 64),
             4: (away_refs[4], 0),
         }
+        sides = (place_ref[1], 1 - place_ref[1])
         for y in range(4):
             for o in range(2):
                 n = ORDER[y * 2 + o]
                 for x, (ref, start) in enumerate(((near_refs[n], 0), across[n])):
-                    row = (y * 2 + x) * 64 + o * 32
-                    mu_a[row : row + 32, :] = ref[start : start + 32, :]
-                    mu_b[row : row + 32, :] = ref[start + 32 : start + 64, :]
-
-        mine = core_ref[0]
+                    row = pl.multiple_of((y * 2 + sides[x]) * 64 + o * 32, 32)
+                    mu_a[pl.ds(row, 32), :] = ref[start : start + 32, :]
+                    mu_b[pl.ds(row, 32), :] = ref[start + 32 : start + 64, :]
+
+        mine = place_ref[0]
 
         def tile(t, carry):
             start = pl.multiple_of(t * 256, 256)
@@ -130,7 +131,7 @@
         cost_estimate=pl.CostEstimate(
             flops=2 * 1024**3, bytes_accessed=10 << 20, transcendentals=0
         ),
-    )(core.reshape(1), nu_a, nu_b, *near, *away, own, other)
+    )(places, nu_a, nu_b, *near, *away, own, other)
 
 
 def program(orbitals, kernel, applied, fit):
@@ -141,13 +142,14 @@
     bands = orbitals.T
     cross = swap(half(bands, 1 - zl, 1), "zl")
     piece = jnp.concatenate([cross, half(bands, zl, 1)], axis=0)
-    piece = lax.ppermute(piece, NAMES, nu_pairs())
-    piece = jnp.concatenate([piece, applied.T], axis=1)
-    other = swap(piece, "xh")
-    both = gather(jnp.stack(ordered(lax.axis_index("xh"), piece, other)), "y", 4)
+    arrivals = []
+    for k in range(2):
+        arrivals.append(lax.ppermute(piece, NAMES, nu_pairs(k)))
+    both = gather(jnp.stack(arrivals), "y", 4)
     partner = swap(both, "core")
-    sides = ordered(core, both[:, :, :, 1024:], partner[:, :, :, 1024:])
-    blocks = jnp.concatenate(sides, axis=3).reshape(512, 1024)
+    own = gather(applied.T, ROW, 8)
+    other = swap(own, "core")
+    blocks = jnp.concatenate(ordered(core, own, other), axis=2).reshape(512, 1024)
     mu_own = half(bands, core, 1)
     mu_other = swap(half(bands, 1 - core, 1), "core")
     near = ring(jnp.concatenate([mu_own, mu_other], axis=0))
@@ -163,7 +165,8 @@
     ]
     fits = lax.optimization_barrier(fits)
 
-    weighted = weigh(core, both, partner, near, away, own, other)
+    places = jnp.stack([core, lax.axis_index("xh")])
+    weighted = weigh(places, both, partner, near, away, own, other)
 
     partial = lax.dot_general(
         weighted, blocks, (((0,), (1,)), ((), ())), preferred_element_type=F32
@@ -175,12 +178,13 @@
     p0 = gather(low, Z, 8).reshape(512, 512)
     p1 = swap(p0, "xl")
     p2 = swap(p0, "core")
-    p3 = swap(p1, "core")
     result = dot(p0, fits[0])
     result = result + dot(p2, fits[2])
+    p1, result = lax.optimization_barrier((p1, result))
+    p3 = swap(p1, "core")
     result = result + dot(p1, fits[1])
     result = result + dot(p3, fits[3])
-    terms = lax.all_to_all((-result).astype(BF).reshape(8, 64, 2048), ("y", "xh"), 0, 0, tiled=False)
+    terms = lax.all_to_all((-result).astype(BF).reshape(8, 64, 2048), ROW, 0, 0, tiled=False)
     return total(terms).astype(BF)
 
 

time: 201 us -> 215 us (1.070)
  waiting for transfers between devices: 64.5 us -> 71 us
  starting transfers between devices: 34.8 us -> 39.4 us
  local copies, waits for them, and re-layouts: 7.49 us -> 9.82 us
    ppermute x14, starting transfers between devices: 15.9 us -> 7.09 us  [swap(): return lax.ppermute(x, axis, PAIR)]
    all_to_all x1 -> x2, starting transfers between devices: 3.49 us -> 9.55 us  [gather(): return lax.all_to_all(copies, axes, 0, 0, tiled=False)]
    ppermute x14, waiting for transfers between devices: 30.7 us -> 36.6 us  [swap(): return lax.ppermute(x, axis, PAIR)]
    ppermute x3, starting transfers between devices: 4.8 us -> 10.2 us  [ring(): far.append(lax.ppermute(near[step - 1], Z, OUTER))]
    ppermute x1 -> x2, starting transfers between devices: 5.18 us -> 10.1 us  [program(): arrivals.append(lax.ppermute(piece, NAMES, nu_pairs(k)))]
    ppermute x4, starting transfers between devices: 5.44 us -> 2.46 us  [ring(): near.append(lax.ppermute(far[step - 1], Z, MATE))]
    concatenate x3, other arithmetic: 0.06 us -> 2.69 us  [program(): piece = near[a] if a == b else jnp.concatenate([near[a], near[b]], axis=0)]
    all_to_all x1, blocking collectives: 31.3 us -> 33.9 us  [program(): lax.all_to_all((-result).astype(BF).reshape(8, 64, 2048), ROW, 0, 0, tile...]
  transfers between devices with their start and end apart: 23 -> 25, of which waited for: 14 -> 16; matrix products, arithmetic and copies ran while one was open for 5% -> 7% of each run, Pallas kernels for 0% -> 0%
where the time goes in v5:
time: 215 us; the launch traced here: 214 us
  blocking collectives  76.9 us (36%)
  waiting for transfers between devices  71 us (33%)
  starting transfers between devices  39.4 us (18%)
  local copies, waits for them, and re-layouts  9.82 us (5%)
  matrix products  6.69 us (3%)
  other arithmetic  5.47 us (3%)
  Pallas kernels  4.69 us (2%)
    ppermute x14, waiting for transfers between devices, swap(): return lax.ppermute(x, axis, PAIR)  36.6 us
    all_to_all x1, blocking collectives, program(): lax.all_to_all((-result).astype(BF).reshape(8, 64, 2048), ROW, 0, 0, tile...  33.9 us
    all_to_all x1, blocking collectives, gather(): return lax.all_to_all(copies, axes, 0, 0, tiled=False)  24.9 us
    all_to_all x1, blocking collectives, program(): terms = lax.all_to_all(two.reshape(8, 64, 512), Z, 0, 0, tiled=False)  18.1 us
    all_to_all x2, waiting for transfers between devices, gather(): return lax.all_to_all(copies, axes, 0, 0, tiled=False)  13.2 us
    ppermute x3, starting transfers between devices, ring(): far.append(lax.ppermute(near[step - 1], Z, OUTER))  10.2 us
    ppermute x2, starting transfers between devices, program(): arrivals.append(lax.ppermute(piece, NAMES, nu_pairs(k)))  10.1 us
    all_to_all x2, starting transfers between devices, gather(): return lax.all_to_all(copies, axes, 0, 0, tiled=False)  9.55 us
  transfers between devices with their start and end apart: 25, of which 16 were waited for; matrix products, arithmetic and copies ran while one was open for 7% of the time, Pallas kernels for 0%

profile of v5, /device:TPU:8, one launch (start us, length us, event | category | flops | bytes accessed | tf_op | source)
XLA Modules:
  0.0 214.1 jit_solution(6122146149575911748)
XLA Ops:
  0.0 1.0 dynamic-slice_bitcast_fusion.1
  1.0 2.0 collective-permute-start
  3.0 2.3 %collective-permute-done = bf16[32,1024]{1,0:T(8,128)(2,1)S(1)} collective-permute-done((bf16[32,1024]{1,0:T(8,128)(2,1)S(1)}, bf16[32,1024]{1,0:T(8,128)(2,1)S(1)}, u32[]{:S(2)}, u32[]{:S(2)}) %collective-permute-start) | collective-permute-done | bytes 65568 | tf_op jit(solution)/shard_map/ppermute | solution.py:49
  5.3 7.8 %collective-permute-start.2 = (bf16[64,1024]{1,0:T(8,128)(2,1)S(1)}, bf16[64,1024]{1,0:T(8,128)(2,1)S(1)}, u32[]{:S(2)}, u32[]{:S(2)}) collective-permute-start(bf16[64,1024]{1,0:T(8,128)(2,1)S(1)} %pad_maximum_fusion.5), channel_id=1, source_target_pairs={{16,0},{17,1},{18,2},{19,3},{52,4},{53,5},{54,6},{55,7},{88,8},{89... | collective-permute-start | bytes 393224 | tf_op jit(solution)/shard_map/ppermute | solution.py:147
  13.1 2.4 %collective-permute-start.1 = (bf16[64,1024]{1,0:T(8,128)(2,1)S(1)}, bf16[64,1024]{1,0:T(8,128)(2,1)S(1)}, u32[]{:S(2)}, u32[]{:S(2)}) collective-permute-start(bf16[64,1024]{1,0:T(8,128)(2,1)S(1)} %pad_maximum_fusion.5), channel_id=1, source_target_pairs={{0,0},{1,1},{2,2},{3,3},{36,4},{37,5},{38,6},{39,7},{72,8},{73,9},... | collective-permute-start | bytes 393224 | tf_op jit(solution)/shard_map/ppermute | solution.py:147
  15.5 7.1 %collective-permute-done.2 = bf16[64,1024]{1,0:T(8,128)(2,1)S(1)} collective-permute-done((bf16[64,1024]{1,0:T(8,128)(2,1)S(1)}, bf16[64,1024]{1,0:T(8,128)(2,1)S(1)}, u32[]{:S(2)}, u32[]{:S(2)}) %collective-permute-start.2) | collective-permute-done | bytes 131104 | tf_op jit(solution)/shard_map/ppermute | solution.py:147
  22.6 1.8 collective-permute-done.1
  24.4 0.1 broadcast_in_dim.8
  24.6 24.9 %all_to_all.25.nu_a_ref = bf16[4,2,64,1024]{3,2,1,0:T(8,128)(2,1)S(1)} all-to-all(bf16[4,2,64,1024]{3,2,1,0:T(8,128)(2,1)S(1)} %broadcast_in_dim.8), channel_id=1, replica_groups=mesh['xh'=2,'y'=4,'xl'=2,'zh'=4,'zl'=2,'core'=2] {'y'}, dimensions={0} | all-to-all | bytes 2097152 | tf_op jit(solution)/shard_map/all_to_all | solution.py:54
  49.5 0.8 broadcast_in_dim.9
  50.3 6.1 %all-to-all-start.1 = ((bf16[8,64,512]{2,1,0:T(8,128)(2,1)}), bf16[8,64,512]{2,1,0:T(8,128)(2,1)}, u32[]{:S(2)}, u32[]{:S(2)}) async-start(bf16[8,64,512]{2,1,0:T(8,128)(2,1)} %broadcast_in_dim.9), calls=%async_computation.1 | async-start | bytes 1048576 | tf_op jit(solution)/shard_map/all_to_all | solution.py:54
  56.4 1.3 collective-permute-done.4
  57.7 1.8 collective-permute-start.5
  59.4 7.0 %collective-permute-start.6 = (bf16[64,1024]{1,0:T(8,128)(2,1)S(1)}, bf16[64,1024]{1,0:T(8,128)(2,1)S(1)}, u32[]{:S(2)}, u32[]{:S(2)}) collective-permute-start(bf16[64,1024]{1,0:T(8,128)(2,1)S(1)} %pad_maximum_fusion.6.refs_0_), channel_id=1, source_target_pairs={{0,14},{2,4},{4,2},{6,8},{8,6},{10,12},{12,10},{14,0},{1,15},{3,5}... | collective-permute-start | bytes 393224 | tf_op jit(solution)/shard_map/ppermute | solution.py:62
  66.4 2.7 %constant_dynamic-slice_fusion.4 = (bf16[512,1024]{1,0:T(8,128)(2,1)}, bf16[512,1024]{1,0:T(8,128)(2,1)S(1)}) fusion(bf16[512,2048]{1,0:T(8,128)(2,1)} %param.5, s32[]{:T(128)S(6)} %select_n.47, s32[]{:T(128)S(6)} %select_n.46), kind=kLoop, calls=%fused_computation.25 | loop fusion | bytes 4194312 | tf_op jit(solution)/shard_map/dynamic_slice | solution.py:68
  69.0 0.0 collective-permute-start.17
  69.0 0.5 collective-permute-start.3
  69.5 0.0 collective-permute-done.5.refs_1_
  69.6 1.5 collective-permute-start.8
  71.0 0.0 collective-permute-done.6.refs_7_
  71.0 0.0 collective-permute-start.7
  71.1 0.1 collective-permute-start.18
  71.2 5.1 %collective-permute-done.8.refs_6_ = bf16[64,1024]{1,0:T(8,128)(2,1)} collective-permute-done((bf16[64,1024]{1,0:T(8,128)(2,1)S(1)}, bf16[64,1024]{1,0:T(8,128)(2,1)}, u32[]{:S(2)}, u32[]{:S(2)}) %collective-permute-start.8) | collective-permute-done | bytes 131104 | tf_op jit(solution)/shard_map/ppermute | solution.py:62
  76.3 0.0 collective-permute-start.9
  76.3 1.7 collective-permute-start.10
  78.0 0.7 pad_maximum_fusion.2
  78.7 2.8 %collective-permute-done.9.refs_3_ = bf16[64,1024]{1,0:T(8,128)(2,1)} collective-permute-done((bf16[64,1024]{1,0:T(8,128)(2,1)}, bf16[64,1024]{1,0:T(8,128)(2,1)}, u32[]{:S(2)}, u32[]{:S(2)}) %collective-permute-start.9) | collective-permute-done | bytes 131104 | tf_op jit(solution)/shard_map/ppermute | solution.py:60
  81.6 0.1 pad_add_fusion.place_ref
  81.6 1.1 collective-permute-done.10.refs_5_
  82.8 0.9 collective-permute-start.12
  83.7 1.0 pad_maximum_fusion.3
  84.7 1.0 pad_maximum_fusion.4
  85.7 5.3 %collective-permute-done.12.refs_8_ = bf16[64,1024]{1,0:T(8,128)(2,1)S(1)} collective-permute-done((bf16[64,1024]{1,0:T(8,128)(2,1)S(1)}, bf16[64,1024]{1,0:T(8,128)(2,1)S(1)}, u32[]{:S(2)}, u32[]{:S(2)}) %collective-permute-start.12) | collective-permute-done | bytes 131104 | tf_op jit(solution)/shard_map/ppermute | solution.py:49
  90.9 0.1 collective-permute-start.14
  91.1 1.9 collective-permute-start.15
  93.0 0.7 collective-permute-start.11
  93.7 1.3 broadcast_select_fusion.1
  95.0 3.2 %collective-permute-done.11.refs_4_ = bf16[64,1024]{1,0:T(8,128)(2,1)S(1)} collective-permute-done((bf16[64,1024]{1,0:T(8,128)(2,1)}, bf16[64,1024]{1,0:T(8,128)(2,1)S(1)}, u32[]{:S(2)}, u32[]{:S(2)}) %collective-permute-start.11) | collective-permute-done | bytes 131104 | tf_op jit(solution)/shard_map/ppermute | solution.py:60
  98.2 0.1 collective-permute-start.16
  98.3 0.1 pad_maximum_fusion
  98.4 1.7 collective-permute-done.14.refs_10_
  100.1 3.3 %collective-permute-done.15.refs_11_ = bf16[128,1024]{1,0:T(8,128)(2,1)S(1)} collective-permute-done((bf16[128,1024]{1,0:T(8,128)(2,1)S(1)}, bf16[128,1024]{1,0:T(8,128)(2,1)S(1)}, u32[]{:S(2)}, u32[]{:S(2)}) %collective-permute-start.15) | collective-permute-done | bytes 262176 | tf_op jit(solution)/shard_map/ppermute | solution.py:49
  103.4 1.4 collective-permute-done.16.refs_12_
  104.8 4.7 %shard_map.46 = bf16[1024,1024]{1,0:T(8,128)(2,1)S(1)} custom-call(s32[2]{0:T(128)S(1)} %pad_add_fusion.place_ref, bf16[4,2,64,1024]{3,2,1,0:T(8,128)(2,1)S(1)} %all_to_all.25.nu_a_ref, bf16[4,2,64,1024]{3,2,1,0:T(8,128)(2,1)} %collective-permute-done.3.nu_b_ref, bf16[64,1024]{1,0:T(8,128)(2,1)S(1)} %pad_maximum_fusion.6.refs_0_, ...), custom_call_target="tpu_custom_call" | custom-call | flops 2147483648 | bytes 10485760 | tf_op jit(solution)/shard_map/pallas_call | solution.py:124
  109.5 1.3 fusion.2
  110.8 0.1 dynamic-slice_convert_fusion
  110.9 0.5 collective-permute-start.19
  111.4 9.8 %collective-permute-done.19 = bf16[512,512]{1,0:T(8,128)(2,1)S(1)} collective-permute-done((bf16[512,512]{1,0:T(8,128)(2,1)S(1)}, bf16[512,512]{1,0:T(8,128)(2,1)S(1)}, u32[]{:S(2)}, u32[]{:S(2)}) %collective-permute-start.19) | collective-permute-done | bytes 524320 | tf_op jit(solution)/shard_map/ppermute | solution.py:49
  121.2 0.2 add_convert_fusion
  121.4 18.1 %all_to_all.26 = bf16[8,64,512]{2,1,0:T(8,128)(2,1)S(1)} all-to-all(bf16[8,64,512]{2,1,0:T(8,128)(2,1)S(1)} %bitcast.32), channel_id=1, replica_groups=mesh['xh'=2,'y'=4,'xl'=2,'zh'=4,'zl'=2,'core'=2] {'zh','zl'}, dimensions={0} | all-to-all | bytes 1048576 | tf_op jit(solution)/shard_map/all_to_all | solution.py:176
  139.5 0.1 fusion.1
  139.5 0.9 broadcast_in_dim.11
  140.4 3.5 %all-to-all-start.3 = ((bf16[8,64,512]{2,1,0:T(8,128)(2,1)}), bf16[8,64,512]{2,1,0:T(8,128)(2,1)S(1)}, u32[]{:S(2)}, u32[]{:S(2)}) async-start(bf16[8,64,512]{2,1,0:T(8,128)(2,1)} %broadcast_in_dim.11), calls=%async_computation.3 | async-start | bytes 1048576 | tf_op jit(solution)/shard_map/all_to_all | solution.py:54
  143.9 13.2 %all-to-all-done.3 = bf16[8,64,512]{2,1,0:T(8,128)(2,1)S(1)} async-done(((bf16[8,64,512]{2,1,0:T(8,128)(2,1)}), bf16[8,64,512]{2,1,0:T(8,128)(2,1)S(1)}, u32[]{:S(2)}, u32[]{:S(2)}) %all-to-all-start.3) | async-done | bytes 524320 | tf_op jit(solution)/shard_map/all_to_all | solution.py:54
  157.1 4.3 %constant_dynamic-slice_fusion = (bf16[512,2048]{1,0:T(8,128)(2,1)S(1)}, bf16[512,2048]{1,0:T(8,128)(2,1)S(1)}, bf16[512,2048]{1,0:T(8,128)(2,1)S(1)}, bf16[512,2048]{1,0:T(8,128)(2,1)S(1)}) fusion(bf16[2048,2048]{1,0:T(8,128)(2,1)} %param.7, s32[]{:T(128)S(6)} %select_n.56, s32[]{:T(128)S(6)} %select_n.54, s32[]{:T(128)S(6)} %select_n.53, s32[]{:T(128)S(6)} %select_n.55), kind=kLoop, calls=%fused_computation.21 | loop fusion | bytes 16777232 | tf_op jit(solution)/shard_map/dynamic_slice | solution.py:164
  161.4 0.9 collective-permute-start.20
  162.3 1.3 fusion.3
  163.6 1.4 convolution_add_fusion
  165.0 10.8 %collective-permute-done.20 = bf16[512,512]{1,0:T(8,128)(2,1)S(1)} collective-permute-done((bf16[512,512]{1,0:T(8,128)(2,1)S(1)}, bf16[512,512]{1,0:T(8,128)(2,1)S(1)}, u32[]{:S(2)}, u32[]{:S(2)}) %collective-permute-start.20) | collective-permute-done | bytes 524320 | tf_op jit(solution)/shard_map/ppermute | solution.py:49
  175.8 1.3 fusion.4
  177.1 0.6 collective-permute-done.22
  177.7 1.5 negate_convert_fusion
  179.2 33.9 %all_to_all.27 = bf16[8,64,2048]{2,1,0:T(8,128)(2,1)S(1)} all-to-all(bf16[8,64,2048]{2,1,0:T(8,128)(2,1)S(1)} %bitcast.31), channel_id=1, replica_groups=mesh['xh'=2,'y'=4,'xl'=2,'zh'=4,'zl'=2,'core'=2] {'xh','y'}, dimensions={0} | all-to-all | bytes 4194304 | tf_op jit(solution)/shard_map/all_to_all | solution.py:187
  213.1 1.0 fusion
  (16 shorter events, 0.1 us)
Async XLA Ops:
  1.0 4.4 %collective-permute-start = (bf16[32,1024]{1,0:T(8,128)(2,1)S(1)}, bf16[32,1024]{1,0:T(8,128)(2,1)S(1)}, u32[]{:S(2)}, u32[]{:S(2)}) collective-permute-start(bf16[32,1024]{1,0:T(8,128)(2,1)S(1)} %get-tuple-element.27), channel_id=1, source_target_pairs={{0,2},{2,0},{1,3},{3,1},{4,6},{6,4},{5,7},{7,5},{8,10},{10,8},{9,1... | collective-permute-start | bytes 196616 | tf_op jit(solution)/shard_map/ppermute | solution.py:49
  5.3 44.2 %copy-start = (bf16[512,64]{0,1:T(8,128)(2,1)S(1)}, bf16[512,64]{0,1:T(8,128)(2,1)}, u32[]{:S(2)}) copy-start(bf16[512,64]{0,1:T(8,128)(2,1)} %param.6) | copy-start | bytes 196612
  5.3 17.3 %collective-permute-start.2 = (bf16[64,1024]{1,0:T(8,128)(2,1)S(1)}, bf16[64,1024]{1,0:T(8,128)(2,1)S(1)}, u32[]{:S(2)}, u32[]{:S(2)}) collective-permute-start(bf16[64,1024]{1,0:T(8,128)(2,1)S(1)} %pad_maximum_fusion.5), channel_id=1, source_target_pairs={{16,0},{17,1},{18,2},{19,3},{52,4},{53,5},{54,6},{55,7},{88,8},{89... | collective-permute-start | bytes 393224 | tf_op jit(solution)/shard_map/ppermute | solution.py:147
  13.1 11.3 %collective-permute-start.1 = (bf16[64,1024]{1,0:T(8,128)(2,1)S(1)}, bf16[64,1024]{1,0:T(8,128)(2,1)S(1)}, u32[]{:S(2)}, u32[]{:S(2)}) collective-permute-start(bf16[64,1024]{1,0:T(8,128)(2,1)S(1)} %pad_maximum_fusion.5), channel_id=1, source_target_pairs={{0,0},{1,1},{2,2},{3,3},{36,4},{37,5},{38,6},{39,7},{72,8},{73,9},... | collective-permute-start | bytes 393224 | tf_op jit(solution)/shard_map/ppermute | solution.py:147
  50.3 20.7 %all-to-all-start.1 = ((bf16[8,64,512]{2,1,0:T(8,128)(2,1)}), bf16[8,64,512]{2,1,0:T(8,128)(2,1)}, u32[]{:S(2)}, u32[]{:S(2)}) async-start(bf16[8,64,512]{2,1,0:T(8,128)(2,1)} %broadcast_in_dim.9), calls=%async_computation.1 | async-start | bytes 1048576 | tf_op jit(solution)/shard_map/all_to_all | solution.py:54
  56.4 1.3 collective-permute-start.4
  57.7 11.9 %collective-permute-start.5 = (bf16[64,1024]{1,0:T(8,128)(2,1)S(1)}, bf16[64,1024]{1,0:T(8,128)(2,1)S(1)}, u32[]{:S(2)}, u32[]{:S(2)}) collective-permute-start(bf16[64,1024]{1,0:T(8,128)(2,1)S(1)} %pad_maximum_fusion.6.refs_0_), channel_id=1, source_target_pairs={{0,2},{2,0},{4,6},{6,4},{8,10},{10,8},{12,14},{14,12},{1,3},{3,1},... | collective-permute-start | bytes 393224 | tf_op jit(solution)/shard_map/ppermute | solution.py:60
  59.4 11.6 %collective-permute-start.6 = (bf16[64,1024]{1,0:T(8,128)(2,1)S(1)}, bf16[64,1024]{1,0:T(8,128)(2,1)S(1)}, u32[]{:S(2)}, u32[]{:S(2)}) collective-permute-start(bf16[64,1024]{1,0:T(8,128)(2,1)S(1)} %pad_maximum_fusion.6.refs_0_), channel_id=1, source_target_pairs={{0,14},{2,4},{4,2},{6,8},{8,6},{10,12},{12,10},{14,0},{1,15},{3,5}... | collective-permute-start | bytes 393224 | tf_op jit(solution)/shard_map/ppermute | solution.py:62
  69.0 35.8 %collective-permute-start.17 = (bf16[512,1024]{1,0:T(8,128)(2,1)}, bf16[512,1024]{1,0:T(8,128)(2,1)S(1)}, u32[]{:S(2)}, u32[]{:S(2)}) collective-permute-start(bf16[512,1024]{1,0:T(8,128)(2,1)} %get-tuple-element.21), channel_id=1, source_target_pairs={{0,1},{1,0},{2,3},{3,2},{4,5},{5,4},{6,7},{7,6},{8,9},{9,8},{10,11... | collective-permute-start | bytes 3145736 | tf_op jit(solution)/shard_map/ppermute | solution.py:49
  69.0 35.8 %collective-permute-start.3 = (bf16[4,2,64,1024]{3,2,1,0:T(8,128)(2,1)S(1)}, bf16[4,2,64,1024]{3,2,1,0:T(8,128)(2,1)}, u32[]{:S(2)}, u32[]{:S(2)}) collective-permute-start(bf16[4,2,64,1024]{3,2,1,0:T(8,128)(2,1)S(1)} %all_to_all.25.nu_a_ref), channel_id=1, source_target_pairs={{0,1},{1,0},{2,3},{3,2},{4,5},{5,4},{6,7},{7,6},{8,9},{9,8},{10,11... | collective-permute-start | bytes 3145736 | tf_op jit(solution)/shard_map/ppermute | solution.py:49
  69.6 6.7 %collective-permute-start.8 = (bf16[64,1024]{1,0:T(8,128)(2,1)S(1)}, bf16[64,1024]{1,0:T(8,128)(2,1)}, u32[]{:S(2)}, u32[]{:S(2)}) collective-permute-start(bf16[64,1024]{1,0:T(8,128)(2,1)S(1)} %collective-permute-done.5.refs_1_), channel_id=1, source_target_pairs={{0,14},{2,4},{4,2},{6,8},{8,6},{10,12},{12,10},{14,0},{1,15},{3,5}... | collective-permute-start | bytes 393224 | tf_op jit(solution)/shard_map/ppermute | solution.py:62
  71.0 5.2 %collective-permute-start.7 = (bf16[64,1024]{1,0:T(8,128)(2,1)S(1)}, bf16[64,1024]{1,0:T(8,128)(2,1)}, u32[]{:S(2)}, u32[]{:S(2)}) collective-permute-start(bf16[64,1024]{1,0:T(8,128)(2,1)S(1)} %collective-permute-done.6.refs_7_), channel_id=1, source_target_pairs={{0,2},{2,0},{4,6},{6,4},{8,10},{10,8},{12,14},{14,12},{1,3},{3,1},... | collective-permute-start | bytes 393224 | tf_op jit(solution)/shard_map/ppermute | solution.py:60
  71.1 21.9 %collective-permute-start.18 = (bf16[8,64,512]{2,1,0:T(8,128)(2,1)}, bf16[8,64,512]{2,1,0:T(8,128)(2,1)}, u32[]{:S(2)}, u32[]{:S(2)}) collective-permute-start(bf16[8,64,512]{2,1,0:T(8,128)(2,1)} %all-to-all-done.1), channel_id=1, source_target_pairs={{0,1},{1,0},{2,3},{3,2},{4,5},{5,4},{6,7},{7,6},{8,9},{9,8},{10,11... | collective-permute-start | bytes 1572872 | tf_op jit(solution)/shard_map/ppermute | solution.py:49
  76.3 5.3 %collective-permute-start.9 = (bf16[64,1024]{1,0:T(8,128)(2,1)}, bf16[64,1024]{1,0:T(8,128)(2,1)}, u32[]{:S(2)}, u32[]{:S(2)}) collective-permute-start(bf16[64,1024]{1,0:T(8,128)(2,1)} %collective-permute-done.8.refs_6_), channel_id=1, source_target_pairs={{0,2},{2,0},{4,6},{6,4},{8,10},{10,8},{12,14},{14,12},{1,3},{3,1},... | collective-permute-start | bytes 393224 | tf_op jit(solution)/shard_map/ppermute | solution.py:60
  76.3 6.5 %collective-permute-start.10 = (bf16[64,1024]{1,0:T(8,128)(2,1)}, bf16[64,1024]{1,0:T(8,128)(2,1)}, u32[]{:S(2)}, u32[]{:S(2)}) collective-permute-start(bf16[64,1024]{1,0:T(8,128)(2,1)} %collective-permute-done.7.refs_2_), channel_id=1, source_target_pairs={{0,14},{2,4},{4,2},{6,8},{8,6},{10,12},{12,10},{14,0},{1,15},{3,5}... | collective-permute-start | bytes 393224 | tf_op jit(solution)/shard_map/ppermute | solution.py:62
  81.6 9.5 %collective-permute-start.13 = (bf16[128,1024]{1,0:T(8,128)(2,1)}, bf16[128,1024]{1,0:T(8,128)(2,1)}, u32[]{:S(2)}, u32[]{:S(2)}) collective-permute-start(bf16[128,1024]{1,0:T(8,128)(2,1)} %pad_maximum_fusion.2), channel_id=1, source_target_pairs={{0,16},{16,0},{1,17},{17,1},{2,18},{18,2},{3,19},{19,3},{4,20},{20... | collective-permute-start | bytes 786440 | tf_op jit(solution)/shard_map/ppermute | solution.py:49
  82.8 8.2 %collective-permute-start.12 = (bf16[64,1024]{1,0:T(8,128)(2,1)S(1)}, bf16[64,1024]{1,0:T(8,128)(2,1)S(1)}, u32[]{:S(2)}, u32[]{:S(2)}) collective-permute-start(bf16[64,1024]{1,0:T(8,128)(2,1)S(1)} %pad_maximum_fusion.6.refs_0_), channel_id=1, source_target_pairs={{0,16},{16,0},{1,17},{17,1},{2,18},{18,2},{3,19},{19,3},{4,20},{20... | collective-permute-start | bytes 393224 | tf_op jit(solution)/shard_map/ppermute | solution.py:49
  90.9 9.2 %collective-permute-start.14 = (bf16[128,1024]{1,0:T(8,128)(2,1)S(1)}, bf16[128,1024]{1,0:T(8,128)(2,1)S(1)}, u32[]{:S(2)}, u32[]{:S(2)}) collective-permute-start(bf16[128,1024]{1,0:T(8,128)(2,1)S(1)} %pad_maximum_fusion.3), channel_id=1, source_target_pairs={{0,16},{16,0},{1,17},{17,1},{2,18},{18,2},{3,19},{19,3},{4,20},{20... | collective-permute-start | bytes 786440 | tf_op jit(solution)/shard_map/ppermute | solution.py:49
  91.1 12.4 %collective-permute-start.15 = (bf16[128,1024]{1,0:T(8,128)(2,1)S(1)}, bf16[128,1024]{1,0:T(8,128)(2,1)S(1)}, u32[]{:S(2)}, u32[]{:S(2)}) collective-permute-start(bf16[128,1024]{1,0:T(8,128)(2,1)S(1)} %pad_maximum_fusion.4), channel_id=1, source_target_pairs={{0,16},{16,0},{1,17},{17,1},{2,18},{18,2},{3,19},{19,3},{4,20},{20... | collective-permute-start | bytes 786440 | tf_op jit(solution)/shard_map/ppermute | solution.py:49
  93.0 5.2 %collective-permute-start.11 = (bf16[64,1024]{1,0:T(8,128)(2,1)}, bf16[64,1024]{1,0:T(8,128)(2,1)S(1)}, u32[]{:S(2)}, u32[]{:S(2)}) collective-permute-start(bf16[64,1024]{1,0:T(8,128)(2,1)} %collective-permute-done.10.refs_5_), channel_id=1, source_target_pairs={{0,2},{2,0},{4,6},{6,4},{8,10},{10,8},{12,14},{14,12},{1,3},{3,1},... | collective-permute-start | bytes 393224 | tf_op jit(solution)/shard_map/ppermute | solution.py:60
  98.2 6.7 %collective-permute-start.16 = (bf16[64,1024]{1,0:T(8,128)(2,1)S(1)}, bf16[64,1024]{1,0:T(8,128)(2,1)S(1)}, u32[]{:S(2)}, u32[]{:S(2)}) collective-permute-start(bf16[64,1024]{1,0:T(8,128)(2,1)S(1)} %collective-permute-done.11.refs_4_), channel_id=1, source_target_pairs={{0,16},{16,0},{1,17},{17,1},{2,18},{18,2},{3,19},{19,3},{4,20},{20... | collective-permute-start | bytes 393224 | tf_op jit(solution)/shard_map/ppermute | solution.py:49
  110.9 10.3 %collective-permute-start.19 = (bf16[512,512]{1,0:T(8,128)(2,1)S(1)}, bf16[512,512]{1,0:T(8,128)(2,1)S(1)}, u32[]{:S(2)}, u32[]{:S(2)}) collective-permute-start(bf16[512,512]{1,0:T(8,128)(2,1)S(1)} %dynamic-slice_convert_fusion), channel_id=1, source_target_pairs={{0,16},{16,0},{1,17},{17,1},{2,18},{18,2},{3,19},{19,3},{4,20},{20... | collective-permute-start | bytes 1572872 | tf_op jit(solution)/shard_map/ppermute | solution.py:49
  140.4 16.7 %all-to-all-start.3 = ((bf16[8,64,512]{2,1,0:T(8,128)(2,1)}), bf16[8,64,512]{2,1,0:T(8,128)(2,1)S(1)}, u32[]{:S(2)}, u32[]{:S(2)}) async-start(bf16[8,64,512]{2,1,0:T(8,128)(2,1)} %broadcast_in_dim.11), calls=%async_computation.3 | async-start | bytes 1048576 | tf_op jit(solution)/shard_map/all_to_all | solution.py:54
  157.1 6.5 %collective-permute-start.21 = (bf16[512,512]{1,0:T(8,128)(2,1)S(1)}, bf16[512,512]{1,0:T(8,128)(2,1)S(1)}, u32[]{:S(2)}, u32[]{:S(2)}) collective-permute-start(bf16[512,512]{1,0:T(8,128)(2,1)S(1)} %bitcast.33), channel_id=1, source_target_pairs={{0,1},{1,0},{2,3},{3,2},{4,5},{5,4},{6,7},{7,6},{8,9},{9,8},{10,11... | collective-permute-start | bytes 1572872 | tf_op jit(solution)/shard_map/ppermute | solution.py:49
  161.4 14.4 %collective-permute-start.20 = (bf16[512,512]{1,0:T(8,128)(2,1)S(1)}, bf16[512,512]{1,0:T(8,128)(2,1)S(1)}, u32[]{:S(2)}, u32[]{:S(2)}) collective-permute-start(bf16[512,512]{1,0:T(8,128)(2,1)S(1)} %bitcast.34), channel_id=1, source_target_pairs={{0,16},{16,0},{1,17},{17,1},{2,18},{18,2},{3,19},{19,3},{4,20},{20... | collective-permute-start | bytes 1572872 | tf_op jit(solution)/shard_map/ppermute | solution.py:49
  175.8 1.9 collective-permute-start.22

commit v6 on v5

--- a/solution.py
+++ b/solution.py
@@ -15,8 +15,6 @@
 NAMES = tuple(name for name, _ in SIZES)
 PAIR = ((0, 1), (1, 0))
 MATE = tuple((z, z ^ 1) for z in range(8))
-STEPS = (0, 3, 1, 2)
-ORDER = (1, 0, 7, 6, 3, 2, 5, 4)
 OUTER = tuple((z, (z - 1) % 8 if z % 2 == 0 else (z + 1) % 8) for z in range(8))
 
 
@@ -27,7 +25,7 @@
     return index
 
 
-def nu_pairs(flip):
+def far_pairs():
     pairs = []
     for xh in range(2):
         for y in range(4):
@@ -35,9 +33,9 @@
                 for zh in range(4):
                     for zl in range(2):
                         for core in range(2):
-                            away = STEPS[y] if zl == 0 else -STEPS[y]
-                            source = (xl, zh, xl ^ xh ^ flip, (zh + away) % 4, zl, core)
-                            pairs.append((flat(source), flat((xh, y, xl, zh, zl, core))))
+                            source = flat((xh, y, xl, zh, zl, core))
+                            place = (2 * y + 2 - zh) % 4
+                            pairs.append((source, flat((xl, place, xh, y, zl, core))))
     return pairs
 
 
@@ -75,10 +73,25 @@
     return parts[0]
 
 
-def ordered(index, own, other):
-    first = jnp.where(index == 0, own, other)
-    second = jnp.where(index == 0, other, own)
-    return first, second
+def fan(ours, pair, over, both, applied):
+    def body(ours_ref, pair_ref, over_ref, both_ref, applied_ref, out_ref):
+        for k in range(4):
+            out_ref[k, 0, 0, :, :1024] = ours_ref[...]
+            out_ref[k, 0, 0, :, 1024:] = applied_ref[:32, :]
+            out_ref[k, 0, 1, :, :1024] = pair_ref[...]
+            out_ref[k, 0, 1, :, 1024:] = applied_ref[32:, :]
+            out_ref[k, 1, 0] = over_ref[:, :1536]
+            out_ref[k, 1, 1, :, :1024] = both_ref[...]
+            out_ref[k, 1, 1, :, 1024:] = over_ref[:, 1536:]
+
+    vmem = pl.BlockSpec(memory_space=pltpu.VMEM)
+    return pl.pallas_call(
+        body,
+        out_shape=jax.ShapeDtypeStruct((4, 2, 2, 32, 1536), BF),
+        in_specs=[vmem] * 5,
+        out_specs=vmem,
+        cost_estimate=pl.CostEstimate(flops=0, bytes_accessed=2 << 20, transcendentals=0),
+    )(ours, pair, over, both, applied)
 
 
 def weigh(places, nu_a, nu_b, near, away, own, other):
@@ -95,21 +108,20 @@
             5: (away_refs[3], 64),
             4: (away_refs[4], 0),
         }
-        sides = (place_ref[1], 1 - place_ref[1])
-        for y in range(4):
-            for o in range(2):
-                n = ORDER[y * 2 + o]
-                for x, (ref, start) in enumerate(((near_refs[n], 0), across[n])):
-                    row = pl.multiple_of((y * 2 + sides[x]) * 64 + o * 32, 32)
-                    mu_a[pl.ds(row, 32), :] = ref[start : start + 32, :]
-                    mu_b[pl.ds(row, 32), :] = ref[start + 32 : start + 64, :]
+        for n in range(8):
+            y = jnp.bitwise_and(place_ref[2] - place_ref[3] * (n // 2), 3)
+            for x, (ref, start) in enumerate(((near_refs[n], 0), across[n])):
+                side = place_ref[1] if x == 0 else 1 - place_ref[1]
+                row = pl.multiple_of(((y * 2 + side) * 2 + n % 2) * 32, 32)
+                mu_a[pl.ds(row, 32), :] = ref[start : start + 32, :]
+                mu_b[pl.ds(row, 32), :] = ref[start + 32 : start + 64, :]
 
         mine = place_ref[0]
 
         def tile(t, carry):
             start = pl.multiple_of(t * 256, 256)
-            part_a = nu_a_ref[:, :, :, pl.ds(start, 256)].reshape(512, 256)
-            part_b = nu_b_ref[:, :, :, pl.ds(start, 256)].reshape(512, 256)
+            part_a = nu_a_ref[:, :, :, :, pl.ds(start, 256)].reshape(512, 256)
+            part_b = nu_b_ref[:, :, :, :, pl.ds(start, 256)].reshape(512, 256)
             density = dot(part_a, mu_a[...]) + dot(part_b, mu_b[...])
             row = pl.multiple_of((t % 2) * 256, 256)
             ours = own_ref[pl.ds(row, 256), :]
@@ -138,18 +150,27 @@
     core = lax.axis_index("core")
     xl = lax.axis_index("xl")
     zl = lax.axis_index("zl")
+    xh = lax.axis_index("xh")
+    zh = lax.axis_index("zh")
 
     bands = orbitals.T
-    cross = swap(half(bands, 1 - zl, 1), "zl")
-    piece = jnp.concatenate([cross, half(bands, zl, 1)], axis=0)
-    arrivals = []
-    for k in range(2):
-        arrivals.append(lax.ppermute(piece, NAMES, nu_pairs(k)))
-    both = gather(jnp.stack(arrivals), "y", 4)
-    partner = swap(both, "core")
-    own = gather(applied.T, ROW, 8)
-    other = swap(own, "core")
-    blocks = jnp.concatenate(ordered(core, own, other), axis=2).reshape(512, 1024)
+    rows = lax.ppermute(bands, NAMES, far_pairs())
+    ours, theirs = half(rows, zl, 1), half(rows, 1 - zl, 1)
+    left, right = applied.T[:32], applied.T[32:]
+    pair = swap(theirs, "zl")
+    over = swap(jnp.concatenate([ours, left, right], axis=1), "xh")
+    both = lax.ppermute(theirs, ("xh", "zl"), ((0, 3), (1, 2), (2, 1), (3, 0)))
+    copies = fan(ours, pair, over, both, applied.T)
+    nu = lax.all_to_all(copies, "y", 0, 0, tiled=False)
+    nu_partner = swap(nu, "core")
+
+    def pick(c, k):
+        sides = [v[:, :, :, :, 1024:].reshape(4, 2, 64, 512) for v in (nu, nu_partner)]
+        mine, other = [jnp.where(xh == 0, v[:, k], v[:, 1 - k]) for v in sides]
+        return jnp.where(core == c, mine, other)
+
+    blocks = [jnp.concatenate([pick(0, k), pick(1, k)], axis=2) for k in range(2)]
+    blocks = jnp.stack(blocks, axis=1).reshape(512, 1024)
     mu_own = half(bands, core, 1)
     mu_other = swap(half(bands, 1 - core, 1), "core")
     near = ring(jnp.concatenate([mu_own, mu_other], axis=0))
@@ -165,8 +186,8 @@
     ]
     fits = lax.optimization_barrier(fits)
 
-    places = jnp.stack([core, lax.axis_index("xh")])
-    weighted = weigh(places, both, partner, near, away, own, other)
+    places = jnp.stack([core, jnp.bitwise_xor(xl, xh), zh + 2, 1 - 2 * zl])
+    weighted = weigh(places, nu, nu_partner, near, away, own, other)
 
     partial = lax.dot_general(
         weighted, blocks, (((0,), (1,)), ((), ())), preferred_element_type=F32
@@ -178,13 +199,12 @@
     p0 = gather(low, Z, 8).reshape(512, 512)
     p1 = swap(p0, "xl")
     p2 = swap(p0, "core")
+    p3 = swap(p1, "core")
     result = dot(p0, fits[0])
     result = result + dot(p2, fits[2])
-    p1, result = lax.optimization_barrier((p1, result))
-    p3 = swap(p1, "core")
     result = result + dot(p1, fits[1])
     result = result + dot(p3, fits[3])
-    terms = lax.all_to_all((-result).astype(BF).reshape(8, 64, 2048), ROW, 0, 0, tiled=False)
+    terms = lax.all_to_all((-result).astype(BF).reshape(8, 64, 2048), ("y", "xh"), 0, 0, tiled=False)
     return total(terms).astype(BF)
 
 

time: 215 us -> 200 us (0.930)
  starting transfers between devices: 39.4 us -> 29.1 us
  waiting for transfers between devices: 71 us -> 62.6 us
  other arithmetic: 5.47 us -> 1.74 us
  Pallas kernels: 4.69 us -> 7.15 us
    ppermute x14, waiting for transfers between devices: 36.6 us -> 23 us  [swap(): return lax.ppermute(x, axis, PAIR)]
    ppermute x2, starting transfers between devices: 10.1 us -> 3.16 us  [the longest x1 3.16 us: program(): rows = lax.ppermute(bands, NAMES, far_pairs())]
    ppermute x14, starting transfers between devices: 7.09 us -> 14 us  [swap(): return lax.ppermute(x, axis, PAIR)]
    all_to_all x2 -> x1, starting transfers between devices: 9.55 us -> 3.49 us  [gather(): return lax.all_to_all(copies, axes, 0, 0, tiled=False)]
    ppermute x2, waiting for transfers between devices: 8.95 us -> 14 us  [the longest x1 8.93 us: program(): rows = lax.ppermute(bands, NAMES, far_pairs())]
    all_to_all x1, blocking collectives: 18.1 us -> 22.4 us  [program(): terms = lax.all_to_all(two.reshape(8, 64, 512), Z, 0, 0, tiled=False)]
    ppermute x3, starting transfers between devices: 10.2 us -> 7.4 us  [ring(): far.append(lax.ppermute(near[step - 1], Z, OUTER))]
    concatenate x3, other arithmetic: 2.69 us -> 0.06 us  [program(): piece = near[a] if a == b else jnp.concatenate([near[a], near[b]], axis=0)]
  transfers between devices with their start and end apart: 25 -> 24, of which waited for: 16 -> 15; matrix products, arithmetic and copies ran while one was open for 7% -> 7% of each run, Pallas kernels for 0% -> 0%
where the time goes in v6:
time: 200 us; the launch traced here: 198 us
  blocking collectives  79 us (40%)
  waiting for transfers between devices  62.6 us (31%)
  starting transfers between devices  29.1 us (15%)
  local copies, waits for them, and re-layouts  11.2 us (6%)
  Pallas kernels  7.15 us (4%)
  matrix products  7.09 us (4%)
    all_to_all x1, blocking collectives, program(): lax.all_to_all((-result).astype(BF).reshape(8, 64, 2048), ('y', 'xh'), 0,...  31.4 us
    all_to_all x1, blocking collectives, program(): nu = lax.all_to_all(copies, 'y', 0, 0, tiled=False)  25.3 us
    ppermute x14, waiting for transfers between devices, swap(): return lax.ppermute(x, axis, PAIR)  23 us
    all_to_all x1, blocking collectives, program(): terms = lax.all_to_all(two.reshape(8, 64, 512), Z, 0, 0, tiled=False)  22.4 us
    ppermute x14, starting transfers between devices, swap(): return lax.ppermute(x, axis, PAIR)  14 us
    all_to_all x1, waiting for transfers between devices, gather(): return lax.all_to_all(copies, axes, 0, 0, tiled=False)  13.4 us
    ppermute x1, waiting for transfers between devices, program(): rows = lax.ppermute(bands, NAMES, far_pairs())  8.93 us
    ppermute x3, starting transfers between devices, ring(): far.append(lax.ppermute(near[step - 1], Z, OUTER))  7.4 us
  transfers between devices with their start and end apart: 24, of which 15 were waited for; matrix products, arithmetic and copies ran while one was open for 7% of the time, Pallas kernels for 0%

profile of v6, /device:TPU:8, one launch (start us, length us, event | category | flops | bytes accessed | tf_op | source)
XLA Modules:
  0.0 198.1 jit_solution(11481952105960666280)
XLA Ops:
  0.0 3.2 %collective-permute-start = (bf16[32,2048]{1,0:T(8,128)(2,1)}, bf16[32,2048]{1,0:T(8,128)(2,1)S(1)}, u32[]{:S(2)}, u32[]{:S(2)}) collective-permute-start(bf16[32,2048]{1,0:T(8,128)(2,1)} %bitcast.110), channel_id=1, source_target_pairs={{0,64},{1,65},{2,66},{3,67},{4,32},{5,33},{6,34},{7,35},{8,0},{9,1... | collective-permute-start | bytes 393224 | tf_op jit(solution)/shard_map/ppermute | solution.py:157
  3.2 0.8 fusion.2
  3.9 8.9 %collective-permute-done = bf16[32,2048]{1,0:T(8,128)(2,1)S(1)} collective-permute-done((bf16[32,2048]{1,0:T(8,128)(2,1)}, bf16[32,2048]{1,0:T(8,128)(2,1)S(1)}, u32[]{:S(2)}, u32[]{:S(2)}) %collective-permute-start) | collective-permute-done | bytes 131104 | tf_op jit(solution)/shard_map/ppermute | solution.py:157
  12.9 5.3 %collective-permute-start.2 = (bf16[32,2048]{1,0:T(8,128)(2,1)S(1)}, bf16[32,2048]{1,0:T(8,128)(2,1)S(1)}, u32[]{:S(2)}, u32[]{:S(2)}) collective-permute-start(bf16[32,2048]{1,0:T(8,128)(2,1)S(1)} %pad_maximum_fusion.4), channel_id=1, source_target_pairs={{0,128},{128,0},{1,129},{129,1},{2,130},{130,2},{3,131},{131,3},{4... | collective-permute-start | bytes 393224 | tf_op jit(solution)/shard_map/ppermute | solution.py:47
  18.2 1.6 collective-permute-start.1
  19.7 5.1 %collective-permute-done.3.both_ref = bf16[32,1024]{1,0:T(8,128)(2,1)S(1)} collective-permute-done((bf16[32,1024]{1,0:T(8,128)(2,1)S(1)}, bf16[32,1024]{1,0:T(8,128)(2,1)S(1)}, u32[]{:S(2)}, u32[]{:S(2)}) %collective-permute-start.3) | collective-permute-done | bytes 65568 | tf_op jit(solution)/shard_map/ppermute | solution.py:162
  24.9 0.6 copy-done.3
  25.5 0.0 copy-done.4
  25.5 0.7 copy-done.2
  26.2 2.3 %shard_map.46 = bf16[4,2,2,32,1536]{4,3,2,1,0:T(8,128)(2,1)} custom-call(bf16[32,1024]{1,0:T(8,128)(2,1)} %copy-done, bf16[32,1024]{1,0:T(8,128)(2,1)} %copy-done.4, bf16[32,2048]{1,0:T(8,128)(2,1)} %copy-done.2, bf16[32,1024]{1,0:T(8,128)(2,1)} %copy-done.3, bf16[64,512]{1,0:T(8,128)(2,1)} %bitcast.109), custom_call_target="tpu_custom_call" | custom-call | bytes 2097152 | tf_op jit(solution)/shard_map/pallas_call | solution.py:88
  28.4 25.3 %all_to_all.20.nu_a_ref = bf16[4,2,2,32,1536]{4,3,2,1,0:T(8,128)(2,1)S(1)} all-to-all(bf16[4,2,2,32,1536]{4,3,2,1,0:T(8,128)(2,1)} %shard_map.46), channel_id=1, replica_groups=mesh['xh'=2,'y'=4,'xl'=2,'zh'=4,'zl'=2,'core'=2] {'y'}, dimensions={0} | all-to-all | bytes 3145728 | tf_op jit(solution)/shard_map/all_to_all | solution.py:164
  53.7 0.0 collective-permute-start.4
  53.7 0.6 collective-permute-start.5
  54.3 2.9 %collective-permute-done.5 = bf16[32,1024]{1,0:T(8,128)(2,1)S(1)} collective-permute-done((bf16[32,1024]{1,0:T(8,128)(2,1)S(1)}, bf16[32,1024]{1,0:T(8,128)(2,1)S(1)}, u32[]{:S(2)}, u32[]{:S(2)}) %collective-permute-start.5) | collective-permute-done | bytes 65568 | tf_op jit(solution)/shard_map/ppermute | solution.py:47
  57.3 2.5 %collective-permute-start.7 = (bf16[64,1024]{1,0:T(8,128)(2,1)S(1)}, bf16[64,1024]{1,0:T(8,128)(2,1)S(1)}, u32[]{:S(2)}, u32[]{:S(2)}) collective-permute-start(bf16[64,1024]{1,0:T(8,128)(2,1)S(1)} %pad_maximum_fusion.5.refs_0_), channel_id=1, source_target_pairs={{0,14},{2,4},{4,2},{6,8},{8,6},{10,12},{12,10},{14,0},{1,15},{3,5}... | collective-permute-start | bytes 393224 | tf_op jit(solution)/shard_map/ppermute | solution.py:60
  59.8 0.1 collective-permute-start.6
  59.9 2.7 %constant_dynamic-slice_fusion.4 = (bf16[512,1024]{1,0:T(8,128)(2,1)}, bf16[512,1024]{1,0:T(8,128)(2,1)S(1)}) fusion(bf16[512,2048]{1,0:T(8,128)(2,1)} %param.5, s32[]{:T(128)S(6)} %select_n.99, s32[]{:T(128)S(6)} %select_n.98), kind=kLoop, calls=%fused_computation.33 | loop fusion | bytes 4194312 | tf_op jit(solution)/shard_map/dynamic_slice | solution.py:66
  62.6 1.5 collective-permute-done.7.refs_7_
  64.1 0.8 collective-permute-start.8
  64.9 0.1 collective-permute-done.6.refs_1_
  65.1 2.4 %collective-permute-start.9 = (bf16[64,1024]{1,0:T(8,128)(2,1)S(1)}, bf16[64,1024]{1,0:T(8,128)(2,1)S(1)}, u32[]{:S(2)}, u32[]{:S(2)}) collective-permute-start(bf16[64,1024]{1,0:T(8,128)(2,1)S(1)} %collective-permute-done.6.refs_1_), channel_id=1, source_target_pairs={{0,14},{2,4},{4,2},{6,8},{8,6},{10,12},{12,10},{14,0},{1,15},{3,5}... | collective-permute-start | bytes 393224 | tf_op jit(solution)/shard_map/ppermute | solution.py:60
  67.5 0.1 pad_add_fusion.place_ref
  67.5 0.2 collective-permute-start.13
  67.8 1.3 collective-permute-done.8.refs_2_
  69.1 2.5 %collective-permute-start.11 = (bf16[64,1024]{1,0:T(8,128)(2,1)S(1)}, bf16[64,1024]{1,0:T(8,128)(2,1)S(1)}, u32[]{:S(2)}, u32[]{:S(2)}) collective-permute-start(bf16[64,1024]{1,0:T(8,128)(2,1)S(1)} %collective-permute-done.8.refs_2_), channel_id=1, source_target_pairs={{0,14},{2,4},{4,2},{6,8},{8,6},{10,12},{12,10},{14,0},{1,15},{3,5}... | collective-permute-start | bytes 393224 | tf_op jit(solution)/shard_map/ppermute | solution.py:60
  71.5 0.2 collective-permute-done.9.refs_6_
  71.7 0.0 collective-permute-start.10
  71.8 3.5 %collective-permute-done.11.refs_5_ = bf16[64,1024]{1,0:T(8,128)(2,1)S(1)} collective-permute-done((bf16[64,1024]{1,0:T(8,128)(2,1)S(1)}, bf16[64,1024]{1,0:T(8,128)(2,1)S(1)}, u32[]{:S(2)}, u32[]{:S(2)}) %collective-permute-start.11) | collective-permute-done | bytes 131104 | tf_op jit(solution)/shard_map/ppermute | solution.py:60
  75.2 0.8 collective-permute-start.14
  76.0 0.7 collective-permute-done.10.refs_3_
  76.7 0.9 collective-permute-start.15
  77.7 0.0 collective-permute-done.4.nu_b_ref
  77.7 1.2 collective-permute-start.16
  78.9 1.1 slice.119
  80.0 0.1 select_bitcast_fusion.3
  80.1 0.1 collective-permute-start.12
  80.2 0.1 maximum_bitcast_fusion
  80.3 4.8 %collective-permute-done.12.refs_4_ = bf16[64,1024]{1,0:T(8,128)(2,1)S(1)} collective-permute-done((bf16[64,1024]{1,0:T(8,128)(2,1)S(1)}, bf16[64,1024]{1,0:T(8,128)(2,1)S(1)}, u32[]{:S(2)}, u32[]{:S(2)}) %collective-permute-start.12) | collective-permute-done | bytes 131104 | tf_op jit(solution)/shard_map/ppermute | solution.py:58
  85.1 0.9 collective-permute-start.17
  86.1 0.1 pad_maximum_fusion
  86.2 3.9 %collective-permute-done.15.refs_10_ = bf16[128,1024]{1,0:T(8,128)(2,1)S(1)} collective-permute-done((bf16[128,1024]{1,0:T(8,128)(2,1)S(1)}, bf16[128,1024]{1,0:T(8,128)(2,1)S(1)}, u32[]{:S(2)}, u32[]{:S(2)}) %collective-permute-start.15) | collective-permute-done | bytes 262176 | tf_op jit(solution)/shard_map/ppermute | solution.py:47
  90.0 4.8 %collective-permute-done.17.refs_12_ = bf16[64,1024]{1,0:T(8,128)(2,1)S(1)} collective-permute-done((bf16[64,1024]{1,0:T(8,128)(2,1)S(1)}, bf16[64,1024]{1,0:T(8,128)(2,1)S(1)}, u32[]{:S(2)}, u32[]{:S(2)}) %collective-permute-start.17) | collective-permute-done | bytes 131104 | tf_op jit(solution)/shard_map/ppermute | solution.py:47
  94.9 4.9 %shard_map.47 = bf16[1024,1024]{1,0:T(8,128)(2,1)S(1)} custom-call(s32[4]{0:T(128)S(1)} %pad_add_fusion.place_ref, bf16[4,2,2,32,1536]{4,3,2,1,0:T(8,128)(2,1)S(1)} %all_to_all.20.nu_a_ref, bf16[4,2,2,32,1536]{4,3,2,1,0:T(8,128)(2,1)} %collective-permute-done.4.nu_b_ref, bf16[64,1024]{1,0:T(8,128)(2,1)S(1)} %pad_maximum_fusion.5.refs_0_, ...), custom_call_target="tpu_custom_call" | custom-call | flops 2147483648 | bytes 10485760 | tf_op jit(solution)/shard_map/pallas_call | solution.py:136
  99.7 1.3 fusion.3
  101.0 0.1 dynamic-slice_convert_fusion
  101.1 1.3 collective-permute-start.19
  102.4 9.2 %collective-permute-done.19 = bf16[512,512]{1,0:T(8,128)(2,1)S(1)} collective-permute-done((bf16[512,512]{1,0:T(8,128)(2,1)S(1)}, bf16[512,512]{1,0:T(8,128)(2,1)S(1)}, u32[]{:S(2)}, u32[]{:S(2)}) %collective-permute-start.19) | collective-permute-done | bytes 524320 | tf_op jit(solution)/shard_map/ppermute | solution.py:47
  111.5 0.2 add_convert_fusion
  111.7 22.4 %all_to_all.21 = bf16[8,64,512]{2,1,0:T(8,128)(2,1)S(1)} all-to-all(bf16[8,64,512]{2,1,0:T(8,128)(2,1)S(1)} %bitcast.101), channel_id=1, replica_groups=mesh['xh'=2,'y'=4,'xl'=2,'zh'=4,'zl'=2,'core'=2] {'zh','zl'}, dimensions={0} | all-to-all | bytes 1048576 | tf_op jit(solution)/shard_map/all_to_all | solution.py:197
  134.1 0.1 fusion.1
  134.1 0.8 broadcast_in_dim.9
  135.0 3.5 %all-to-all-start.2 = ((bf16[8,64,512]{2,1,0:T(8,128)(2,1)}), bf16[8,64,512]{2,1,0:T(8,128)(2,1)S(1)}, u32[]{:S(2)}, u32[]{:S(2)}) async-start(bf16[8,64,512]{2,1,0:T(8,128)(2,1)} %broadcast_in_dim.9), calls=%async_computation.2 | async-start | bytes 1048576 | tf_op jit(solution)/shard_map/all_to_all | solution.py:52
  138.5 13.4 %all-to-all-done.2 = bf16[8,64,512]{2,1,0:T(8,128)(2,1)S(1)} async-done(((bf16[8,64,512]{2,1,0:T(8,128)(2,1)}), bf16[8,64,512]{2,1,0:T(8,128)(2,1)S(1)}, u32[]{:S(2)}, u32[]{:S(2)}) %all-to-all-start.2) | async-done | bytes 524320 | tf_op jit(solution)/shard_map/all_to_all | solution.py:52
  151.9 1.2 collective-permute-start.21
  153.1 4.3 %constant_dynamic-slice_fusion = (bf16[512,2048]{1,0:T(8,128)(2,1)S(1)}, bf16[512,2048]{1,0:T(8,128)(2,1)S(1)}, bf16[512,2048]{1,0:T(8,128)(2,1)S(1)}, bf16[512,2048]{1,0:T(8,128)(2,1)S(1)}) fusion(bf16[2048,2048]{1,0:T(8,128)(2,1)} %param.7, s32[]{:T(128)S(6)} %select_n.120, s32[]{:T(128)S(6)} %select_n.118, s32[]{:T(128)S(6)} %select_n.117, s32[]{:T(128)S(6)} %select_n.119), kind=kLoop, calls=%fused_computation.29 | loop fusion | bytes 16777232 | tf_op jit(solution)/shard_map/dynamic_slice | solution.py:185
  157.5 0.1 collective-permute-start.20
  157.6 1.3 fusion.4
  158.9 2.2 %collective-permute-done.21 = bf16[512,512]{1,0:T(8,128)(2,1)S(1)} collective-permute-done((bf16[512,512]{1,0:T(8,128)(2,1)S(1)}, bf16[512,512]{1,0:T(8,128)(2,1)S(1)}, u32[]{:S(2)}, u32[]{:S(2)}) %collective-permute-start.21) | collective-permute-done | bytes 524320 | tf_op jit(solution)/shard_map/ppermute | solution.py:47
  161.1 0.0 collective-permute-start.22
  161.1 1.3 fusion.6
  162.4 1.3 fusion.5
  163.7 1.9 negate_convert_fusion
  165.6 31.4 %all_to_all.22 = bf16[8,64,2048]{2,1,0:T(8,128)(2,1)S(1)} all-to-all(bf16[8,64,2048]{2,1,0:T(8,128)(2,1)S(1)} %bitcast.100), channel_id=1, replica_groups=mesh['xh'=2,'y'=4,'xl'=2,'zh'=4,'zl'=2,'core'=2] {'y','xh'}, dimensions={0} | all-to-all | bytes 4194304 | tf_op jit(solution)/shard_map/all_to_all | solution.py:207
  197.0 1.0 fusion
  (25 shorter events, 0.2 us)
Async XLA Ops:
  0.0 12.9 %collective-permute-start = (bf16[32,2048]{1,0:T(8,128)(2,1)}, bf16[32,2048]{1,0:T(8,128)(2,1)S(1)}, u32[]{:S(2)}, u32[]{:S(2)}) collective-permute-start(bf16[32,2048]{1,0:T(8,128)(2,1)} %bitcast.110), channel_id=1, source_target_pairs={{0,64},{1,65},{2,66},{3,67},{4,32},{5,33},{6,34},{7,35},{8,0},{9,1... | collective-permute-start | bytes 393224 | tf_op jit(solution)/shard_map/ppermute | solution.py:157
  12.9 12.0 %copy-start = (bf16[32,1024]{1,0:T(8,128)(2,1)}, bf16[32,1024]{1,0:T(8,128)(2,1)S(1)}, u32[]{:S(2)}) copy-start(bf16[32,1024]{1,0:T(8,128)(2,1)S(1)} %get-tuple-element.26.ours_ref) | copy-start | bytes 196612
  12.9 11.9 %collective-permute-start.2 = (bf16[32,2048]{1,0:T(8,128)(2,1)S(1)}, bf16[32,2048]{1,0:T(8,128)(2,1)S(1)}, u32[]{:S(2)}, u32[]{:S(2)}) collective-permute-start(bf16[32,2048]{1,0:T(8,128)(2,1)S(1)} %pad_maximum_fusion.4), channel_id=1, source_target_pairs={{0,128},{128,0},{1,129},{129,1},{2,130},{130,2},{3,131},{131,3},{4... | collective-permute-start | bytes 393224 | tf_op jit(solution)/shard_map/ppermute | solution.py:47
  18.2 35.5 %copy-start.1 = (bf16[2048,32]{0,1:T(8,128)(2,1)S(1)}, bf16[2048,32]{0,1:T(8,128)(2,1)}, u32[]{:S(2)}) copy-start(bf16[2048,32]{0,1:T(8,128)(2,1)} %param.4) | copy-start | bytes 393220
  18.2 6.7 %collective-permute-start.3 = (bf16[32,1024]{1,0:T(8,128)(2,1)S(1)}, bf16[32,1024]{1,0:T(8,128)(2,1)S(1)}, u32[]{:S(2)}, u32[]{:S(2)}) collective-permute-start(bf16[32,1024]{1,0:T(8,128)(2,1)S(1)} %get-tuple-element.25), channel_id=1, source_target_pairs={{0,130},{2,128},{128,2},{130,0},{1,131},{3,129},{129,3},{131,1},{4... | collective-permute-start | bytes 196616 | tf_op jit(solution)/shard_map/ppermute | solution.py:162
  18.2 6.7 %collective-permute-start.1 = (bf16[32,1024]{1,0:T(8,128)(2,1)S(1)}, bf16[32,1024]{1,0:T(8,128)(2,1)S(1)}, u32[]{:S(2)}, u32[]{:S(2)}) collective-permute-start(bf16[32,1024]{1,0:T(8,128)(2,1)S(1)} %get-tuple-element.25), channel_id=1, source_target_pairs={{0,2},{2,0},{1,3},{3,1},{4,6},{6,4},{5,7},{7,5},{8,10},{10,8},{9,1... | collective-permute-start | bytes 196616 | tf_op jit(solution)/shard_map/ppermute | solution.py:47
  24.8 0.6 copy-start.3
  24.8 0.7 copy-start.4
  25.5 0.7 copy-start.2
  53.7 24.0 %collective-permute-start.4 = (bf16[4,2,2,32,1536]{4,3,2,1,0:T(8,128)(2,1)S(1)}, bf16[4,2,2,32,1536]{4,3,2,1,0:T(8,128)(2,1)}, u32[]{:S(2)}, u32[]{:S(2)}) collective-permute-start(bf16[4,2,2,32,1536]{4,3,2,1,0:T(8,128)(2,1)S(1)} %all_to_all.20.nu_a_ref), channel_id=1, source_target_pairs={{0,1},{1,0},{2,3},{3,2},{4,5},{5,4},{6,7},{7,6},{8,9},{9,8},{10,11... | collective-permute-start | bytes 4718600 | tf_op jit(solution)/shard_map/ppermute | solution.py:47
  53.7 3.5 %collective-permute-start.5 = (bf16[32,1024]{1,0:T(8,128)(2,1)S(1)}, bf16[32,1024]{1,0:T(8,128)(2,1)S(1)}, u32[]{:S(2)}, u32[]{:S(2)}) collective-permute-start(bf16[32,1024]{1,0:T(8,128)(2,1)S(1)} %get-tuple-element.24), channel_id=1, source_target_pairs={{0,1},{1,0},{2,3},{3,2},{4,5},{5,4},{6,7},{7,6},{8,9},{9,8},{10,11... | collective-permute-start | bytes 196616 | tf_op jit(solution)/shard_map/ppermute | solution.py:47
  57.3 6.8 %collective-permute-start.7 = (bf16[64,1024]{1,0:T(8,128)(2,1)S(1)}, bf16[64,1024]{1,0:T(8,128)(2,1)S(1)}, u32[]{:S(2)}, u32[]{:S(2)}) collective-permute-start(bf16[64,1024]{1,0:T(8,128)(2,1)S(1)} %pad_maximum_fusion.5.refs_0_), channel_id=1, source_target_pairs={{0,14},{2,4},{4,2},{6,8},{8,6},{10,12},{12,10},{14,0},{1,15},{3,5}... | collective-permute-start | bytes 393224 | tf_op jit(solution)/shard_map/ppermute | solution.py:60
  59.8 5.3 %collective-permute-start.6 = (bf16[64,1024]{1,0:T(8,128)(2,1)S(1)}, bf16[64,1024]{1,0:T(8,128)(2,1)S(1)}, u32[]{:S(2)}, u32[]{:S(2)}) collective-permute-start(bf16[64,1024]{1,0:T(8,128)(2,1)S(1)} %pad_maximum_fusion.5.refs_0_), channel_id=1, source_target_pairs={{0,2},{2,0},{4,6},{6,4},{8,10},{10,8},{12,14},{14,12},{1,3},{3,1},... | collective-permute-start | bytes 393224 | tf_op jit(solution)/shard_map/ppermute | solution.py:58
  62.6 32.3 %collective-permute-start.18 = (bf16[512,1024]{1,0:T(8,128)(2,1)}, bf16[512,1024]{1,0:T(8,128)(2,1)}, u32[]{:S(2)}, u32[]{:S(2)}) collective-permute-start(bf16[512,1024]{1,0:T(8,128)(2,1)} %get-tuple-element.17), channel_id=1, source_target_pairs={{0,1},{1,0},{2,3},{3,2},{4,5},{5,4},{6,7},{7,6},{8,9},{9,8},{10,11... | collective-permute-start | bytes 3145736 | tf_op jit(solution)/shard_map/ppermute | solution.py:47
  64.1 5.0 %collective-permute-start.8 = (bf16[64,1024]{1,0:T(8,128)(2,1)S(1)}, bf16[64,1024]{1,0:T(8,128)(2,1)S(1)}, u32[]{:S(2)}, u32[]{:S(2)}) collective-permute-start(bf16[64,1024]{1,0:T(8,128)(2,1)S(1)} %collective-permute-done.7.refs_7_), channel_id=1, source_target_pairs={{0,2},{2,0},{4,6},{6,4},{8,10},{10,8},{12,14},{14,12},{1,3},{3,1},... | collective-permute-start | bytes 393224 | tf_op jit(solution)/shard_map/ppermute | solution.py:58
  65.1 6.7 %collective-permute-start.9 = (bf16[64,1024]{1,0:T(8,128)(2,1)S(1)}, bf16[64,1024]{1,0:T(8,128)(2,1)S(1)}, u32[]{:S(2)}, u32[]{:S(2)}) collective-permute-start(bf16[64,1024]{1,0:T(8,128)(2,1)S(1)} %collective-permute-done.6.refs_1_), channel_id=1, source_target_pairs={{0,14},{2,4},{4,2},{6,8},{8,6},{10,12},{12,10},{14,0},{1,15},{3,5}... | collective-permute-start | bytes 393224 | tf_op jit(solution)/shard_map/ppermute | solution.py:60
  67.5 12.5 %collective-permute-start.13 = (bf16[64,1024]{1,0:T(8,128)(2,1)S(1)}, bf16[64,1024]{1,0:T(8,128)(2,1)S(1)}, u32[]{:S(2)}, u32[]{:S(2)}) collective-permute-start(bf16[64,1024]{1,0:T(8,128)(2,1)S(1)} %pad_maximum_fusion.5.refs_0_), channel_id=1, source_target_pairs={{0,16},{16,0},{1,17},{17,1},{2,18},{18,2},{3,19},{19,3},{4,20},{20... | collective-permute-start | bytes 393224 | tf_op jit(solution)/shard_map/ppermute | solution.py:47
  69.1 6.2 %collective-permute-start.11 = (bf16[64,1024]{1,0:T(8,128)(2,1)S(1)}, bf16[64,1024]{1,0:T(8,128)(2,1)S(1)}, u32[]{:S(2)}, u32[]{:S(2)}) collective-permute-start(bf16[64,1024]{1,0:T(8,128)(2,1)S(1)} %collective-permute-done.8.refs_2_), channel_id=1, source_target_pairs={{0,14},{2,4},{4,2},{6,8},{8,6},{10,12},{12,10},{14,0},{1,15},{3,5}... | collective-permute-start | bytes 393224 | tf_op jit(solution)/shard_map/ppermute | solution.py:60
  71.7 5.0 %collective-permute-start.10 = (bf16[64,1024]{1,0:T(8,128)(2,1)S(1)}, bf16[64,1024]{1,0:T(8,128)(2,1)S(1)}, u32[]{:S(2)}, u32[]{:S(2)}) collective-permute-start(bf16[64,1024]{1,0:T(8,128)(2,1)S(1)} %collective-permute-done.9.refs_6_), channel_id=1, source_target_pairs={{0,2},{2,0},{4,6},{6,4},{8,10},{10,8},{12,14},{14,12},{1,3},{3,1},... | collective-permute-start | bytes 393224 | tf_op jit(solution)/shard_map/ppermute | solution.py:58
  75.2 10.9 %collective-permute-start.14 = (bf16[128,1024]{1,0:T(8,128)(2,1)S(1)}, bf16[128,1024]{1,0:T(8,128)(2,1)S(1)}, u32[]{:S(2)}, u32[]{:S(2)}) collective-permute-start(bf16[128,1024]{1,0:T(8,128)(2,1)S(1)} %pad_maximum_fusion.1), channel_id=1, source_target_pairs={{0,16},{16,0},{1,17},{17,1},{2,18},{18,2},{3,19},{19,3},{4,20},{20... | collective-permute-start | bytes 786440 | tf_op jit(solution)/shard_map/ppermute | solution.py:47
  76.7 13.3 %collective-permute-start.15 = (bf16[128,1024]{1,0:T(8,128)(2,1)S(1)}, bf16[128,1024]{1,0:T(8,128)(2,1)S(1)}, u32[]{:S(2)}, u32[]{:S(2)}) collective-permute-start(bf16[128,1024]{1,0:T(8,128)(2,1)S(1)} %pad_maximum_fusion.2), channel_id=1, source_target_pairs={{0,16},{16,0},{1,17},{17,1},{2,18},{18,2},{3,19},{19,3},{4,20},{20... | collective-permute-start | bytes 786440 | tf_op jit(solution)/shard_map/ppermute | solution.py:47
  77.7 17.2 %collective-permute-start.16 = (bf16[128,1024]{1,0:T(8,128)(2,1)S(1)}, bf16[128,1024]{1,0:T(8,128)(2,1)S(1)}, u32[]{:S(2)}, u32[]{:S(2)}) collective-permute-start(bf16[128,1024]{1,0:T(8,128)(2,1)S(1)} %pad_maximum_fusion.3), channel_id=1, source_target_pairs={{0,16},{16,0},{1,17},{17,1},{2,18},{18,2},{3,19},{19,3},{4,20},{20... | collective-permute-start | bytes 786440 | tf_op jit(solution)/shard_map/ppermute | solution.py:47
  80.1 5.1 %collective-permute-start.12 = (bf16[64,1024]{1,0:T(8,128)(2,1)S(1)}, bf16[64,1024]{1,0:T(8,128)(2,1)S(1)}, u32[]{:S(2)}, u32[]{:S(2)}) collective-permute-start(bf16[64,1024]{1,0:T(8,128)(2,1)S(1)} %collective-permute-done.11.refs_5_), channel_id=1, source_target_pairs={{0,2},{2,0},{4,6},{6,4},{8,10},{10,8},{12,14},{14,12},{1,3},{3,1},... | collective-permute-start | bytes 393224 | tf_op jit(solution)/shard_map/ppermute | solution.py:58
  85.1 9.7 %collective-permute-start.17 = (bf16[64,1024]{1,0:T(8,128)(2,1)S(1)}, bf16[64,1024]{1,0:T(8,128)(2,1)S(1)}, u32[]{:S(2)}, u32[]{:S(2)}) collective-permute-start(bf16[64,1024]{1,0:T(8,128)(2,1)S(1)} %collective-permute-done.12.refs_4_), channel_id=1, source_target_pairs={{0,16},{16,0},{1,17},{17,1},{2,18},{18,2},{3,19},{19,3},{4,20},{20... | collective-permute-start | bytes 393224 | tf_op jit(solution)/shard_map/ppermute | solution.py:47
  101.1 10.4 %collective-permute-start.19 = (bf16[512,512]{1,0:T(8,128)(2,1)S(1)}, bf16[512,512]{1,0:T(8,128)(2,1)S(1)}, u32[]{:S(2)}, u32[]{:S(2)}) collective-permute-start(bf16[512,512]{1,0:T(8,128)(2,1)S(1)} %dynamic-slice_convert_fusion), channel_id=1, source_target_pairs={{0,16},{16,0},{1,17},{17,1},{2,18},{18,2},{3,19},{19,3},{4,20},{20... | collective-permute-start | bytes 1572872 | tf_op jit(solution)/shard_map/ppermute | solution.py:47
  135.0 16.9 %all-to-all-start.2 = ((bf16[8,64,512]{2,1,0:T(8,128)(2,1)}), bf16[8,64,512]{2,1,0:T(8,128)(2,1)S(1)}, u32[]{:S(2)}, u32[]{:S(2)}) async-start(bf16[8,64,512]{2,1,0:T(8,128)(2,1)} %broadcast_in_dim.9), calls=%async_computation.2 | async-start | bytes 1048576 | tf_op jit(solution)/shard_map/all_to_all | solution.py:52
  151.9 9.2 %collective-permute-start.21 = (bf16[512,512]{1,0:T(8,128)(2,1)S(1)}, bf16[512,512]{1,0:T(8,128)(2,1)S(1)}, u32[]{:S(2)}, u32[]{:S(2)}) collective-permute-start(bf16[512,512]{1,0:T(8,128)(2,1)S(1)} %bitcast.104), channel_id=1, source_target_pairs={{0,16},{16,0},{1,17},{17,1},{2,18},{18,2},{3,19},{19,3},{4,20},{20... | collective-permute-start | bytes 1572872 | tf_op jit(solution)/shard_map/ppermute | solution.py:47
  157.5 4.9 %collective-permute-start.20 = (bf16[512,512]{1,0:T(8,128)(2,1)S(1)}, bf16[512,512]{1,0:T(8,128)(2,1)S(1)}, u32[]{:S(2)}, u32[]{:S(2)}) collective-permute-start(bf16[512,512]{1,0:T(8,128)(2,1)S(1)} %bitcast.105), channel_id=1, source_target_pairs={{0,1},{1,0},{2,3},{3,2},{4,5},{5,4},{6,7},{7,6},{8,9},{9,8},{10,11... | collective-permute-start | bytes 1572872 | tf_op jit(solution)/shard_map/ppermute | solution.py:47
  161.1 2.6 %collective-permute-start.22 = (bf16[512,512]{1,0:T(8,128)(2,1)S(1)}, bf16[512,512]{1,0:T(8,128)(2,1)S(1)}, u32[]{:S(2)}, u32[]{:S(2)}) collective-permute-start(bf16[512,512]{1,0:T(8,128)(2,1)S(1)} %collective-permute-done.21), channel_id=1, source_target_pairs={{0,1},{1,0},{2,3},{3,2},{4,5},{5,4},{6,7},{7,6},{8,9},{9,8},{10,11... | collective-permute-start | bytes 1572872 | tf_op jit(solution)/shard_map/ppermute | solution.py:47

commit v7 on v6

--- a/solution.py
+++ b/solution.py
@@ -47,11 +47,6 @@
     return lax.ppermute(x, axis, PAIR)
 
 
-def gather(x, axes, count):
-    copies = jnp.broadcast_to(x[None], (count,) + x.shape)
-    return lax.all_to_all(copies, axes, 0, 0, tiled=False)
-
-
 def ring(x):
     near, far = [x], [x]
     for step in range(1, 5):
@@ -94,10 +89,28 @@
     )(ours, pair, over, both, applied)
 
 
-def weigh(places, nu_a, nu_b, near, away, own, other):
+def round_and_fan(terms):
+    def body(terms_ref, out_ref):
+        value = total(terms_ref[...]).astype(BF)
+        for k in range(8):
+            out_ref[k] = value
+
+    vmem = pl.BlockSpec(memory_space=pltpu.VMEM)
+    return pl.pallas_call(
+        body,
+        out_shape=jax.ShapeDtypeStruct(terms.shape, BF),
+        in_specs=[vmem],
+        out_specs=vmem,
+        cost_estimate=pl.CostEstimate(flops=1 << 18, bytes_accessed=1 << 20, transcendentals=0),
+    )(terms)
+
+
+def weigh(places, nu_a, nu_b, near, away, own, other, first):
     def body(place_ref, nu_a_ref, nu_b_ref, *refs):
         near_refs, away_refs = refs[:8], refs[8:13]
-        own_ref, other_ref, out_ref, mu_a, mu_b = refs[13:]
+        own_ref, other_ref, out_ref = refs[13:16]
+        mu_a, mu_b = refs[-2:]
+        points = pl.ds(pl.multiple_of(place_ref[4] * 512, 512), 512)
         across = {
             0: (away_refs[0], 0),
             1: (away_refs[1], 0),
@@ -113,8 +126,8 @@
             for x, (ref, start) in enumerate(((near_refs[n], 0), across[n])):
                 side = place_ref[1] if x == 0 else 1 - place_ref[1]
                 row = pl.multiple_of(((y * 2 + side) * 2 + n % 2) * 32, 32)
-                mu_a[pl.ds(row, 32), :] = ref[start : start + 32, :]
-                mu_b[pl.ds(row, 32), :] = ref[start + 32 : start + 64, :]
+                mu_a[pl.ds(row, 32), :] = ref[start : start + 32, points]
+                mu_b[pl.ds(row, 32), :] = ref[start + 32 : start + 64, points]
 
         mine = place_ref[0]
 
@@ -124,24 +137,36 @@
             part_b = nu_b_ref[:, :, :, :, pl.ds(start, 256)].reshape(512, 256)
             density = dot(part_a, mu_a[...]) + dot(part_b, mu_b[...])
             row = pl.multiple_of((t % 2) * 256, 256)
-            ours = own_ref[pl.ds(row, 256), :]
-            theirs = other_ref[pl.ds(row, 256), :]
+            ours = own_ref[pl.ds(row, 256), points]
+            theirs = other_ref[pl.ds(row, 256), points]
             factor = jnp.where(t // 2 == mine, ours.astype(F32), theirs.astype(F32))
             out_ref[pl.ds(start, 256), :] = (density * factor).astype(BF)
             return carry
 
         lax.fori_loop(0, 4, tile, 0)
+        if first:
+            flip = jnp.bitwise_xor(mine, 1)
+            for ref, side in ((nu_a_ref, mine), (nu_b_ref, flip)):
+                lanes = pl.ds(pl.multiple_of(side * 512, 512), 512)
+                for y in range(4):
+                    for k in range(2):
+                        row = pl.multiple_of((y * 2 + jnp.bitwise_xor(place_ref[5], k)) * 64, 64)
+                        values = ref[y, k, :, :, 1024:].reshape(64, 512)
+                        refs[16][pl.ds(row, 64), lanes] = values
 
     vmem = pl.BlockSpec(memory_space=pltpu.VMEM)
     return pl.pallas_call(
         body,
-        out_shape=jax.ShapeDtypeStruct((1024, 1024), BF),
+        out_shape=[
+            jax.ShapeDtypeStruct((1024, 512), BF),
+            jax.ShapeDtypeStruct((512, 1024), BF),
+        ][: 1 + first],
         in_specs=[pl.BlockSpec(memory_space=pltpu.SMEM)] + [vmem] * 17,
-        out_specs=vmem,
-        scratch_shapes=[pltpu.VMEM((512, 1024), BF), pltpu.VMEM((512, 1024), BF)],
+        out_specs=[vmem] * (1 + first),
+        scratch_shapes=[pltpu.VMEM((512, 512), BF), pltpu.VMEM((512, 512), BF)],
         compiler_params=pltpu.CompilerParams(vmem_limit_bytes=32 << 20),
         cost_estimate=pl.CostEstimate(
-            flops=2 * 1024**3, bytes_accessed=10 << 20, transcendentals=0
+            flops=1024**3, bytes_accessed=10 << 20, transcendentals=0
         ),
     )(places, nu_a, nu_b, *near, *away, own, other)
 
@@ -163,14 +188,6 @@
     copies = fan(ours, pair, over, both, applied.T)
     nu = lax.all_to_all(copies, "y", 0, 0, tiled=False)
     nu_partner = swap(nu, "core")
-
-    def pick(c, k):
-        sides = [v[:, :, :, :, 1024:].reshape(4, 2, 64, 512) for v in (nu, nu_partner)]
-        mine, other = [jnp.where(xh == 0, v[:, k], v[:, 1 - k]) for v in sides]
-        return jnp.where(core == c, mine, other)
-
-    blocks = [jnp.concatenate([pick(0, k), pick(1, k)], axis=2) for k in range(2)]
-    blocks = jnp.stack(blocks, axis=1).reshape(512, 1024)
     mu_own = half(bands, core, 1)
     mu_other = swap(half(bands, 1 - core, 1), "core")
     near = ring(jnp.concatenate([mu_own, mu_other], axis=0))
@@ -186,25 +203,31 @@
     ]
     fits = lax.optimization_barrier(fits)
 
-    places = jnp.stack([core, jnp.bitwise_xor(xl, xh), zh + 2, 1 - 2 * zl])
-    weighted = weigh(places, nu, nu_partner, near, away, own, other)
-
-    partial = lax.dot_general(
-        weighted, blocks, (((0,), (1,)), ((), ())), preferred_element_type=F32
-    )
-    arrived = swap(half(partial, 1 - xl, 0).astype(BF), "xl")
-    two = (half(partial, xl, 0) + arrived.astype(F32)).astype(BF)
+    operands = (nu, nu_partner, near, away, own, other)
+    shared = [core, jnp.bitwise_xor(xl, xh), zh + 2, 1 - 2 * zl]
+    far_half, blocks = weigh(jnp.stack(shared + [1 - xl, xh]), *operands, True)
+    (own_half,) = weigh(jnp.stack(shared + [xl, xh]), *operands, False)
+
+    def project(weighted):
+        return lax.dot_general(
+            weighted, blocks, (((0,), (1,)), ((), ())), preferred_element_type=F32
+        )
+
+    arrived = swap(project(far_half).astype(BF), "xl")
+    two = (project(own_half) + arrived.astype(F32)).astype(BF)
     terms = lax.all_to_all(two.reshape(8, 64, 512), Z, 0, 0, tiled=False)
-    low = total(terms).astype(BF)
-    p0 = gather(low, Z, 8).reshape(512, 512)
+    p0 = lax.all_to_all(round_and_fan(terms), Z, 0, 0, tiled=False).reshape(512, 512)
     p1 = swap(p0, "xl")
     p2 = swap(p0, "core")
-    p3 = swap(p1, "core")
     result = dot(p0, fits[0])
     result = result + dot(p2, fits[2])
+    p1, result = lax.optimization_barrier((p1, result))
+    p3 = swap(p1, "core")
     result = result + dot(p1, fits[1])
     result = result + dot(p3, fits[3])
-    terms = lax.all_to_all((-result).astype(BF).reshape(8, 64, 2048), ("y", "xh"), 0, 0, tiled=False)
+    terms = lax.all_to_all(
+        (-result).astype(BF).reshape(8, 64, 2048), ("y", "xh"), 0, 0, tiled=False
+    )
     return total(terms).astype(BF)
 
 

time: 200 us -> 210 us (1.050)
  Pallas kernels: 7.15 us -> 12.2 us
  local copies, waits for them, and re-layouts: 11.2 us -> 14.3 us
  waiting for transfers between devices: 62.6 us -> 64.8 us
    pallas_call x1 -> x3, Pallas kernels: 4.87 us -> 9.95 us  [the longest x2 8.05 us: weigh(): pl.pallas_call(body, out_shape=[jax.ShapeDtypeStruct((1024, 512), BF), ja...]
    unnamed x10 -> x26, local copies, waits for them, and re-layouts: 1.3 us -> 6.33 us
    all_to_all x1, blocking collectives: 22.4 us -> 18.8 us  [program(): terms = lax.all_to_all(two.reshape(8, 64, 512), Z, 0, 0, tiled=False)]
    ppermute x14, starting transfers between devices: 14 us -> 10.5 us  [swap(): return lax.ppermute(x, axis, PAIR)]
    ppermute x4, waiting for transfers between devices: 6.93 us -> 9.79 us  [ring(): near.append(lax.ppermute(far[step - 1], Z, MATE))]
    ppermute x1, waiting for transfers between devices: 5.1 us -> 2.4 us  [program(): both = lax.ppermute(theirs, ('xh', 'zl'), ((0, 3), (1, 2), (2, 1), (3, 0)))]
    ppermute x4, starting transfers between devices: 0.99 us -> 3.16 us  [ring(): near.append(lax.ppermute(far[step - 1], Z, MATE))]
  transfers between devices with their start and end apart: 24 -> 24, of which waited for: 15 -> 17; matrix products, arithmetic and copies ran while one was open for 7% -> 6% of each run, Pallas kernels for 0% -> 2%
where the time goes in v7:
time: 210 us; the launch traced here: 208 us
  blocking collectives  77 us (37%)
  waiting for transfers between devices  64.8 us (31%)
  starting transfers between devices  28 us (13%)
  local copies, waits for them, and re-layouts  14.3 us (7%)
  Pallas kernels  12.2 us (6%)
  matrix products  8.75 us (4%)
  other arithmetic  2.52 us (1%)
    all_to_all x1, blocking collectives, program(): lax.all_to_all((-result).astype(BF).reshape(8, 64, 2048), ('y', 'xh'), 0,...  31.1 us
    all_to_all x1, blocking collectives, program(): nu = lax.all_to_all(copies, 'y', 0, 0, tiled=False)  27 us
    ppermute x14, waiting for transfers between devices, swap(): return lax.ppermute(x, axis, PAIR)  24.4 us
    all_to_all x1, blocking collectives, program(): terms = lax.all_to_all(two.reshape(8, 64, 512), Z, 0, 0, tiled=False)  18.8 us
    all_to_all x1, waiting for transfers between devices, program(): lax.all_to_all(round_and_fan(terms), Z, 0, 0, tiled=False).reshape(512, 512)  13.5 us
    ppermute x14, starting transfers between devices, swap(): return lax.ppermute(x, axis, PAIR)  10.5 us
    ppermute x4, waiting for transfers between devices, ring(): near.append(lax.ppermute(far[step - 1], Z, MATE))  9.79 us
    ppermute x1, waiting for transfers between devices, program(): rows = lax.ppermute(bands, NAMES, far_pairs())  8.93 us
  transfers between devices with their start and end apart: 24, of which 17 were waited for; matrix products, arithmetic and copies ran while one was open for 6% of the time, Pallas kernels for 2%

profile of v7, /device:TPU:8, one launch (start us, length us, event | category | flops | bytes accessed | tf_op | source)
XLA Modules:
  0.0 207.8 jit_solution(16504904872973733711)
XLA Ops:
  0.0 3.2 %collective-permute-start = (bf16[32,2048]{1,0:T(8,128)(2,1)}, bf16[32,2048]{1,0:T(8,128)(2,1)S(1)}, u32[]{:S(2)}, u32[]{:S(2)}) collective-permute-start(bf16[32,2048]{1,0:T(8,128)(2,1)} %bitcast.37), channel_id=1, source_target_pairs={{0,64},{1,65},{2,66},{3,67},{4,32},{5,33},{6,34},{7,35},{8,0},{9,1... | collective-permute-start | bytes 393224 | tf_op jit(solution)/shard_map/ppermute | solution.py:182
  3.2 0.8 fusion.2
  3.9 8.9 %collective-permute-done = bf16[32,2048]{1,0:T(8,128)(2,1)S(1)} collective-permute-done((bf16[32,2048]{1,0:T(8,128)(2,1)}, bf16[32,2048]{1,0:T(8,128)(2,1)S(1)}, u32[]{:S(2)}, u32[]{:S(2)}) %collective-permute-start) | collective-permute-done | bytes 131104 | tf_op jit(solution)/shard_map/ppermute | solution.py:182
  12.9 5.3 %collective-permute-start.2 = (bf16[32,2048]{1,0:T(8,128)(2,1)S(1)}, bf16[32,2048]{1,0:T(8,128)(2,1)S(1)}, u32[]{:S(2)}, u32[]{:S(2)}) collective-permute-start(bf16[32,2048]{1,0:T(8,128)(2,1)S(1)} %pad_maximum_fusion.3), channel_id=1, source_target_pairs={{0,128},{128,0},{1,129},{129,1},{2,130},{130,2},{3,131},{131,3},{4... | collective-permute-start | bytes 393224 | tf_op jit(solution)/shard_map/ppermute | solution.py:47
  18.2 1.6 collective-permute-start.3
  19.7 2.7 %collective-permute-done.1.pair_ref = bf16[32,1024]{1,0:T(8,128)(2,1)S(1)} collective-permute-done((bf16[32,1024]{1,0:T(8,128)(2,1)S(1)}, bf16[32,1024]{1,0:T(8,128)(2,1)S(1)}, u32[]{:S(2)}, u32[]{:S(2)}) %collective-permute-start.1) | collective-permute-done | bytes 65568 | tf_op jit(solution)/shard_map/ppermute | solution.py:47
  22.4 2.4 %collective-permute-done.3.both_ref = bf16[32,1024]{1,0:T(8,128)(2,1)S(1)} collective-permute-done((bf16[32,1024]{1,0:T(8,128)(2,1)S(1)}, bf16[32,1024]{1,0:T(8,128)(2,1)S(1)}, u32[]{:S(2)}, u32[]{:S(2)}) %collective-permute-start.3) | collective-permute-done | bytes 65568 | tf_op jit(solution)/shard_map/ppermute | solution.py:187
  24.8 0.0 collective-permute-done.2.over_ref
  24.9 0.6 copy-done.12
  25.5 0.7 copy-done.10
  26.1 2.3 %shard_map.46 = bf16[4,2,2,32,1536]{4,3,2,1,0:T(8,128)(2,1)} custom-call(bf16[32,1024]{1,0:T(8,128)(2,1)} %copy-done.8, bf16[32,1024]{1,0:T(8,128)(2,1)} %copy-done.11, bf16[32,2048]{1,0:T(8,128)(2,1)} %copy-done.10, bf16[32,1024]{1,0:T(8,128)(2,1)} %copy-done.12, bf16[64,512]{1,0:T(8,128)(2,1)} %bitcast.36), custom_call_target="tpu_custom_call" | custom-call | bytes 2097152 | tf_op jit(solution)/shard_map/pallas_call | solution.py:83
  28.4 27.0 %all_to_all.20.nu_a_ref = bf16[4,2,2,32,1536]{4,3,2,1,0:T(8,128)(2,1)S(1)} all-to-all(bf16[4,2,2,32,1536]{4,3,2,1,0:T(8,128)(2,1)} %shard_map.46), channel_id=1, replica_groups=mesh['xh'=2,'y'=4,'xl'=2,'zh'=4,'zl'=2,'core'=2] {'y'}, dimensions={0} | all-to-all | bytes 3145728 | tf_op jit(solution)/shard_map/all_to_all | solution.py:189
  55.5 0.6 collective-permute-start.5
  56.1 2.7 %constant_dynamic-slice_fusion.4 = (bf16[512,1024]{1,0:T(8,128)(2,1)}, bf16[512,1024]{1,0:T(8,128)(2,1)S(1)}) fusion(bf16[512,2048]{1,0:T(8,128)(2,1)} %param.5, s32[]{:T(128)S(6)} %select_n.29, s32[]{:T(128)S(6)} %select_n.28), kind=kLoop, calls=%fused_computation.18 | loop fusion | bytes 4194312 | tf_op jit(solution)/shard_map/dynamic_slice | solution.py:61
  58.8 0.0 collective-permute-start.18
  58.8 0.2 collective-permute-done.5
  59.0 0.4 collective-permute-start.6
  59.4 2.5 %collective-permute-start.7 = (bf16[64,1024]{1,0:T(8,128)(2,1)S(1)}, bf16[64,1024]{1,0:T(8,128)(2,1)S(1)}, u32[]{:S(2)}, u32[]{:S(2)}) collective-permute-start(bf16[64,1024]{1,0:T(8,128)(2,1)S(1)} %pad_maximum_fusion.4.refs_0_), channel_id=1, source_target_pairs={{0,14},{2,4},{4,2},{6,8},{8,6},{10,12},{12,10},{14,0},{1,15},{3,5}... | collective-permute-start | bytes 393224 | tf_op jit(solution)/shard_map/ppermute | solution.py:55
  61.9 2.9 %collective-permute-done.6.refs_1_ = bf16[64,1024]{1,0:T(8,128)(2,1)S(1)} collective-permute-done((bf16[64,1024]{1,0:T(8,128)(2,1)S(1)}, bf16[64,1024]{1,0:T(8,128)(2,1)S(1)}, u32[]{:S(2)}, u32[]{:S(2)}) %collective-permute-start.6) | collective-permute-done | bytes 131104 | tf_op jit(solution)/shard_map/ppermute | solution.py:53
  64.8 2.5 %collective-permute-start.9 = (bf16[64,1024]{1,0:T(8,128)(2,1)S(1)}, bf16[64,1024]{1,0:T(8,128)(2,1)S(1)}, u32[]{:S(2)}, u32[]{:S(2)}) collective-permute-start(bf16[64,1024]{1,0:T(8,128)(2,1)S(1)} %collective-permute-done.6.refs_1_), channel_id=1, source_target_pairs={{0,14},{2,4},{4,2},{6,8},{8,6},{10,12},{12,10},{14,0},{1,15},{3,5}... | collective-permute-start | bytes 393224 | tf_op jit(solution)/shard_map/ppermute | solution.py:55
  67.3 3.7 %collective-permute-done.9.refs_6_ = bf16[64,1024]{1,0:T(8,128)(2,1)S(1)} collective-permute-done((bf16[64,1024]{1,0:T(8,128)(2,1)S(1)}, bf16[64,1024]{1,0:T(8,128)(2,1)S(1)}, u32[]{:S(2)}, u32[]{:S(2)}) %collective-permute-start.9) | collective-permute-done | bytes 131104 | tf_op jit(solution)/shard_map/ppermute | solution.py:55
  71.0 0.1 collective-permute-start.14
  71.1 1.6 collective-permute-done.8.refs_2_
  72.7 1.0 collective-permute-start.11
  73.7 2.2 %collective-permute-done.10.refs_3_ = bf16[64,1024]{1,0:T(8,128)(2,1)S(1)} collective-permute-done((bf16[64,1024]{1,0:T(8,128)(2,1)S(1)}, bf16[64,1024]{1,0:T(8,128)(2,1)S(1)}, u32[]{:S(2)}, u32[]{:S(2)}) %collective-permute-start.10) | collective-permute-done | bytes 131104 | tf_op jit(solution)/shard_map/ppermute | solution.py:53
  75.9 0.7 pad_maximum_fusion.1
  76.7 2.2 %collective-permute-done.11.refs_5_ = bf16[64,1024]{1,0:T(8,128)(2,1)S(1)} collective-permute-done((bf16[64,1024]{1,0:T(8,128)(2,1)S(1)}, bf16[64,1024]{1,0:T(8,128)(2,1)S(1)}, u32[]{:S(2)}, u32[]{:S(2)}) %collective-permute-start.11) | collective-permute-done | bytes 131104 | tf_op jit(solution)/shard_map/ppermute | solution.py:55
  78.9 0.4 collective-permute-start.15
  79.3 0.7 pad_maximum_fusion.2
  80.0 2.3 %collective-permute-done.13.refs_8_ = bf16[64,1024]{1,0:T(8,128)(2,1)S(1)} collective-permute-done((bf16[64,1024]{1,0:T(8,128)(2,1)S(1)}, bf16[64,1024]{1,0:T(8,128)(2,1)S(1)}, u32[]{:S(2)}, u32[]{:S(2)}) %collective-permute-start.13) | collective-permute-done | bytes 131104 | tf_op jit(solution)/shard_map/ppermute | solution.py:47
  82.3 0.6 copy-done.3
  83.0 0.0 collective-permute-start.16
  83.0 0.7 copy-done
  83.7 2.8 %collective-permute-start.12 = (bf16[64,1024]{1,0:T(8,128)(2,1)S(1)}, bf16[64,1024]{1,0:T(8,128)(2,1)}, u32[]{:S(2)}, u32[]{:S(2)}) collective-permute-start(bf16[64,1024]{1,0:T(8,128)(2,1)S(1)} %collective-permute-done.11.refs_5_), channel_id=1, source_target_pairs={{0,2},{2,0},{4,6},{6,4},{8,10},{10,8},{12,14},{14,12},{1,3},{3,1},... | collective-permute-start | bytes 393224 | tf_op jit(solution)/shard_map/ppermute | solution.py:53
  86.4 3.0 %collective-permute-done.12.refs_4_ = bf16[64,1024]{1,0:T(8,128)(2,1)} collective-permute-done((bf16[64,1024]{1,0:T(8,128)(2,1)S(1)}, bf16[64,1024]{1,0:T(8,128)(2,1)}, u32[]{:S(2)}, u32[]{:S(2)}) %collective-permute-start.12) | collective-permute-done | bytes 131104 | tf_op jit(solution)/shard_map/ppermute | solution.py:53
  89.5 2.0 collective-permute-start.17
  91.5 0.1 stack.40.place_ref
  91.6 1.5 collective-permute-done.16.refs_11_
  93.1 1.6 collective-permute-done.17.refs_12_
  94.8 0.9 copy-done.1
  95.7 0.9 copy-done.4
  96.6 4.0 %shard_map.48 = (bf16[1024,512]{1,0:T(8,128)(2,1)S(1)}, bf16[512,1024]{1,0:T(8,128)(2,1)S(1)}) custom-call(s32[6]{0:T(128)S(1)} %stack.40.place_ref, bf16[4,2,2,32,1536]{4,3,2,1,0:T(8,128)(2,1)S(1)} %all_to_all.20.nu_a_ref, bf16[4,2,2,32,1536]{4,3,2,1,0:T(8,128)(2,1)} %collective-permute-done.4.nu_b_ref, bf16[64,1024]{1,0:T(8,128)(2,1)S(1)} %pad_maximum_fusion.4.refs_0_, ...), custom_call_target="tpu_custom_call" | custom-call | flops 1073741824 | bytes 10485760 | tf_op jit(solution)/shard_map/pallas_call | solution.py:158
  100.7 1.6 convolution_convert_fusion
  102.2 2.0 collective-permute-start.19
  104.3 0.1 stack.38.place_ref
  104.4 1.0 copy-done.2
  105.3 0.9 copy-done.5
  106.2 4.0 %shard_map.47 = bf16[1024,512]{1,0:T(8,128)(2,1)S(1)} custom-call(s32[6]{0:T(128)S(1)} %stack.38.place_ref, bf16[4,2,2,32,1536]{4,3,2,1,0:T(8,128)(2,1)S(1)} %all_to_all.20.nu_a_ref, bf16[4,2,2,32,1536]{4,3,2,1,0:T(8,128)(2,1)} %collective-permute-done.4.nu_b_ref, bf16[64,1024]{1,0:T(8,128)(2,1)S(1)} %pad_maximum_fusion.4.refs_0_, ...), custom_call_target="tpu_custom_call" | custom-call | flops 1073741824 | bytes 10485760 | tf_op jit(solution)/shard_map/pallas_call | solution.py:158
  110.3 3.7 %collective-permute-done.19 = bf16[512,512]{1,0:T(8,128)(2,1)} collective-permute-done((bf16[512,512]{1,0:T(8,128)(2,1)}, bf16[512,512]{1,0:T(8,128)(2,1)}, u32[]{:S(2)}, u32[]{:S(2)}) %collective-permute-start.19) | collective-permute-done | bytes 524320 | tf_op jit(solution)/shard_map/ppermute | solution.py:47
  114.0 1.8 fusion
  115.8 18.8 %all_to_all.21.terms_ref = bf16[8,64,512]{2,1,0:T(8,128)(2,1)} all-to-all(bf16[8,64,512]{2,1,0:T(8,128)(2,1)S(1)} %bitcast.34), channel_id=1, replica_groups=mesh['xh'=2,'y'=4,'xl'=2,'zh'=4,'zl'=2,'core'=2] {'zh','zl'}, dimensions={0} | all-to-all | bytes 1048576 | tf_op jit(solution)/shard_map/all_to_all | solution.py:218
  134.6 1.9 shard_map.49
  136.5 3.5 %all-to-all-start.2 = ((bf16[8,64,512]{2,1,0:T(8,128)(2,1)}), bf16[8,64,512]{2,1,0:T(8,128)(2,1)S(1)}, u32[]{:S(2)}, u32[]{:S(2)}) async-start(bf16[8,64,512]{2,1,0:T(8,128)(2,1)} %shard_map.49), calls=%async_computation.2 | async-start | bytes 1048576 | tf_op jit(solution)/shard_map/all_to_all | solution.py:219
  140.0 13.5 %all-to-all-done.2 = bf16[8,64,512]{2,1,0:T(8,128)(2,1)S(1)} async-done(((bf16[8,64,512]{2,1,0:T(8,128)(2,1)}), bf16[8,64,512]{2,1,0:T(8,128)(2,1)S(1)}, u32[]{:S(2)}, u32[]{:S(2)}) %all-to-all-start.2) | async-done | bytes 524320 | tf_op jit(solution)/shard_map/all_to_all | solution.py:219
  153.5 4.3 %constant_dynamic-slice_fusion = (bf16[512,2048]{1,0:T(8,128)(2,1)S(1)}, bf16[512,2048]{1,0:T(8,128)(2,1)S(1)}, bf16[512,2048]{1,0:T(8,128)(2,1)S(1)}, bf16[512,2048]{1,0:T(8,128)(2,1)S(1)}) fusion(bf16[2048,2048]{1,0:T(8,128)(2,1)} %param.7, s32[]{:T(128)S(6)} %select_n.33, s32[]{:T(128)S(6)} %select_n.31, s32[]{:T(128)S(6)} %select_n.30, s32[]{:T(128)S(6)} %select_n.32), kind=kLoop, calls=%fused_computation.14 | loop fusion | bytes 16777232 | tf_op jit(solution)/shard_map/dynamic_slice | solution.py:202
  157.8 0.1 collective-permute-start.20
  157.9 1.3 fusion.3
  159.2 1.4 convolution_add_fusion
  160.5 11.7 %collective-permute-done.20 = bf16[512,512]{1,0:T(8,128)(2,1)S(1)} collective-permute-done((bf16[512,512]{1,0:T(8,128)(2,1)S(1)}, bf16[512,512]{1,0:T(8,128)(2,1)S(1)}, u32[]{:S(2)}, u32[]{:S(2)}) %collective-permute-start.20) | collective-permute-done | bytes 524320 | tf_op jit(solution)/shard_map/ppermute | solution.py:47
  172.2 1.3 fusion.4
  173.5 0.6 collective-permute-done.22
  174.1 1.5 negate_convert_fusion
  175.6 31.1 %all_to_all.22 = bf16[8,64,2048]{2,1,0:T(8,128)(2,1)S(1)} all-to-all(bf16[8,64,2048]{2,1,0:T(8,128)(2,1)S(1)} %bitcast.30), channel_id=1, replica_groups=mesh['xh'=2,'y'=4,'xl'=2,'zh'=4,'zl'=2,'core'=2] {'y','xh'}, dimensions={0} | all-to-all | bytes 4194304 | tf_op jit(solution)/shard_map/all_to_all | solution.py:228
  206.7 1.0 fusion.1
  (36 shorter events, 0.1 us)
Async XLA Ops:
  0.0 12.9 %collective-permute-start = (bf16[32,2048]{1,0:T(8,128)(2,1)}, bf16[32,2048]{1,0:T(8,128)(2,1)S(1)}, u32[]{:S(2)}, u32[]{:S(2)}) collective-permute-start(bf16[32,2048]{1,0:T(8,128)(2,1)} %bitcast.37), channel_id=1, source_target_pairs={{0,64},{1,65},{2,66},{3,67},{4,32},{5,33},{6,34},{7,35},{8,0},{9,1... | collective-permute-start | bytes 393224 | tf_op jit(solution)/shard_map/ppermute | solution.py:182
  12.9 12.0 %copy-start.8 = (bf16[32,1024]{1,0:T(8,128)(2,1)}, bf16[32,1024]{1,0:T(8,128)(2,1)S(1)}, u32[]{:S(2)}) copy-start(bf16[32,1024]{1,0:T(8,128)(2,1)S(1)} %get-tuple-element.30.ours_ref) | copy-start | bytes 196612
  12.9 11.9 %collective-permute-start.2 = (bf16[32,2048]{1,0:T(8,128)(2,1)S(1)}, bf16[32,2048]{1,0:T(8,128)(2,1)S(1)}, u32[]{:S(2)}, u32[]{:S(2)}) collective-permute-start(bf16[32,2048]{1,0:T(8,128)(2,1)S(1)} %pad_maximum_fusion.3), channel_id=1, source_target_pairs={{0,128},{128,0},{1,129},{129,1},{2,130},{130,2},{3,131},{131,3},{4... | collective-permute-start | bytes 393224 | tf_op jit(solution)/shard_map/ppermute | solution.py:47
  18.2 37.3 %copy-start.9 = (bf16[2048,32]{0,1:T(8,128)(2,1)S(1)}, bf16[2048,32]{0,1:T(8,128)(2,1)}, u32[]{:S(2)}) copy-start(bf16[2048,32]{0,1:T(8,128)(2,1)} %param.4) | copy-start | bytes 393220
  18.2 4.3 %collective-permute-start.1 = (bf16[32,1024]{1,0:T(8,128)(2,1)S(1)}, bf16[32,1024]{1,0:T(8,128)(2,1)S(1)}, u32[]{:S(2)}, u32[]{:S(2)}) collective-permute-start(bf16[32,1024]{1,0:T(8,128)(2,1)S(1)} %get-tuple-element.29), channel_id=1, source_target_pairs={{0,2},{2,0},{1,3},{3,1},{4,6},{6,4},{5,7},{7,5},{8,10},{10,8},{9,1... | collective-permute-start | bytes 196616 | tf_op jit(solution)/shard_map/ppermute | solution.py:47
  18.2 6.7 %collective-permute-start.3 = (bf16[32,1024]{1,0:T(8,128)(2,1)S(1)}, bf16[32,1024]{1,0:T(8,128)(2,1)S(1)}, u32[]{:S(2)}, u32[]{:S(2)}) collective-permute-start(bf16[32,1024]{1,0:T(8,128)(2,1)S(1)} %get-tuple-element.29), channel_id=1, source_target_pairs={{0,130},{2,128},{128,2},{130,0},{1,131},{3,129},{129,3},{131,1},{4... | collective-permute-start | bytes 196616 | tf_op jit(solution)/shard_map/ppermute | solution.py:187
  22.4 2.4 %copy-start.11 = (bf16[32,1024]{1,0:T(8,128)(2,1)}, bf16[32,1024]{1,0:T(8,128)(2,1)S(1)}, u32[]{:S(2)}) copy-start(bf16[32,1024]{1,0:T(8,128)(2,1)S(1)} %collective-permute-done.1.pair_ref) | copy-start | bytes 196612
  24.8 0.6 copy-start.12
  25.5 0.7 copy-start.10
  55.4 39.3 %collective-permute-start.4 = (bf16[4,2,2,32,1536]{4,3,2,1,0:T(8,128)(2,1)S(1)}, bf16[4,2,2,32,1536]{4,3,2,1,0:T(8,128)(2,1)}, u32[]{:S(2)}, u32[]{:S(2)}) collective-permute-start(bf16[4,2,2,32,1536]{4,3,2,1,0:T(8,128)(2,1)S(1)} %all_to_all.20.nu_a_ref), channel_id=1, source_target_pairs={{0,1},{1,0},{2,3},{3,2},{4,5},{5,4},{6,7},{7,6},{8,9},{9,8},{10,11... | collective-permute-start | bytes 4718600 | tf_op jit(solution)/shard_map/ppermute | solution.py:47
  55.5 3.5 %collective-permute-start.5 = (bf16[32,1024]{1,0:T(8,128)(2,1)S(1)}, bf16[32,1024]{1,0:T(8,128)(2,1)S(1)}, u32[]{:S(2)}, u32[]{:S(2)}) collective-permute-start(bf16[32,1024]{1,0:T(8,128)(2,1)S(1)} %get-tuple-element.28), channel_id=1, source_target_pairs={{0,1},{1,0},{2,3},{3,2},{4,5},{5,4},{6,7},{7,6},{8,9},{9,8},{10,11... | collective-permute-start | bytes 196616 | tf_op jit(solution)/shard_map/ppermute | solution.py:47
  58.8 36.0 %collective-permute-start.18 = (bf16[512,1024]{1,0:T(8,128)(2,1)}, bf16[512,1024]{1,0:T(8,128)(2,1)}, u32[]{:S(2)}, u32[]{:S(2)}) collective-permute-start(bf16[512,1024]{1,0:T(8,128)(2,1)} %get-tuple-element.25), channel_id=1, source_target_pairs={{0,1},{1,0},{2,3},{3,2},{4,5},{5,4},{6,7},{7,6},{8,9},{9,8},{10,11... | collective-permute-start | bytes 3145736 | tf_op jit(solution)/shard_map/ppermute | solution.py:47
  59.0 5.8 %collective-permute-start.6 = (bf16[64,1024]{1,0:T(8,128)(2,1)S(1)}, bf16[64,1024]{1,0:T(8,128)(2,1)S(1)}, u32[]{:S(2)}, u32[]{:S(2)}) collective-permute-start(bf16[64,1024]{1,0:T(8,128)(2,1)S(1)} %pad_maximum_fusion.4.refs_0_), channel_id=1, source_target_pairs={{0,2},{2,0},{4,6},{6,4},{8,10},{10,8},{12,14},{14,12},{1,3},{3,1},... | collective-permute-start | bytes 393224 | tf_op jit(solution)/shard_map/ppermute | solution.py:53
  59.4 7.9 %collective-permute-start.7 = (bf16[64,1024]{1,0:T(8,128)(2,1)S(1)}, bf16[64,1024]{1,0:T(8,128)(2,1)S(1)}, u32[]{:S(2)}, u32[]{:S(2)}) collective-permute-start(bf16[64,1024]{1,0:T(8,128)(2,1)S(1)} %pad_maximum_fusion.4.refs_0_), channel_id=1, source_target_pairs={{0,14},{2,4},{4,2},{6,8},{8,6},{10,12},{12,10},{14,0},{1,15},{3,5}... | collective-permute-start | bytes 393224 | tf_op jit(solution)/shard_map/ppermute | solution.py:55
  64.8 6.2 %collective-permute-start.9 = (bf16[64,1024]{1,0:T(8,128)(2,1)S(1)}, bf16[64,1024]{1,0:T(8,128)(2,1)S(1)}, u32[]{:S(2)}, u32[]{:S(2)}) collective-permute-start(bf16[64,1024]{1,0:T(8,128)(2,1)S(1)} %collective-permute-done.6.refs_1_), channel_id=1, source_target_pairs={{0,14},{2,4},{4,2},{6,8},{8,6},{10,12},{12,10},{14,0},{1,15},{3,5}... | collective-permute-start | bytes 393224 | tf_op jit(solution)/shard_map/ppermute | solution.py:55
  67.3 5.4 %collective-permute-start.8 = (bf16[64,1024]{1,0:T(8,128)(2,1)S(1)}, bf16[64,1024]{1,0:T(8,128)(2,1)S(1)}, u32[]{:S(2)}, u32[]{:S(2)}) collective-permute-start(bf16[64,1024]{1,0:T(8,128)(2,1)S(1)} %collective-permute-done.7.refs_7_), channel_id=1, source_target_pairs={{0,2},{2,0},{4,6},{6,4},{8,10},{10,8},{12,14},{14,12},{1,3},{3,1},... | collective-permute-start | bytes 393224 | tf_op jit(solution)/shard_map/ppermute | solution.py:53
  71.0 5.0 %collective-permute-start.10 = (bf16[64,1024]{1,0:T(8,128)(2,1)S(1)}, bf16[64,1024]{1,0:T(8,128)(2,1)S(1)}, u32[]{:S(2)}, u32[]{:S(2)}) collective-permute-start(bf16[64,1024]{1,0:T(8,128)(2,1)S(1)} %collective-permute-done.9.refs_6_), channel_id=1, source_target_pairs={{0,2},{2,0},{4,6},{6,4},{8,10},{10,8},{12,14},{14,12},{1,3},{3,1},... | collective-permute-start | bytes 393224 | tf_op jit(solution)/shard_map/ppermute | solution.py:53
  71.0 12.0 %collective-permute-start.14 = (bf16[128,1024]{1,0:T(8,128)(2,1)S(1)}, bf16[128,1024]{1,0:T(8,128)(2,1)S(1)}, u32[]{:S(2)}, u32[]{:S(2)}) collective-permute-start(bf16[128,1024]{1,0:T(8,128)(2,1)S(1)} %pad_maximum_fusion), channel_id=1, source_target_pairs={{0,16},{16,0},{1,17},{17,1},{2,18},{18,2},{3,19},{19,3},{4,20},{20... | collective-permute-start | bytes 786440 | tf_op jit(solution)/shard_map/ppermute | solution.py:47
  72.7 6.2 %collective-permute-start.11 = (bf16[64,1024]{1,0:T(8,128)(2,1)S(1)}, bf16[64,1024]{1,0:T(8,128)(2,1)S(1)}, u32[]{:S(2)}, u32[]{:S(2)}) collective-permute-start(bf16[64,1024]{1,0:T(8,128)(2,1)S(1)} %collective-permute-done.8.refs_2_), channel_id=1, source_target_pairs={{0,14},{2,4},{4,2},{6,8},{8,6},{10,12},{12,10},{14,0},{1,15},{3,5}... | collective-permute-start | bytes 393224 | tf_op jit(solution)/shard_map/ppermute | solution.py:55
  75.9 6.4 %collective-permute-start.13 = (bf16[64,1024]{1,0:T(8,128)(2,1)S(1)}, bf16[64,1024]{1,0:T(8,128)(2,1)S(1)}, u32[]{:S(2)}, u32[]{:S(2)}) collective-permute-start(bf16[64,1024]{1,0:T(8,128)(2,1)S(1)} %pad_maximum_fusion.4.refs_0_), channel_id=1, source_target_pairs={{0,16},{16,0},{1,17},{17,1},{2,18},{18,2},{3,19},{19,3},{4,20},{20... | collective-permute-start | bytes 393224 | tf_op jit(solution)/shard_map/ppermute | solution.py:47
  78.9 12.7 %collective-permute-start.15 = (bf16[128,1024]{1,0:T(8,128)(2,1)}, bf16[128,1024]{1,0:T(8,128)(2,1)}, u32[]{:S(2)}, u32[]{:S(2)}) collective-permute-start(bf16[128,1024]{1,0:T(8,128)(2,1)} %pad_maximum_fusion.1), channel_id=1, source_target_pairs={{0,16},{16,0},{1,17},{17,1},{2,18},{18,2},{3,19},{19,3},{4,20},{20... | collective-permute-start | bytes 786440 | tf_op jit(solution)/shard_map/ppermute | solution.py:47
  82.3 0.7 copy-start.3
  83.0 10.2 %collective-permute-start.16 = (bf16[128,1024]{1,0:T(8,128)(2,1)}, bf16[128,1024]{1,0:T(8,128)(2,1)}, u32[]{:S(2)}, u32[]{:S(2)}) collective-permute-start(bf16[128,1024]{1,0:T(8,128)(2,1)} %pad_maximum_fusion.2), channel_id=1, source_target_pairs={{0,16},{16,0},{1,17},{17,1},{2,18},{18,2},{3,19},{19,3},{4,20},{20... | collective-permute-start | bytes 786440 | tf_op jit(solution)/shard_map/ppermute | solution.py:47
  83.0 0.7 copy-start
  83.7 5.8 %collective-permute-start.12 = (bf16[64,1024]{1,0:T(8,128)(2,1)S(1)}, bf16[64,1024]{1,0:T(8,128)(2,1)}, u32[]{:S(2)}, u32[]{:S(2)}) collective-permute-start(bf16[64,1024]{1,0:T(8,128)(2,1)S(1)} %collective-permute-done.11.refs_5_), channel_id=1, source_target_pairs={{0,2},{2,0},{4,6},{6,4},{8,10},{10,8},{12,14},{14,12},{1,3},{3,1},... | collective-permute-start | bytes 393224 | tf_op jit(solution)/shard_map/ppermute | solution.py:53
  89.5 5.3 %collective-permute-start.17 = (bf16[64,1024]{1,0:T(8,128)(2,1)}, bf16[64,1024]{1,0:T(8,128)(2,1)}, u32[]{:S(2)}, u32[]{:S(2)}) collective-permute-start(bf16[64,1024]{1,0:T(8,128)(2,1)} %collective-permute-done.12.refs_4_), channel_id=1, source_target_pairs={{0,16},{16,0},{1,17},{17,1},{2,18},{18,2},{3,19},{19,3},{4,20},{20... | collective-permute-start | bytes 393224 | tf_op jit(solution)/shard_map/ppermute | solution.py:47
  94.8 1.0 copy-start.1
  95.7 0.9 copy-start.4
  100.7 3.6 %copy-start.6 = (bf16[512,1024]{1,0:T(8,128)(2,1)}, bf16[512,1024]{1,0:T(8,128)(2,1)S(1)}, u32[]{:S(2)}) copy-start(bf16[512,1024]{1,0:T(8,128)(2,1)S(1)} %get-tuple-element.13) | copy-start | bytes 3145732
  102.2 11.7 %collective-permute-start.19 = (bf16[512,512]{1,0:T(8,128)(2,1)}, bf16[512,512]{1,0:T(8,128)(2,1)}, u32[]{:S(2)}, u32[]{:S(2)}) collective-permute-start(bf16[512,512]{1,0:T(8,128)(2,1)} %convolution_convert_fusion), channel_id=1, source_target_pairs={{0,16},{16,0},{1,17},{17,1},{2,18},{18,2},{3,19},{19,3},{4,20},{20... | collective-permute-start | bytes 1572872 | tf_op jit(solution)/shard_map/ppermute | solution.py:47
  104.4 1.0 copy-start.2
  105.3 0.9 copy-start.5
  106.2 7.8 %copy-start.7 = (bf16[512,1024]{1,0:T(8,128)(2,1)S(1)}, bf16[512,1024]{1,0:T(8,128)(2,1)}, u32[]{:S(2)}) copy-start(bf16[512,1024]{1,0:T(8,128)(2,1)} %copy-done.6) | copy-start | bytes 3145732
  136.5 17.0 %all-to-all-start.2 = ((bf16[8,64,512]{2,1,0:T(8,128)(2,1)}), bf16[8,64,512]{2,1,0:T(8,128)(2,1)S(1)}, u32[]{:S(2)}, u32[]{:S(2)}) async-start(bf16[8,64,512]{2,1,0:T(8,128)(2,1)} %shard_map.49), calls=%async_computation.2 | async-start | bytes 1048576 | tf_op jit(solution)/shard_map/all_to_all | solution.py:219
  153.5 5.7 %collective-permute-start.21 = (bf16[512,512]{1,0:T(8,128)(2,1)S(1)}, bf16[512,512]{1,0:T(8,128)(2,1)S(1)}, u32[]{:S(2)}, u32[]{:S(2)}) collective-permute-start(bf16[512,512]{1,0:T(8,128)(2,1)S(1)} %bitcast.31), channel_id=1, source_target_pairs={{0,1},{1,0},{2,3},{3,2},{4,5},{5,4},{6,7},{7,6},{8,9},{9,8},{10,11... | collective-permute-start | bytes 1572872 | tf_op jit(solution)/shard_map/ppermute | solution.py:47
  157.8 14.4 %collective-permute-start.20 = (bf16[512,512]{1,0:T(8,128)(2,1)S(1)}, bf16[512,512]{1,0:T(8,128)(2,1)S(1)}, u32[]{:S(2)}, u32[]{:S(2)}) collective-permute-start(bf16[512,512]{1,0:T(8,128)(2,1)S(1)} %bitcast.32), channel_id=1, source_target_pairs={{0,16},{16,0},{1,17},{17,1},{2,18},{18,2},{3,19},{19,3},{4,20},{20... | collective-permute-start | bytes 1572872 | tf_op jit(solution)/shard_map/ppermute | solution.py:47
  172.2 1.9 collective-permute-start.22

commit v8 on v7

--- a/solution.py
+++ b/solution.py
@@ -47,6 +47,11 @@
     return lax.ppermute(x, axis, PAIR)
 
 
+def gather(x, axes, count):
+    copies = jnp.broadcast_to(x[None], (count,) + x.shape)
+    return lax.all_to_all(copies, axes, 0, 0, tiled=False)
+
+
 def ring(x):
     near, far = [x], [x]
     for step in range(1, 5):
@@ -87,22 +92,6 @@
         out_specs=vmem,
         cost_estimate=pl.CostEstimate(flops=0, bytes_accessed=2 << 20, transcendentals=0),
     )(ours, pair, over, both, applied)
-
-
-def round_and_fan(terms):
-    def body(terms_ref, out_ref):
-        value = total(terms_ref[...]).astype(BF)
-        for k in range(8):
-            out_ref[k] = value
-
-    vmem = pl.BlockSpec(memory_space=pltpu.VMEM)
-    return pl.pallas_call(
-        body,
-        out_shape=jax.ShapeDtypeStruct(terms.shape, BF),
-        in_specs=[vmem],
-        out_specs=vmem,
-        cost_estimate=pl.CostEstimate(flops=1 << 18, bytes_accessed=1 << 20, transcendentals=0),
-    )(terms)
 
 
 def weigh(places, nu_a, nu_b, near, away, own, other, first):
@@ -150,9 +139,9 @@
                 lanes = pl.ds(pl.multiple_of(side * 512, 512), 512)
                 for y in range(4):
                     for k in range(2):
-                        row = pl.multiple_of((y * 2 + jnp.bitwise_xor(place_ref[5], k)) * 64, 64)
+                        row = ((1 - k) * 4 + y) * 64
                         values = ref[y, k, :, :, 1024:].reshape(64, 512)
-                        refs[16][pl.ds(row, 64), lanes] = values
+                        refs[16][row : row + 64, lanes] = values
 
     vmem = pl.BlockSpec(memory_space=pltpu.VMEM)
     return pl.pallas_call(
@@ -205,8 +194,8 @@
 
     operands = (nu, nu_partner, near, away, own, other)
     shared = [core, jnp.bitwise_xor(xl, xh), zh + 2, 1 - 2 * zl]
-    far_half, blocks = weigh(jnp.stack(shared + [1 - xl, xh]), *operands, True)
-    (own_half,) = weigh(jnp.stack(shared + [xl, xh]), *operands, False)
+    far_half, blocks = weigh(jnp.stack(shared + [1 - xl]), *operands, True)
+    (own_half,) = weigh(jnp.stack(shared + [xl]), *operands, False)
 
     def project(weighted):
         return lax.dot_general(
@@ -214,21 +203,26 @@
         )
 
     arrived = swap(project(far_half).astype(BF), "xl")
-    two = (project(own_half) + arrived.astype(F32)).astype(BF)
+    mine = lax.optimization_barrier(project(own_half))
+    two = (mine + arrived.astype(F32)).astype(BF)
     terms = lax.all_to_all(two.reshape(8, 64, 512), Z, 0, 0, tiled=False)
-    p0 = lax.all_to_all(round_and_fan(terms), Z, 0, 0, tiled=False).reshape(512, 512)
+    p0 = gather(total(terms).astype(BF), Z, 8).reshape(512, 512)
     p1 = swap(p0, "xl")
     p2 = swap(p0, "core")
-    result = dot(p0, fits[0])
-    result = result + dot(p2, fits[2])
-    p1, result = lax.optimization_barrier((p1, result))
     p3 = swap(p1, "core")
-    result = result + dot(p1, fits[1])
-    result = result + dot(p3, fits[3])
-    terms = lax.all_to_all(
-        (-result).astype(BF).reshape(8, 64, 2048), ("y", "xh"), 0, 0, tiled=False
-    )
-    return total(terms).astype(BF)
+    sums = []
+    for h in range(2):
+        part = slice(h * 256, h * 256 + 256)
+        result = dot(p0[:, part], fits[0])
+        result = result + dot(p2[:, part], fits[2])
+        result = result + dot(p1[:, part], fits[1])
+        result = result + dot(p3[:, part], fits[3])
+        terms = lax.all_to_all(
+            (-result).astype(BF).reshape(4, 64, 2048), "y", 0, 0, tiled=False
+        )
+        sums.append(total(terms))
+    crossed = swap(sums[0].astype(BF), "xh")
+    return (sums[1] + crossed.astype(F32)).astype(BF)
 
 
 def solution(mesh):

time: 210 us -> 213 us (1.014)
  blocking collectives: 77 us -> 45.4 us
  waiting for transfers between devices: 64.8 us -> 79.2 us
  starting transfers between devices: 28 us -> 37.3 us
  matrix products: 8.75 us -> 15.7 us
  local copies, waits for them, and re-layouts: 14.3 us -> 19.3 us
    all_to_all x1 -> x0, blocking collectives: 31.1 us -> none  [program(): lax.all_to_all((-result).astype(BF).reshape(8, 64, 2048), ('y', 'xh'), 0,...]
    all_to_all x1 -> x3, waiting for transfers between devices: 13.5 us -> 28.4 us  [the longest x2 21.2 us: program(): lax.all_to_all((-result).astype(BF).reshape(4, 64, 2048), 'y', 0, 0, tile...]
    all_to_all x1 -> x3, starting transfers between devices: 3.49 us -> 13.8 us  [the longest x2 10.3 us: program(): lax.all_to_all((-result).astype(BF).reshape(4, 64, 2048), 'y', 0, 0, tile...]
    dot_general x4 -> x8, matrix products: 5.4 us -> 13.4 us  [dot(): lax.dot_general(a, b, (((0,), (0,)), ((), ())), preferred_element_type=F32)]
    ppermute x4, starting transfers between devices: 3.16 us -> 0.1 us  [ring(): near.append(lax.ppermute(far[step - 1], Z, MATE))]
    dynamic_slice x1, local copies, waits for them, and re-layouts: 4.31 us -> 6.67 us  [program(): lax.dynamic_slice_in_dim(fit, jnp.bitwise_xor(place, k) * 512, 512, 0)]
    convert_element_type x0 -> x3, other arithmetic: none -> 2.21 us  [the longest x1 1.2 us: program(): two = (mine + arrived.astype(F32)).astype(BF)]
    ppermute x14 -> x15, waiting for transfers between devices: 24.4 us -> 22.3 us  [swap(): return lax.ppermute(x, axis, PAIR)]
  transfers between devices with their start and end apart: 24 -> 27, of which waited for: 17 -> 19; matrix products, arithmetic and copies ran while one was open for 6% -> 12% of each run, Pallas kernels for 2% -> 2%
where the time goes in v8:
time: 213 us; the launch traced here: 211 us
  waiting for transfers between devices  79.2 us (37%)
  blocking collectives  45.4 us (21%)
  starting transfers between devices  37.3 us (18%)
  local copies, waits for them, and re-layouts  19.3 us (9%)
  matrix products  15.7 us (7%)
  Pallas kernels  10.3 us (5%)
  other arithmetic  3.78 us (2%)
    all_to_all x1, blocking collectives, program(): nu = lax.all_to_all(copies, 'y', 0, 0, tiled=False)  27 us
    ppermute x15, waiting for transfers between devices, swap(): return lax.ppermute(x, axis, PAIR)  22.3 us
    all_to_all x2, waiting for transfers between devices, program(): lax.all_to_all((-result).astype(BF).reshape(4, 64, 2048), 'y', 0, 0, tile...  21.2 us
    all_to_all x1, blocking collectives, program(): terms = lax.all_to_all(two.reshape(8, 64, 512), Z, 0, 0, tiled=False)  18.4 us
    dot_general x8, matrix products, dot(): lax.dot_general(a, b, (((0,), (0,)), ((), ())), preferred_element_type=F32)  13.4 us
    ppermute x15, starting transfers between devices, swap(): return lax.ppermute(x, axis, PAIR)  12 us
    all_to_all x2, starting transfers between devices, program(): lax.all_to_all((-result).astype(BF).reshape(4, 64, 2048), 'y', 0, 0, tile...  10.3 us
    ppermute x4, waiting for transfers between devices, ring(): near.append(lax.ppermute(far[step - 1], Z, MATE))  9.32 us
  transfers between devices with their start and end apart: 27, of which 19 were waited for; matrix products, arithmetic and copies ran while one was open for 12% of the time, Pallas kernels for 2%

profile of v8, /device:TPU:8, one launch (start us, length us, event | category | flops | bytes accessed | tf_op | source)
XLA Modules:
  0.0 211.2 jit_solution(16012466218029852658)
XLA Ops:
  0.0 3.2 %collective-permute-start = (bf16[32,2048]{1,0:T(8,128)(2,1)}, bf16[32,2048]{1,0:T(8,128)(2,1)S(1)}, u32[]{:S(2)}, u32[]{:S(2)}) collective-permute-start(bf16[32,2048]{1,0:T(8,128)(2,1)} %bitcast.44), channel_id=1, source_target_pairs={{0,64},{1,65},{2,66},{3,67},{4,32},{5,33},{6,34},{7,35},{8,0},{9,1... | collective-permute-start | bytes 393224 | tf_op jit(solution)/shard_map/ppermute | solution.py:171
  3.2 0.8 fusion.17
  3.9 8.9 %collective-permute-done = bf16[32,2048]{1,0:T(8,128)(2,1)S(1)} collective-permute-done((bf16[32,2048]{1,0:T(8,128)(2,1)}, bf16[32,2048]{1,0:T(8,128)(2,1)S(1)}, u32[]{:S(2)}, u32[]{:S(2)}) %collective-permute-start) | collective-permute-done | bytes 131104 | tf_op jit(solution)/shard_map/ppermute | solution.py:171
  12.9 5.3 %collective-permute-start.2 = (bf16[32,2048]{1,0:T(8,128)(2,1)S(1)}, bf16[32,2048]{1,0:T(8,128)(2,1)S(1)}, u32[]{:S(2)}, u32[]{:S(2)}) collective-permute-start(bf16[32,2048]{1,0:T(8,128)(2,1)S(1)} %pad_maximum_fusion.3), channel_id=1, source_target_pairs={{0,128},{128,0},{1,129},{129,1},{2,130},{130,2},{3,131},{131,3},{4... | collective-permute-start | bytes 393224 | tf_op jit(solution)/shard_map/ppermute | solution.py:47
  18.2 1.6 collective-permute-start.3
  19.7 2.7 %collective-permute-done.1.pair_ref = bf16[32,1024]{1,0:T(8,128)(2,1)S(1)} collective-permute-done((bf16[32,1024]{1,0:T(8,128)(2,1)S(1)}, bf16[32,1024]{1,0:T(8,128)(2,1)S(1)}, u32[]{:S(2)}, u32[]{:S(2)}) %collective-permute-start.1) | collective-permute-done | bytes 65568 | tf_op jit(solution)/shard_map/ppermute | solution.py:47
  22.4 2.4 %collective-permute-done.3.both_ref = bf16[32,1024]{1,0:T(8,128)(2,1)S(1)} collective-permute-done((bf16[32,1024]{1,0:T(8,128)(2,1)S(1)}, bf16[32,1024]{1,0:T(8,128)(2,1)S(1)}, u32[]{:S(2)}, u32[]{:S(2)}) %collective-permute-start.3) | collective-permute-done | bytes 65568 | tf_op jit(solution)/shard_map/ppermute | solution.py:176
  24.9 0.6 copy-done.21
  25.5 0.7 copy-done.19
  26.1 2.3 %shard_map.46 = bf16[4,2,2,32,1536]{4,3,2,1,0:T(8,128)(2,1)} custom-call(bf16[32,1024]{1,0:T(8,128)(2,1)} %copy-done.12, bf16[32,1024]{1,0:T(8,128)(2,1)} %copy-done.20, bf16[32,2048]{1,0:T(8,128)(2,1)} %copy-done.19, bf16[32,1024]{1,0:T(8,128)(2,1)} %copy-done.21, bf16[64,512]{1,0:T(8,128)(2,1)} %bitcast.43), custom_call_target="tpu_custom_call" | custom-call | bytes 2097152 | tf_op jit(solution)/shard_map/pallas_call | solution.py:88
  28.4 27.0 %all_to_all.25.nu_a_ref = bf16[4,2,2,32,1536]{4,3,2,1,0:T(8,128)(2,1)S(1)} all-to-all(bf16[4,2,2,32,1536]{4,3,2,1,0:T(8,128)(2,1)} %shard_map.46), channel_id=1, replica_groups=mesh['xh'=2,'y'=4,'xl'=2,'zh'=4,'zl'=2,'core'=2] {'y'}, dimensions={0} | all-to-all | bytes 3145728 | tf_op jit(solution)/shard_map/all_to_all | solution.py:178
  55.5 0.6 collective-permute-start.5
  56.0 2.7 %constant_dynamic-slice_fusion.4 = (bf16[512,1024]{1,0:T(8,128)(2,1)}, bf16[512,1024]{1,0:T(8,128)(2,1)S(1)}) fusion(bf16[512,2048]{1,0:T(8,128)(2,1)} %param.5, s32[]{:T(128)S(6)} %select_n.29, s32[]{:T(128)S(6)} %select_n.28), kind=kLoop, calls=%fused_computation.39 | loop fusion | bytes 4194312 | tf_op jit(solution)/shard_map/dynamic_slice | solution.py:66
  58.7 0.2 collective-permute-done.5
  59.0 2.6 %collective-permute-start.7 = (bf16[64,1024]{1,0:T(8,128)(2,1)S(1)}, bf16[64,1024]{1,0:T(8,128)(2,1)S(1)}, u32[]{:S(2)}, u32[]{:S(2)}) collective-permute-start(bf16[64,1024]{1,0:T(8,128)(2,1)S(1)} %pad_maximum_fusion.4.refs_0_), channel_id=1, source_target_pairs={{0,14},{2,4},{4,2},{6,8},{8,6},{10,12},{12,10},{14,0},{1,15},{3,5}... | collective-permute-start | bytes 393224 | tf_op jit(solution)/shard_map/ppermute | solution.py:60
  61.6 4.3 %collective-permute-done.7.refs_7_ = bf16[64,1024]{1,0:T(8,128)(2,1)S(1)} collective-permute-done((bf16[64,1024]{1,0:T(8,128)(2,1)S(1)}, bf16[64,1024]{1,0:T(8,128)(2,1)S(1)}, u32[]{:S(2)}, u32[]{:S(2)}) %collective-permute-start.7) | collective-permute-done | bytes 131104 | tf_op jit(solution)/shard_map/ppermute | solution.py:60
  66.0 1.0 collective-permute-done.6.refs_1_
  67.0 1.5 collective-permute-start.9
  68.5 2.4 %collective-permute-done.8.refs_2_ = bf16[64,1024]{1,0:T(8,128)(2,1)S(1)} collective-permute-done((bf16[64,1024]{1,0:T(8,128)(2,1)S(1)}, bf16[64,1024]{1,0:T(8,128)(2,1)S(1)}, u32[]{:S(2)}, u32[]{:S(2)}) %collective-permute-start.8) | collective-permute-done | bytes 131104 | tf_op jit(solution)/shard_map/ppermute | solution.py:58
  70.9 2.5 %collective-permute-start.11 = (bf16[64,1024]{1,0:T(8,128)(2,1)S(1)}, bf16[64,1024]{1,0:T(8,128)(2,1)S(1)}, u32[]{:S(2)}, u32[]{:S(2)}) collective-permute-start(bf16[64,1024]{1,0:T(8,128)(2,1)S(1)} %collective-permute-done.8.refs_2_), channel_id=1, source_target_pairs={{0,14},{2,4},{4,2},{6,8},{8,6},{10,12},{12,10},{14,0},{1,15},{3,5}... | collective-permute-start | bytes 393224 | tf_op jit(solution)/shard_map/ppermute | solution.py:60
  73.7 3.4 %collective-permute-done.11.refs_5_ = bf16[64,1024]{1,0:T(8,128)(2,1)S(1)} collective-permute-done((bf16[64,1024]{1,0:T(8,128)(2,1)S(1)}, bf16[64,1024]{1,0:T(8,128)(2,1)S(1)}, u32[]{:S(2)}, u32[]{:S(2)}) %collective-permute-start.11) | collective-permute-done | bytes 131104 | tf_op jit(solution)/shard_map/ppermute | solution.py:60
  77.1 0.7 pad_maximum_fusion.1
  77.8 0.8 collective-permute-done.10.refs_3_
  78.6 1.9 collective-permute-start.15
  80.5 0.7 pad_maximum_fusion.2
  81.3 4.3 %collective-permute-done.13.refs_8_ = bf16[64,1024]{1,0:T(8,128)(2,1)S(1)} collective-permute-done((bf16[64,1024]{1,0:T(8,128)(2,1)S(1)}, bf16[64,1024]{1,0:T(8,128)(2,1)S(1)}, u32[]{:S(2)}, u32[]{:S(2)}) %collective-permute-start.13) | collective-permute-done | bytes 131104 | tf_op jit(solution)/shard_map/ppermute | solution.py:47
  85.5 0.7 copy-done.3
  86.2 0.7 copy-done
  86.9 5.1 %collective-permute-done.12.refs_4_ = bf16[64,1024]{1,0:T(8,128)(2,1)} collective-permute-done((bf16[64,1024]{1,0:T(8,128)(2,1)S(1)}, bf16[64,1024]{1,0:T(8,128)(2,1)}, u32[]{:S(2)}, u32[]{:S(2)}) %collective-permute-start.12) | collective-permute-done | bytes 131104 | tf_op jit(solution)/shard_map/ppermute | solution.py:58
  92.0 2.0 collective-permute-start.17
  94.1 1.3 collective-permute-done.16.refs_11_
  95.3 1.9 collective-permute-done.17.refs_12_
  97.3 0.9 copy-done.1
  98.2 0.9 copy-done.4
  99.1 4.0 %shard_map.48 = (bf16[1024,512]{1,0:T(8,128)(2,1)S(1)}, bf16[512,1024]{1,0:T(8,128)(2,1)S(1)}) custom-call(s32[5]{0:T(128)S(1)} %stack.35.place_ref, bf16[4,2,2,32,1536]{4,3,2,1,0:T(8,128)(2,1)S(1)} %all_to_all.25.nu_a_ref, bf16[4,2,2,32,1536]{4,3,2,1,0:T(8,128)(2,1)} %collective-permute-done.4.nu_b_ref, bf16[64,1024]{1,0:T(8,128)(2,1)S(1)} %pad_maximum_fusion.4.refs_0_, ...), custom_call_target="tpu_custom_call" | custom-call | flops 1073741824 | bytes 10485760 | tf_op jit(solution)/shard_map/pallas_call | solution.py:147
  103.2 1.6 convolution_convert_fusion
  104.7 2.0 collective-permute-start.19
  106.8 0.9 copy-done.2
  107.8 0.9 copy-done.5
  108.7 4.0 %shard_map.47 = bf16[1024,512]{1,0:T(8,128)(2,1)S(1)} custom-call(s32[5]{0:T(128)S(1)} %stack.33.place_ref, bf16[4,2,2,32,1536]{4,3,2,1,0:T(8,128)(2,1)S(1)} %all_to_all.25.nu_a_ref, bf16[4,2,2,32,1536]{4,3,2,1,0:T(8,128)(2,1)} %collective-permute-done.4.nu_b_ref, bf16[64,1024]{1,0:T(8,128)(2,1)S(1)} %pad_maximum_fusion.4.refs_0_, ...), custom_call_target="tpu_custom_call" | custom-call | flops 1073741824 | bytes 10485760 | tf_op jit(solution)/shard_map/pallas_call | solution.py:147
  112.7 0.8 fusion.18
  113.5 2.0 collective-permute-done.19
  115.5 1.2 add_convert_fusion
  116.7 18.4 %all_to_all.26 = bf16[8,64,512]{2,1,0:T(8,128)(2,1)S(1)} all-to-all(bf16[8,64,512]{2,1,0:T(8,128)(2,1)S(1)} %bitcast.41), channel_id=1, replica_groups=mesh['xh'=2,'y'=4,'xl'=2,'zh'=4,'zl'=2,'core'=2] {'zh','zl'}, dimensions={0} | all-to-all | bytes 1048576 | tf_op jit(solution)/shard_map/all_to_all | solution.py:208
  135.2 0.8 broadcast_in_dim.9
  136.0 3.5 %all-to-all-start.2 = ((bf16[8,64,512]{2,1,0:T(8,128)(2,1)}), bf16[8,64,512]{2,1,0:T(8,128)(2,1)S(1)}, u32[]{:S(2)}, u32[]{:S(2)}) async-start(bf16[8,64,512]{2,1,0:T(8,128)(2,1)} %broadcast_in_dim.9), calls=%async_computation.2 | async-start | bytes 1048576 | tf_op jit(solution)/shard_map/all_to_all | solution.py:52
  139.6 6.7 %constant_dynamic-slice_fusion = (bf16[512,2048]{1,0:T(8,128)(2,1)}, bf16[512,2048]{1,0:T(8,128)(2,1)S(1)}, bf16[512,2048]{1,0:T(8,128)(2,1)}, bf16[512,2048]{1,0:T(8,128)(2,1)}) fusion(bf16[2048,2048]{1,0:T(8,128)(2,1)} %param.7, s32[]{:T(128)S(6)} %select_n.33, s32[]{:T(128)S(6)} %select_n.31, s32[]{:T(128)S(6)} %select_n.30, s32[]{:T(128)S(6)} %select_n.32), kind=kLoop, calls=%fused_computation.35 | loop fusion | bytes 16777232 | tf_op jit(solution)/shard_map/dynamic_slice | solution.py:191
  146.2 7.2 %all-to-all-done.2 = bf16[8,64,512]{2,1,0:T(8,128)(2,1)S(1)} async-done(((bf16[8,64,512]{2,1,0:T(8,128)(2,1)}), bf16[8,64,512]{2,1,0:T(8,128)(2,1)S(1)}, u32[]{:S(2)}, u32[]{:S(2)}) %all-to-all-start.2) | async-done | bytes 524320 | tf_op jit(solution)/shard_map/all_to_all | solution.py:52
  153.5 3.8 %fusion.14 = f32[256,2048]{1,0:T(8,128)} fusion(bf16[512,2048]{1,0:T(8,128)(2,1)} %get-tuple-element.13, bf16[512,512]{1,0:T(8,128)(2,1)S(1)} %bitcast.39), kind=kOutput, calls=%fused_computation.24 | convolution fusion | flops 536870912 | bytes 4456448 | tf_op jit(solution)/shard_map/dot_general | solution.py:43
  157.3 0.7 fusion.9
  158.0 9.8 %collective-permute-done.21 = bf16[512,512]{1,0:T(8,128)(2,1)S(1)} collective-permute-done((bf16[512,512]{1,0:T(8,128)(2,1)S(1)}, bf16[512,512]{1,0:T(8,128)(2,1)S(1)}, u32[]{:S(2)}, u32[]{:S(2)}) %collective-permute-start.21) | collective-permute-done | bytes 524320 | tf_op jit(solution)/shard_map/ppermute | solution.py:47
  167.8 0.7 convolution_add_fusion.2
  168.8 0.8 convolution_add_fusion.1
  169.7 0.7 copy-done.9
  170.4 1.7 fusion.3
  172.1 5.4 %all-to-all-start.4 = ((bf16[4,64,2048]{2,1,0:T(8,128)(2,1)}), bf16[4,64,2048]{2,1,0:T(8,128)(2,1)S(1)}, u32[]{:S(2)}, u32[]{:S(2)}) async-start(bf16[4,64,2048]{2,1,0:T(8,128)(2,1)} %bitcast.36), calls=%async_computation.4 | async-start | bytes 2097152 | tf_op jit(solution)/shard_map/all_to_all | solution.py:220
  177.5 3.1 %convolution_add_fusion.5 = f32[256,2048]{1,0:T(8,128)S(1)} fusion(f32[256,2048]{1,0:T(8,128)} %fusion.14, bf16[512,2048]{1,0:T(8,128)(2,1)} %get-tuple-element.14, bf16[512,512]{1,0:T(8,128)(2,1)} %copy-done.13), kind=kOutput, calls=%fused_computation.7 | convolution fusion | flops 537395200 | bytes 6553600 | tf_op jit(solution)/shard_map/dot_general | solution.py:43
  180.6 0.8 convolution_add_fusion.4
  181.4 0.8 copy-done.10
  182.2 1.7 fusion.2
  184.0 7.9 %all-to-all-done.4 = bf16[4,64,2048]{2,1,0:T(8,128)(2,1)S(1)} async-done(((bf16[4,64,2048]{2,1,0:T(8,128)(2,1)}), bf16[4,64,2048]{2,1,0:T(8,128)(2,1)S(1)}, u32[]{:S(2)}, u32[]{:S(2)}) %all-to-all-start.4) | async-done | bytes 1048608 | tf_op jit(solution)/shard_map/all_to_all | solution.py:220
  191.9 4.9 %all-to-all-start.3 = ((bf16[4,64,2048]{2,1,0:T(8,128)(2,1)}), bf16[4,64,2048]{2,1,0:T(8,128)(2,1)S(1)}, u32[]{:S(2)}, u32[]{:S(2)}) async-start(bf16[4,64,2048]{2,1,0:T(8,128)(2,1)} %bitcast.13), calls=%async_computation.3 | async-start | bytes 2097152 | tf_op jit(solution)/shard_map/all_to_all | solution.py:220
  197.1 13.3 %all-to-all-done.3 = bf16[4,64,2048]{2,1,0:T(8,128)(2,1)S(1)} async-done(((bf16[4,64,2048]{2,1,0:T(8,128)(2,1)}), bf16[4,64,2048]{2,1,0:T(8,128)(2,1)S(1)}, u32[]{:S(2)}, u32[]{:S(2)}) %all-to-all-start.3) | async-done | bytes 1048608 | tf_op jit(solution)/shard_map/all_to_all | solution.py:220
  210.4 0.9 fusion.4
  (66 shorter events, 1.3 us)
Async XLA Ops:
  0.0 12.9 %collective-permute-start = (bf16[32,2048]{1,0:T(8,128)(2,1)}, bf16[32,2048]{1,0:T(8,128)(2,1)S(1)}, u32[]{:S(2)}, u32[]{:S(2)}) collective-permute-start(bf16[32,2048]{1,0:T(8,128)(2,1)} %bitcast.44), channel_id=1, source_target_pairs={{0,64},{1,65},{2,66},{3,67},{4,32},{5,33},{6,34},{7,35},{8,0},{9,1... | collective-permute-start | bytes 393224 | tf_op jit(solution)/shard_map/ppermute | solution.py:171
  12.9 12.0 %copy-start.12 = (bf16[32,1024]{1,0:T(8,128)(2,1)}, bf16[32,1024]{1,0:T(8,128)(2,1)S(1)}, u32[]{:S(2)}) copy-start(bf16[32,1024]{1,0:T(8,128)(2,1)S(1)} %get-tuple-element.26.ours_ref) | copy-start | bytes 196612
  12.9 11.9 %collective-permute-start.2 = (bf16[32,2048]{1,0:T(8,128)(2,1)S(1)}, bf16[32,2048]{1,0:T(8,128)(2,1)S(1)}, u32[]{:S(2)}, u32[]{:S(2)}) collective-permute-start(bf16[32,2048]{1,0:T(8,128)(2,1)S(1)} %pad_maximum_fusion.3), channel_id=1, source_target_pairs={{0,128},{128,0},{1,129},{129,1},{2,130},{130,2},{3,131},{131,3},{4... | collective-permute-start | bytes 393224 | tf_op jit(solution)/shard_map/ppermute | solution.py:47
  18.2 37.3 %copy-start.18 = (bf16[2048,32]{0,1:T(8,128)(2,1)S(1)}, bf16[2048,32]{0,1:T(8,128)(2,1)}, u32[]{:S(2)}) copy-start(bf16[2048,32]{0,1:T(8,128)(2,1)} %param.4) | copy-start | bytes 393220
  18.2 4.3 %collective-permute-start.1 = (bf16[32,1024]{1,0:T(8,128)(2,1)S(1)}, bf16[32,1024]{1,0:T(8,128)(2,1)S(1)}, u32[]{:S(2)}, u32[]{:S(2)}) collective-permute-start(bf16[32,1024]{1,0:T(8,128)(2,1)S(1)} %get-tuple-element.25), channel_id=1, source_target_pairs={{0,2},{2,0},{1,3},{3,1},{4,6},{6,4},{5,7},{7,5},{8,10},{10,8},{9,1... | collective-permute-start | bytes 196616 | tf_op jit(solution)/shard_map/ppermute | solution.py:47
  18.2 6.7 %collective-permute-start.3 = (bf16[32,1024]{1,0:T(8,128)(2,1)S(1)}, bf16[32,1024]{1,0:T(8,128)(2,1)S(1)}, u32[]{:S(2)}, u32[]{:S(2)}) collective-permute-start(bf16[32,1024]{1,0:T(8,128)(2,1)S(1)} %get-tuple-element.25), channel_id=1, source_target_pairs={{0,130},{2,128},{128,2},{130,0},{1,131},{3,129},{129,3},{131,1},{4... | collective-permute-start | bytes 196616 | tf_op jit(solution)/shard_map/ppermute | solution.py:176
  22.4 2.4 %copy-start.20 = (bf16[32,1024]{1,0:T(8,128)(2,1)}, bf16[32,1024]{1,0:T(8,128)(2,1)S(1)}, u32[]{:S(2)}) copy-start(bf16[32,1024]{1,0:T(8,128)(2,1)S(1)} %collective-permute-done.1.pair_ref) | copy-start | bytes 196612
  24.8 0.6 copy-start.21
  25.5 0.7 copy-start.19
  55.4 41.8 %collective-permute-start.4 = (bf16[4,2,2,32,1536]{4,3,2,1,0:T(8,128)(2,1)S(1)}, bf16[4,2,2,32,1536]{4,3,2,1,0:T(8,128)(2,1)}, u32[]{:S(2)}, u32[]{:S(2)}) collective-permute-start(bf16[4,2,2,32,1536]{4,3,2,1,0:T(8,128)(2,1)S(1)} %all_to_all.25.nu_a_ref), channel_id=1, source_target_pairs={{0,1},{1,0},{2,3},{3,2},{4,5},{5,4},{6,7},{7,6},{8,9},{9,8},{10,11... | collective-permute-start | bytes 4718600 | tf_op jit(solution)/shard_map/ppermute | solution.py:47
  55.5 3.5 %collective-permute-start.5 = (bf16[32,1024]{1,0:T(8,128)(2,1)S(1)}, bf16[32,1024]{1,0:T(8,128)(2,1)S(1)}, u32[]{:S(2)}, u32[]{:S(2)}) collective-permute-start(bf16[32,1024]{1,0:T(8,128)(2,1)S(1)} %get-tuple-element.24), channel_id=1, source_target_pairs={{0,1},{1,0},{2,3},{3,2},{4,5},{5,4},{6,7},{7,6},{8,9},{9,8},{10,11... | collective-permute-start | bytes 196616 | tf_op jit(solution)/shard_map/ppermute | solution.py:47
  58.7 38.5 %collective-permute-start.18 = (bf16[512,1024]{1,0:T(8,128)(2,1)}, bf16[512,1024]{1,0:T(8,128)(2,1)}, u32[]{:S(2)}, u32[]{:S(2)}) collective-permute-start(bf16[512,1024]{1,0:T(8,128)(2,1)} %get-tuple-element.21), channel_id=1, source_target_pairs={{0,1},{1,0},{2,3},{3,2},{4,5},{5,4},{6,7},{7,6},{8,9},{9,8},{10,11... | collective-permute-start | bytes 3145736 | tf_op jit(solution)/shard_map/ppermute | solution.py:47
  59.0 7.0 %collective-permute-start.7 = (bf16[64,1024]{1,0:T(8,128)(2,1)S(1)}, bf16[64,1024]{1,0:T(8,128)(2,1)S(1)}, u32[]{:S(2)}, u32[]{:S(2)}) collective-permute-start(bf16[64,1024]{1,0:T(8,128)(2,1)S(1)} %pad_maximum_fusion.4.refs_0_), channel_id=1, source_target_pairs={{0,14},{2,4},{4,2},{6,8},{8,6},{10,12},{12,10},{14,0},{1,15},{3,5}... | collective-permute-start | bytes 393224 | tf_op jit(solution)/shard_map/ppermute | solution.py:60
  61.6 5.4 %collective-permute-start.6 = (bf16[64,1024]{1,0:T(8,128)(2,1)S(1)}, bf16[64,1024]{1,0:T(8,128)(2,1)S(1)}, u32[]{:S(2)}, u32[]{:S(2)}) collective-permute-start(bf16[64,1024]{1,0:T(8,128)(2,1)S(1)} %pad_maximum_fusion.4.refs_0_), channel_id=1, source_target_pairs={{0,2},{2,0},{4,6},{6,4},{8,10},{10,8},{12,14},{14,12},{1,3},{3,1},... | collective-permute-start | bytes 393224 | tf_op jit(solution)/shard_map/ppermute | solution.py:58
  65.9 5.0 %collective-permute-start.8 = (bf16[64,1024]{1,0:T(8,128)(2,1)S(1)}, bf16[64,1024]{1,0:T(8,128)(2,1)S(1)}, u32[]{:S(2)}, u32[]{:S(2)}) collective-permute-start(bf16[64,1024]{1,0:T(8,128)(2,1)S(1)} %collective-permute-done.7.refs_7_), channel_id=1, source_target_pairs={{0,2},{2,0},{4,6},{6,4},{8,10},{10,8},{12,14},{14,12},{1,3},{3,1},... | collective-permute-start | bytes 393224 | tf_op jit(solution)/shard_map/ppermute | solution.py:58
  67.0 6.6 %collective-permute-start.9 = (bf16[64,1024]{1,0:T(8,128)(2,1)S(1)}, bf16[64,1024]{1,0:T(8,128)(2,1)S(1)}, u32[]{:S(2)}, u32[]{:S(2)}) collective-permute-start(bf16[64,1024]{1,0:T(8,128)(2,1)S(1)} %collective-permute-done.6.refs_1_), channel_id=1, source_target_pairs={{0,14},{2,4},{4,2},{6,8},{8,6},{10,12},{12,10},{14,0},{1,15},{3,5}... | collective-permute-start | bytes 393224 | tf_op jit(solution)/shard_map/ppermute | solution.py:60
  70.9 6.2 %collective-permute-start.11 = (bf16[64,1024]{1,0:T(8,128)(2,1)S(1)}, bf16[64,1024]{1,0:T(8,128)(2,1)S(1)}, u32[]{:S(2)}, u32[]{:S(2)}) collective-permute-start(bf16[64,1024]{1,0:T(8,128)(2,1)S(1)} %collective-permute-done.8.refs_2_), channel_id=1, source_target_pairs={{0,14},{2,4},{4,2},{6,8},{8,6},{10,12},{12,10},{14,0},{1,15},{3,5}... | collective-permute-start | bytes 393224 | tf_op jit(solution)/shard_map/ppermute | solution.py:60
  73.5 12.7 %collective-permute-start.14 = (bf16[128,1024]{1,0:T(8,128)(2,1)S(1)}, bf16[128,1024]{1,0:T(8,128)(2,1)S(1)}, u32[]{:S(2)}, u32[]{:S(2)}) collective-permute-start(bf16[128,1024]{1,0:T(8,128)(2,1)S(1)} %pad_maximum_fusion), channel_id=1, source_target_pairs={{0,16},{16,0},{1,17},{17,1},{2,18},{18,2},{3,19},{19,3},{4,20},{20... | collective-permute-start | bytes 786440 | tf_op jit(solution)/shard_map/ppermute | solution.py:47
  73.6 5.1 %collective-permute-start.10 = (bf16[64,1024]{1,0:T(8,128)(2,1)S(1)}, bf16[64,1024]{1,0:T(8,128)(2,1)S(1)}, u32[]{:S(2)}, u32[]{:S(2)}) collective-permute-start(bf16[64,1024]{1,0:T(8,128)(2,1)S(1)} %collective-permute-done.9.refs_6_), channel_id=1, source_target_pairs={{0,2},{2,0},{4,6},{6,4},{8,10},{10,8},{12,14},{14,12},{1,3},{3,1},... | collective-permute-start | bytes 393224 | tf_op jit(solution)/shard_map/ppermute | solution.py:58
  77.1 8.4 %collective-permute-start.13 = (bf16[64,1024]{1,0:T(8,128)(2,1)S(1)}, bf16[64,1024]{1,0:T(8,128)(2,1)S(1)}, u32[]{:S(2)}, u32[]{:S(2)}) collective-permute-start(bf16[64,1024]{1,0:T(8,128)(2,1)S(1)} %pad_maximum_fusion.4.refs_0_), channel_id=1, source_target_pairs={{0,16},{16,0},{1,17},{17,1},{2,18},{18,2},{3,19},{19,3},{4,20},{20... | collective-permute-start | bytes 393224 | tf_op jit(solution)/shard_map/ppermute | solution.py:47
  78.6 15.5 %collective-permute-start.15 = (bf16[128,1024]{1,0:T(8,128)(2,1)}, bf16[128,1024]{1,0:T(8,128)(2,1)}, u32[]{:S(2)}, u32[]{:S(2)}) collective-permute-start(bf16[128,1024]{1,0:T(8,128)(2,1)} %pad_maximum_fusion.1), channel_id=1, source_target_pairs={{0,16},{16,0},{1,17},{17,1},{2,18},{18,2},{3,19},{19,3},{4,20},{20... | collective-permute-start | bytes 786440 | tf_op jit(solution)/shard_map/ppermute | solution.py:47
  85.5 0.7 copy-start.3
  86.2 9.1 %collective-permute-start.16 = (bf16[128,1024]{1,0:T(8,128)(2,1)}, bf16[128,1024]{1,0:T(8,128)(2,1)}, u32[]{:S(2)}, u32[]{:S(2)}) collective-permute-start(bf16[128,1024]{1,0:T(8,128)(2,1)} %pad_maximum_fusion.2), channel_id=1, source_target_pairs={{0,16},{16,0},{1,17},{17,1},{2,18},{18,2},{3,19},{19,3},{4,20},{20... | collective-permute-start | bytes 786440 | tf_op jit(solution)/shard_map/ppermute | solution.py:47
  86.2 0.7 copy-start
  86.9 5.1 %collective-permute-start.12 = (bf16[64,1024]{1,0:T(8,128)(2,1)S(1)}, bf16[64,1024]{1,0:T(8,128)(2,1)}, u32[]{:S(2)}, u32[]{:S(2)}) collective-permute-start(bf16[64,1024]{1,0:T(8,128)(2,1)S(1)} %collective-permute-done.11.refs_5_), channel_id=1, source_target_pairs={{0,2},{2,0},{4,6},{6,4},{8,10},{10,8},{12,14},{14,12},{1,3},{3,1},... | collective-permute-start | bytes 393224 | tf_op jit(solution)/shard_map/ppermute | solution.py:58
  92.0 5.3 %collective-permute-start.17 = (bf16[64,1024]{1,0:T(8,128)(2,1)}, bf16[64,1024]{1,0:T(8,128)(2,1)}, u32[]{:S(2)}, u32[]{:S(2)}) collective-permute-start(bf16[64,1024]{1,0:T(8,128)(2,1)} %collective-permute-done.12.refs_4_), channel_id=1, source_target_pairs={{0,16},{16,0},{1,17},{17,1},{2,18},{18,2},{3,19},{19,3},{4,20},{20... | collective-permute-start | bytes 393224 | tf_op jit(solution)/shard_map/ppermute | solution.py:47
  97.3 1.0 copy-start.1
  98.2 0.9 copy-start.4
  103.2 3.6 %copy-start.6 = (bf16[512,1024]{1,0:T(8,128)(2,1)}, bf16[512,1024]{1,0:T(8,128)(2,1)S(1)}, u32[]{:S(2)}) copy-start(bf16[512,1024]{1,0:T(8,128)(2,1)S(1)} %get-tuple-element.11) | copy-start | bytes 3145732
  104.7 10.8 %collective-permute-start.19 = (bf16[512,512]{1,0:T(8,128)(2,1)}, bf16[512,512]{1,0:T(8,128)(2,1)}, u32[]{:S(2)}, u32[]{:S(2)}) collective-permute-start(bf16[512,512]{1,0:T(8,128)(2,1)} %convolution_convert_fusion), channel_id=1, source_target_pairs={{0,16},{16,0},{1,17},{17,1},{2,18},{18,2},{3,19},{19,3},{4,20},{20... | collective-permute-start | bytes 1572872 | tf_op jit(solution)/shard_map/ppermute | solution.py:47
  106.8 1.0 copy-start.2
  107.8 0.9 copy-start.5
  108.7 4.0 %copy-start.7 = (bf16[512,1024]{1,0:T(8,128)(2,1)S(1)}, bf16[512,1024]{1,0:T(8,128)(2,1)}, u32[]{:S(2)}) copy-start(bf16[512,1024]{1,0:T(8,128)(2,1)} %copy-done.6) | copy-start | bytes 3145732
  136.0 17.4 %all-to-all-start.2 = ((bf16[8,64,512]{2,1,0:T(8,128)(2,1)}), bf16[8,64,512]{2,1,0:T(8,128)(2,1)S(1)}, u32[]{:S(2)}, u32[]{:S(2)}) async-start(bf16[8,64,512]{2,1,0:T(8,128)(2,1)} %broadcast_in_dim.9), calls=%async_computation.2 | async-start | bytes 1048576 | tf_op jit(solution)/shard_map/all_to_all | solution.py:52
  153.5 3.8 %copy-start.11 = (bf16[512,2048]{1,0:T(8,128)(2,1)S(1)}, bf16[512,2048]{1,0:T(8,128)(2,1)}, u32[]{:S(2)}) copy-start(bf16[512,2048]{1,0:T(8,128)(2,1)} %get-tuple-element.13) | copy-start | bytes 6291460
  153.5 14.3 %collective-permute-start.20 = (bf16[512,512]{1,0:T(8,128)(2,1)S(1)}, bf16[512,512]{1,0:T(8,128)(2,1)S(1)}, u32[]{:S(2)}, u32[]{:S(2)}) collective-permute-start(bf16[512,512]{1,0:T(8,128)(2,1)S(1)} %bitcast.37), channel_id=1, source_target_pairs={{0,1},{1,0},{2,3},{3,2},{4,5},{5,4},{6,7},{7,6},{8,9},{9,8},{10,11... | collective-permute-start | bytes 1572872 | tf_op jit(solution)/shard_map/ppermute | solution.py:47
  153.5 14.3 %collective-permute-start.21 = (bf16[512,512]{1,0:T(8,128)(2,1)S(1)}, bf16[512,512]{1,0:T(8,128)(2,1)S(1)}, u32[]{:S(2)}, u32[]{:S(2)}) collective-permute-start(bf16[512,512]{1,0:T(8,128)(2,1)S(1)} %bitcast.38), channel_id=1, source_target_pairs={{0,16},{16,0},{1,17},{17,1},{2,18},{18,2},{3,19},{19,3},{4,20},{20... | collective-permute-start | bytes 1572872 | tf_op jit(solution)/shard_map/ppermute | solution.py:47
  157.3 10.5 %copy-start.8 = (bf16[512,2048]{1,0:T(8,128)(2,1)S(1)}, bf16[512,2048]{1,0:T(8,128)(2,1)}, u32[]{:S(2)}) copy-start(bf16[512,2048]{1,0:T(8,128)(2,1)} %get-tuple-element.14) | copy-start | bytes 6291460
  167.8 0.9 copy-start.14
  167.8 1.9 collective-permute-start.22
  167.8 1.0 copy-start.13
  168.8 1.6 copy-start.9
  170.4 1.7 copy-start.16
  172.1 19.8 %all-to-all-start.4 = ((bf16[4,64,2048]{2,1,0:T(8,128)(2,1)}), bf16[4,64,2048]{2,1,0:T(8,128)(2,1)S(1)}, u32[]{:S(2)}, u32[]{:S(2)}) async-start(bf16[4,64,2048]{2,1,0:T(8,128)(2,1)} %bitcast.36), calls=%async_computation.4 | async-start | bytes 2097152 | tf_op jit(solution)/shard_map/all_to_all | solution.py:220
  177.5 3.1 %copy-start.15 = (bf16[512,512]{1,0:T(8,128)(2,1)S(1)}, bf16[512,512]{1,0:T(8,128)(2,1)}, u32[]{:S(2)}) copy-start(bf16[512,512]{1,0:T(8,128)(2,1)} %copy-done.14) | copy-start | bytes 1572868
  180.6 1.6 copy-start.10
  180.6 1.7 copy-start.17
  191.9 18.5 %all-to-all-start.3 = ((bf16[4,64,2048]{2,1,0:T(8,128)(2,1)}), bf16[4,64,2048]{2,1,0:T(8,128)(2,1)S(1)}, u32[]{:S(2)}, u32[]{:S(2)}) async-start(bf16[4,64,2048]{2,1,0:T(8,128)(2,1)} %bitcast.13), calls=%async_computation.3 | async-start | bytes 2097152 | tf_op jit(solution)/shard_map/all_to_all | solution.py:220
  197.0 13.4 %collective-permute-start.23 = (bf16[64,2048]{1,0:T(8,128)(2,1)S(1)}, bf16[64,2048]{1,0:T(8,128)(2,1)S(1)}, u32[]{:S(2)}, u32[]{:S(2)}) collective-permute-start(bf16[64,2048]{1,0:T(8,128)(2,1)S(1)} %fusion.5), channel_id=1, source_target_pairs={{0,128},{128,0},{1,129},{129,1},{2,130},{130,2},{3,131},{131,3},{4... | collective-permute-start | bytes 786440 | tf_op jit(solution)/shard_map/ppermute | solution.py:47

commit v9 on v7

--- a/solution.py
+++ b/solution.py
@@ -47,6 +47,11 @@
     return lax.ppermute(x, axis, PAIR)
 
 
+def gather(x, axes, count):
+    copies = jnp.broadcast_to(x[None], (count,) + x.shape)
+    return lax.all_to_all(copies, axes, 0, 0, tiled=False)
+
+
 def ring(x):
     near, far = [x], [x]
     for step in range(1, 5):
@@ -87,22 +92,6 @@
         out_specs=vmem,
         cost_estimate=pl.CostEstimate(flops=0, bytes_accessed=2 << 20, transcendentals=0),
     )(ours, pair, over, both, applied)
-
-
-def round_and_fan(terms):
-    def body(terms_ref, out_ref):
-        value = total(terms_ref[...]).astype(BF)
-        for k in range(8):
-            out_ref[k] = value
-
-    vmem = pl.BlockSpec(memory_space=pltpu.VMEM)
-    return pl.pallas_call(
-        body,
-        out_shape=jax.ShapeDtypeStruct(terms.shape, BF),
-        in_specs=[vmem],
-        out_specs=vmem,
-        cost_estimate=pl.CostEstimate(flops=1 << 18, bytes_accessed=1 << 20, transcendentals=0),
-    )(terms)
 
 
 def weigh(places, nu_a, nu_b, near, away, own, other, first):
@@ -214,9 +203,10 @@
         )
 
     arrived = swap(project(far_half).astype(BF), "xl")
-    two = (project(own_half) + arrived.astype(F32)).astype(BF)
+    mine = lax.optimization_barrier(project(own_half))
+    two = (mine + arrived.astype(F32)).astype(BF)
     terms = lax.all_to_all(two.reshape(8, 64, 512), Z, 0, 0, tiled=False)
-    p0 = lax.all_to_all(round_and_fan(terms), Z, 0, 0, tiled=False).reshape(512, 512)
+    p0 = gather(total(terms).astype(BF), Z, 8).reshape(512, 512)
     p1 = swap(p0, "xl")
     p2 = swap(p0, "core")
     result = dot(p0, fits[0])

time: 210 us -> 208 us (level)
  transfers between devices with their start and end apart: 24 -> 24, of which waited for: 17 -> 17; matrix products, arithmetic and copies ran while one was open for 6% -> 7% of each run, Pallas kernels for 2% -> 2%
where the time goes in v9:
time: 208 us; the launch traced here: 206 us
  blocking collectives  76.9 us (37%)
  waiting for transfers between devices  64 us (31%)
  starting transfers between devices  28 us (13%)
  local copies, waits for them, and re-layouts  15.2 us (7%)
  Pallas kernels  10.3 us (5%)
  matrix products  7.71 us (4%)
  other arithmetic  3.79 us (2%)
    all_to_all x1, blocking collectives, program(): lax.all_to_all((-result).astype(BF).reshape(8, 64, 2048), ('y', 'xh'), 0,...  31.1 us
    all_to_all x1, blocking collectives, program(): nu = lax.all_to_all(copies, 'y', 0, 0, tiled=False)  27 us
    ppermute x14, waiting for transfers between devices, swap(): return lax.ppermute(x, axis, PAIR)  23.6 us
    all_to_all x1, blocking collectives, program(): terms = lax.all_to_all(two.reshape(8, 64, 512), Z, 0, 0, tiled=False)  18.7 us
    all_to_all x1, waiting for transfers between devices, gather(): return lax.all_to_all(copies, axes, 0, 0, tiled=False)  13.4 us
    ppermute x14, starting transfers between devices, swap(): return lax.ppermute(x, axis, PAIR)  10.5 us
    ppermute x4, waiting for transfers between devices, ring(): near.append(lax.ppermute(far[step - 1], Z, MATE))  9.79 us
    ppermute x1, waiting for transfers between devices, program(): rows = lax.ppermute(bands, NAMES, far_pairs())  8.93 us
  transfers between devices with their start and end apart: 24, of which 17 were waited for; matrix products, arithmetic and copies ran while one was open for 7% of the time, Pallas kernels for 2%

profile of v9, /device:TPU:8, one launch (start us, length us, event | category | flops | bytes accessed | tf_op | source)
XLA Modules:
  0.0 206.1 jit_solution(15203534624292871567)
XLA Ops:
  0.0 3.2 %collective-permute-start = (bf16[32,2048]{1,0:T(8,128)(2,1)}, bf16[32,2048]{1,0:T(8,128)(2,1)S(1)}, u32[]{:S(2)}, u32[]{:S(2)}) collective-permute-start(bf16[32,2048]{1,0:T(8,128)(2,1)} %bitcast.39), channel_id=1, source_target_pairs={{0,64},{1,65},{2,66},{3,67},{4,32},{5,33},{6,34},{7,35},{8,0},{9,1... | collective-permute-start | bytes 393224 | tf_op jit(solution)/shard_map/ppermute | solution.py:171
  3.2 0.8 fusion.2
  3.9 8.9 %collective-permute-done = bf16[32,2048]{1,0:T(8,128)(2,1)S(1)} collective-permute-done((bf16[32,2048]{1,0:T(8,128)(2,1)}, bf16[32,2048]{1,0:T(8,128)(2,1)S(1)}, u32[]{:S(2)}, u32[]{:S(2)}) %collective-permute-start) | collective-permute-done | bytes 131104 | tf_op jit(solution)/shard_map/ppermute | solution.py:171
  12.9 5.3 %collective-permute-start.2 = (bf16[32,2048]{1,0:T(8,128)(2,1)S(1)}, bf16[32,2048]{1,0:T(8,128)(2,1)S(1)}, u32[]{:S(2)}, u32[]{:S(2)}) collective-permute-start(bf16[32,2048]{1,0:T(8,128)(2,1)S(1)} %pad_maximum_fusion.3), channel_id=1, source_target_pairs={{0,128},{128,0},{1,129},{129,1},{2,130},{130,2},{3,131},{131,3},{4... | collective-permute-start | bytes 393224 | tf_op jit(solution)/shard_map/ppermute | solution.py:47
  18.2 1.6 collective-permute-start.3
  19.7 2.7 %collective-permute-done.1.pair_ref = bf16[32,1024]{1,0:T(8,128)(2,1)S(1)} collective-permute-done((bf16[32,1024]{1,0:T(8,128)(2,1)S(1)}, bf16[32,1024]{1,0:T(8,128)(2,1)S(1)}, u32[]{:S(2)}, u32[]{:S(2)}) %collective-permute-start.1) | collective-permute-done | bytes 65568 | tf_op jit(solution)/shard_map/ppermute | solution.py:47
  22.4 2.4 %collective-permute-done.3.both_ref = bf16[32,1024]{1,0:T(8,128)(2,1)S(1)} collective-permute-done((bf16[32,1024]{1,0:T(8,128)(2,1)S(1)}, bf16[32,1024]{1,0:T(8,128)(2,1)S(1)}, u32[]{:S(2)}, u32[]{:S(2)}) %collective-permute-start.3) | collective-permute-done | bytes 65568 | tf_op jit(solution)/shard_map/ppermute | solution.py:176
  24.9 0.6 copy-done.12
  25.5 0.7 copy-done.10
  26.1 2.3 %shard_map.46 = bf16[4,2,2,32,1536]{4,3,2,1,0:T(8,128)(2,1)} custom-call(bf16[32,1024]{1,0:T(8,128)(2,1)} %copy-done.8, bf16[32,1024]{1,0:T(8,128)(2,1)} %copy-done.11, bf16[32,2048]{1,0:T(8,128)(2,1)} %copy-done.10, bf16[32,1024]{1,0:T(8,128)(2,1)} %copy-done.12, bf16[64,512]{1,0:T(8,128)(2,1)} %bitcast.38), custom_call_target="tpu_custom_call" | custom-call | bytes 2097152 | tf_op jit(solution)/shard_map/pallas_call | solution.py:88
  28.4 27.0 %all_to_all.20.nu_a_ref = bf16[4,2,2,32,1536]{4,3,2,1,0:T(8,128)(2,1)S(1)} all-to-all(bf16[4,2,2,32,1536]{4,3,2,1,0:T(8,128)(2,1)} %shard_map.46), channel_id=1, replica_groups=mesh['xh'=2,'y'=4,'xl'=2,'zh'=4,'zl'=2,'core'=2] {'y'}, dimensions={0} | all-to-all | bytes 3145728 | tf_op jit(solution)/shard_map/all_to_all | solution.py:178
  55.5 0.6 collective-permute-start.5
  56.1 2.7 %constant_dynamic-slice_fusion.4 = (bf16[512,1024]{1,0:T(8,128)(2,1)}, bf16[512,1024]{1,0:T(8,128)(2,1)S(1)}) fusion(bf16[512,2048]{1,0:T(8,128)(2,1)} %param.5, s32[]{:T(128)S(6)} %select_n.29, s32[]{:T(128)S(6)} %select_n.28), kind=kLoop, calls=%fused_computation.19 | loop fusion | bytes 4194312 | tf_op jit(solution)/shard_map/dynamic_slice | solution.py:66
  58.8 0.0 collective-permute-start.18
  58.8 0.2 collective-permute-done.5
  59.0 0.4 collective-permute-start.6
  59.4 2.5 %collective-permute-start.7 = (bf16[64,1024]{1,0:T(8,128)(2,1)S(1)}, bf16[64,1024]{1,0:T(8,128)(2,1)S(1)}, u32[]{:S(2)}, u32[]{:S(2)}) collective-permute-start(bf16[64,1024]{1,0:T(8,128)(2,1)S(1)} %pad_maximum_fusion.4.refs_0_), channel_id=1, source_target_pairs={{0,14},{2,4},{4,2},{6,8},{8,6},{10,12},{12,10},{14,0},{1,15},{3,5}... | collective-permute-start | bytes 393224 | tf_op jit(solution)/shard_map/ppermute | solution.py:60
  61.9 2.9 %collective-permute-done.6.refs_1_ = bf16[64,1024]{1,0:T(8,128)(2,1)S(1)} collective-permute-done((bf16[64,1024]{1,0:T(8,128)(2,1)S(1)}, bf16[64,1024]{1,0:T(8,128)(2,1)S(1)}, u32[]{:S(2)}, u32[]{:S(2)}) %collective-permute-start.6) | collective-permute-done | bytes 131104 | tf_op jit(solution)/shard_map/ppermute | solution.py:58
  64.8 2.5 %collective-permute-start.9 = (bf16[64,1024]{1,0:T(8,128)(2,1)S(1)}, bf16[64,1024]{1,0:T(8,128)(2,1)S(1)}, u32[]{:S(2)}, u32[]{:S(2)}) collective-permute-start(bf16[64,1024]{1,0:T(8,128)(2,1)S(1)} %collective-permute-done.6.refs_1_), channel_id=1, source_target_pairs={{0,14},{2,4},{4,2},{6,8},{8,6},{10,12},{12,10},{14,0},{1,15},{3,5}... | collective-permute-start | bytes 393224 | tf_op jit(solution)/shard_map/ppermute | solution.py:60
  67.3 3.7 %collective-permute-done.9.refs_6_ = bf16[64,1024]{1,0:T(8,128)(2,1)S(1)} collective-permute-done((bf16[64,1024]{1,0:T(8,128)(2,1)S(1)}, bf16[64,1024]{1,0:T(8,128)(2,1)S(1)}, u32[]{:S(2)}, u32[]{:S(2)}) %collective-permute-start.9) | collective-permute-done | bytes 131104 | tf_op jit(solution)/shard_map/ppermute | solution.py:60
  71.0 0.1 collective-permute-start.14
  71.1 1.6 collective-permute-done.8.refs_2_
  72.7 1.0 collective-permute-start.11
  73.7 2.2 %collective-permute-done.10.refs_3_ = bf16[64,1024]{1,0:T(8,128)(2,1)S(1)} collective-permute-done((bf16[64,1024]{1,0:T(8,128)(2,1)S(1)}, bf16[64,1024]{1,0:T(8,128)(2,1)S(1)}, u32[]{:S(2)}, u32[]{:S(2)}) %collective-permute-start.10) | collective-permute-done | bytes 131104 | tf_op jit(solution)/shard_map/ppermute | solution.py:58
  75.9 0.7 pad_maximum_fusion.1
  76.7 2.2 %collective-permute-done.11.refs_5_ = bf16[64,1024]{1,0:T(8,128)(2,1)S(1)} collective-permute-done((bf16[64,1024]{1,0:T(8,128)(2,1)S(1)}, bf16[64,1024]{1,0:T(8,128)(2,1)S(1)}, u32[]{:S(2)}, u32[]{:S(2)}) %collective-permute-start.11) | collective-permute-done | bytes 131104 | tf_op jit(solution)/shard_map/ppermute | solution.py:60
  78.9 0.4 collective-permute-start.15
  79.3 0.7 pad_maximum_fusion.2
  80.0 2.3 %collective-permute-done.13.refs_8_ = bf16[64,1024]{1,0:T(8,128)(2,1)S(1)} collective-permute-done((bf16[64,1024]{1,0:T(8,128)(2,1)S(1)}, bf16[64,1024]{1,0:T(8,128)(2,1)S(1)}, u32[]{:S(2)}, u32[]{:S(2)}) %collective-permute-start.13) | collective-permute-done | bytes 131104 | tf_op jit(solution)/shard_map/ppermute | solution.py:47
  82.3 0.6 copy-done.3
  83.0 0.7 copy-done
  83.7 2.8 %collective-permute-start.12 = (bf16[64,1024]{1,0:T(8,128)(2,1)S(1)}, bf16[64,1024]{1,0:T(8,128)(2,1)}, u32[]{:S(2)}, u32[]{:S(2)}) collective-permute-start(bf16[64,1024]{1,0:T(8,128)(2,1)S(1)} %collective-permute-done.11.refs_5_), channel_id=1, source_target_pairs={{0,2},{2,0},{4,6},{6,4},{8,10},{10,8},{12,14},{14,12},{1,3},{3,1},... | collective-permute-start | bytes 393224 | tf_op jit(solution)/shard_map/ppermute | solution.py:58
  86.4 3.0 %collective-permute-done.12.refs_4_ = bf16[64,1024]{1,0:T(8,128)(2,1)} collective-permute-done((bf16[64,1024]{1,0:T(8,128)(2,1)S(1)}, bf16[64,1024]{1,0:T(8,128)(2,1)}, u32[]{:S(2)}, u32[]{:S(2)}) %collective-permute-start.12) | collective-permute-done | bytes 131104 | tf_op jit(solution)/shard_map/ppermute | solution.py:58
  89.5 2.0 collective-permute-start.17
  91.5 0.1 stack.40.place_ref
  91.6 1.5 collective-permute-done.16.refs_11_
  93.1 1.6 collective-permute-done.17.refs_12_
  94.8 0.9 copy-done.1
  95.7 0.9 copy-done.4
  96.6 4.0 %shard_map.48 = (bf16[1024,512]{1,0:T(8,128)(2,1)S(1)}, bf16[512,1024]{1,0:T(8,128)(2,1)S(1)}) custom-call(s32[6]{0:T(128)S(1)} %stack.40.place_ref, bf16[4,2,2,32,1536]{4,3,2,1,0:T(8,128)(2,1)S(1)} %all_to_all.20.nu_a_ref, bf16[4,2,2,32,1536]{4,3,2,1,0:T(8,128)(2,1)} %collective-permute-done.4.nu_b_ref, bf16[64,1024]{1,0:T(8,128)(2,1)S(1)} %pad_maximum_fusion.4.refs_0_, ...), custom_call_target="tpu_custom_call" | custom-call | flops 1073741824 | bytes 10485760 | tf_op jit(solution)/shard_map/pallas_call | solution.py:147
  100.7 1.6 convolution_convert_fusion
  102.2 2.0 collective-permute-start.19
  104.3 0.1 stack.38.place_ref
  104.4 1.0 copy-done.2
  105.3 0.9 copy-done.5
  106.2 4.0 %shard_map.47 = bf16[1024,512]{1,0:T(8,128)(2,1)S(1)} custom-call(s32[6]{0:T(128)S(1)} %stack.38.place_ref, bf16[4,2,2,32,1536]{4,3,2,1,0:T(8,128)(2,1)S(1)} %all_to_all.20.nu_a_ref, bf16[4,2,2,32,1536]{4,3,2,1,0:T(8,128)(2,1)} %collective-permute-done.4.nu_b_ref, bf16[64,1024]{1,0:T(8,128)(2,1)S(1)} %pad_maximum_fusion.4.refs_0_, ...), custom_call_target="tpu_custom_call" | custom-call | flops 1073741824 | bytes 10485760 | tf_op jit(solution)/shard_map/pallas_call | solution.py:147
  110.3 0.8 fusion.3
  111.0 3.0 %collective-permute-done.19 = bf16[512,512]{1,0:T(8,128)(2,1)} collective-permute-done((bf16[512,512]{1,0:T(8,128)(2,1)}, bf16[512,512]{1,0:T(8,128)(2,1)}, u32[]{:S(2)}, u32[]{:S(2)}) %collective-permute-start.19) | collective-permute-done | bytes 524320 | tf_op jit(solution)/shard_map/ppermute | solution.py:47
  114.0 1.2 add_convert_fusion
  115.2 18.7 %all_to_all.21 = bf16[8,64,512]{2,1,0:T(8,128)(2,1)S(1)} all-to-all(bf16[8,64,512]{2,1,0:T(8,128)(2,1)S(1)} %bitcast.33), channel_id=1, replica_groups=mesh['xh'=2,'y'=4,'xl'=2,'zh'=4,'zl'=2,'core'=2] {'zh','zl'}, dimensions={0} | all-to-all | bytes 1048576 | tf_op jit(solution)/shard_map/all_to_all | solution.py:208
  133.9 0.1 fusion.1
  134.0 0.8 broadcast_in_dim.9
  134.8 3.5 %all-to-all-start.2 = ((bf16[8,64,512]{2,1,0:T(8,128)(2,1)}), bf16[8,64,512]{2,1,0:T(8,128)(2,1)S(1)}, u32[]{:S(2)}, u32[]{:S(2)}) async-start(bf16[8,64,512]{2,1,0:T(8,128)(2,1)} %broadcast_in_dim.9), calls=%async_computation.2 | async-start | bytes 1048576 | tf_op jit(solution)/shard_map/all_to_all | solution.py:52
  138.3 13.4 %all-to-all-done.2 = bf16[8,64,512]{2,1,0:T(8,128)(2,1)S(1)} async-done(((bf16[8,64,512]{2,1,0:T(8,128)(2,1)}), bf16[8,64,512]{2,1,0:T(8,128)(2,1)S(1)}, u32[]{:S(2)}, u32[]{:S(2)}) %all-to-all-start.2) | async-done | bytes 524320 | tf_op jit(solution)/shard_map/all_to_all | solution.py:52
  151.8 4.3 %constant_dynamic-slice_fusion = (bf16[512,2048]{1,0:T(8,128)(2,1)S(1)}, bf16[512,2048]{1,0:T(8,128)(2,1)S(1)}, bf16[512,2048]{1,0:T(8,128)(2,1)S(1)}, bf16[512,2048]{1,0:T(8,128)(2,1)S(1)}) fusion(bf16[2048,2048]{1,0:T(8,128)(2,1)} %param.7, s32[]{:T(128)S(6)} %select_n.33, s32[]{:T(128)S(6)} %select_n.31, s32[]{:T(128)S(6)} %select_n.30, s32[]{:T(128)S(6)} %select_n.32), kind=kLoop, calls=%fused_computation.15 | loop fusion | bytes 16777232 | tf_op jit(solution)/shard_map/dynamic_slice | solution.py:191
  156.1 0.1 collective-permute-start.20
  156.2 1.3 fusion.4
  157.5 1.4 convolution_add_fusion
  158.8 11.7 %collective-permute-done.20 = bf16[512,512]{1,0:T(8,128)(2,1)S(1)} collective-permute-done((bf16[512,512]{1,0:T(8,128)(2,1)S(1)}, bf16[512,512]{1,0:T(8,128)(2,1)S(1)}, u32[]{:S(2)}, u32[]{:S(2)}) %collective-permute-start.20) | collective-permute-done | bytes 524320 | tf_op jit(solution)/shard_map/ppermute | solution.py:47
  170.5 1.3 fusion.5
  171.8 0.6 collective-permute-done.22
  172.4 1.5 negate_convert_fusion
  173.9 31.1 %all_to_all.22 = bf16[8,64,2048]{2,1,0:T(8,128)(2,1)S(1)} all-to-all(bf16[8,64,2048]{2,1,0:T(8,128)(2,1)S(1)} %bitcast.32), channel_id=1, replica_groups=mesh['xh'=2,'y'=4,'xl'=2,'zh'=4,'zl'=2,'core'=2] {'y','xh'}, dimensions={0} | all-to-all | bytes 4194304 | tf_op jit(solution)/shard_map/all_to_all | solution.py:218
  205.0 1.0 fusion
  (38 shorter events, 0.1 us)
Async XLA Ops:
  0.0 12.9 %collective-permute-start = (bf16[32,2048]{1,0:T(8,128)(2,1)}, bf16[32,2048]{1,0:T(8,128)(2,1)S(1)}, u32[]{:S(2)}, u32[]{:S(2)}) collective-permute-start(bf16[32,2048]{1,0:T(8,128)(2,1)} %bitcast.39), channel_id=1, source_target_pairs={{0,64},{1,65},{2,66},{3,67},{4,32},{5,33},{6,34},{7,35},{8,0},{9,1... | collective-permute-start | bytes 393224 | tf_op jit(solution)/shard_map/ppermute | solution.py:171
  12.9 12.0 %copy-start.8 = (bf16[32,1024]{1,0:T(8,128)(2,1)}, bf16[32,1024]{1,0:T(8,128)(2,1)S(1)}, u32[]{:S(2)}) copy-start(bf16[32,1024]{1,0:T(8,128)(2,1)S(1)} %get-tuple-element.30.ours_ref) | copy-start | bytes 196612
  12.9 11.9 %collective-permute-start.2 = (bf16[32,2048]{1,0:T(8,128)(2,1)S(1)}, bf16[32,2048]{1,0:T(8,128)(2,1)S(1)}, u32[]{:S(2)}, u32[]{:S(2)}) collective-permute-start(bf16[32,2048]{1,0:T(8,128)(2,1)S(1)} %pad_maximum_fusion.3), channel_id=1, source_target_pairs={{0,128},{128,0},{1,129},{129,1},{2,130},{130,2},{3,131},{131,3},{4... | collective-permute-start | bytes 393224 | tf_op jit(solution)/shard_map/ppermute | solution.py:47
  18.2 37.3 %copy-start.9 = (bf16[2048,32]{0,1:T(8,128)(2,1)S(1)}, bf16[2048,32]{0,1:T(8,128)(2,1)}, u32[]{:S(2)}) copy-start(bf16[2048,32]{0,1:T(8,128)(2,1)} %param.4) | copy-start | bytes 393220
  18.2 4.3 %collective-permute-start.1 = (bf16[32,1024]{1,0:T(8,128)(2,1)S(1)}, bf16[32,1024]{1,0:T(8,128)(2,1)S(1)}, u32[]{:S(2)}, u32[]{:S(2)}) collective-permute-start(bf16[32,1024]{1,0:T(8,128)(2,1)S(1)} %get-tuple-element.29), channel_id=1, source_target_pairs={{0,2},{2,0},{1,3},{3,1},{4,6},{6,4},{5,7},{7,5},{8,10},{10,8},{9,1... | collective-permute-start | bytes 196616 | tf_op jit(solution)/shard_map/ppermute | solution.py:47
  18.2 6.7 %collective-permute-start.3 = (bf16[32,1024]{1,0:T(8,128)(2,1)S(1)}, bf16[32,1024]{1,0:T(8,128)(2,1)S(1)}, u32[]{:S(2)}, u32[]{:S(2)}) collective-permute-start(bf16[32,1024]{1,0:T(8,128)(2,1)S(1)} %get-tuple-element.29), channel_id=1, source_target_pairs={{0,130},{2,128},{128,2},{130,0},{1,131},{3,129},{129,3},{131,1},{4... | collective-permute-start | bytes 196616 | tf_op jit(solution)/shard_map/ppermute | solution.py:176
  22.4 2.4 %copy-start.11 = (bf16[32,1024]{1,0:T(8,128)(2,1)}, bf16[32,1024]{1,0:T(8,128)(2,1)S(1)}, u32[]{:S(2)}) copy-start(bf16[32,1024]{1,0:T(8,128)(2,1)S(1)} %collective-permute-done.1.pair_ref) | copy-start | bytes 196612
  24.8 0.6 copy-start.12
  25.5 0.7 copy-start.10
  55.4 39.3 %collective-permute-start.4 = (bf16[4,2,2,32,1536]{4,3,2,1,0:T(8,128)(2,1)S(1)}, bf16[4,2,2,32,1536]{4,3,2,1,0:T(8,128)(2,1)}, u32[]{:S(2)}, u32[]{:S(2)}) collective-permute-start(bf16[4,2,2,32,1536]{4,3,2,1,0:T(8,128)(2,1)S(1)} %all_to_all.20.nu_a_ref), channel_id=1, source_target_pairs={{0,1},{1,0},{2,3},{3,2},{4,5},{5,4},{6,7},{7,6},{8,9},{9,8},{10,11... | collective-permute-start | bytes 4718600 | tf_op jit(solution)/shard_map/ppermute | solution.py:47
  55.5 3.5 %collective-permute-start.5 = (bf16[32,1024]{1,0:T(8,128)(2,1)S(1)}, bf16[32,1024]{1,0:T(8,128)(2,1)S(1)}, u32[]{:S(2)}, u32[]{:S(2)}) collective-permute-start(bf16[32,1024]{1,0:T(8,128)(2,1)S(1)} %get-tuple-element.28), channel_id=1, source_target_pairs={{0,1},{1,0},{2,3},{3,2},{4,5},{5,4},{6,7},{7,6},{8,9},{9,8},{10,11... | collective-permute-start | bytes 196616 | tf_op jit(solution)/shard_map/ppermute | solution.py:47
  58.8 36.0 %collective-permute-start.18 = (bf16[512,1024]{1,0:T(8,128)(2,1)}, bf16[512,1024]{1,0:T(8,128)(2,1)}, u32[]{:S(2)}, u32[]{:S(2)}) collective-permute-start(bf16[512,1024]{1,0:T(8,128)(2,1)} %get-tuple-element.25), channel_id=1, source_target_pairs={{0,1},{1,0},{2,3},{3,2},{4,5},{5,4},{6,7},{7,6},{8,9},{9,8},{10,11... | collective-permute-start | bytes 3145736 | tf_op jit(solution)/shard_map/ppermute | solution.py:47
  59.0 5.8 %collective-permute-start.6 = (bf16[64,1024]{1,0:T(8,128)(2,1)S(1)}, bf16[64,1024]{1,0:T(8,128)(2,1)S(1)}, u32[]{:S(2)}, u32[]{:S(2)}) collective-permute-start(bf16[64,1024]{1,0:T(8,128)(2,1)S(1)} %pad_maximum_fusion.4.refs_0_), channel_id=1, source_target_pairs={{0,2},{2,0},{4,6},{6,4},{8,10},{10,8},{12,14},{14,12},{1,3},{3,1},... | collective-permute-start | bytes 393224 | tf_op jit(solution)/shard_map/ppermute | solution.py:58
  59.4 7.9 %collective-permute-start.7 = (bf16[64,1024]{1,0:T(8,128)(2,1)S(1)}, bf16[64,1024]{1,0:T(8,128)(2,1)S(1)}, u32[]{:S(2)}, u32[]{:S(2)}) collective-permute-start(bf16[64,1024]{1,0:T(8,128)(2,1)S(1)} %pad_maximum_fusion.4.refs_0_), channel_id=1, source_target_pairs={{0,14},{2,4},{4,2},{6,8},{8,6},{10,12},{12,10},{14,0},{1,15},{3,5}... | collective-permute-start | bytes 393224 | tf_op jit(solution)/shard_map/ppermute | solution.py:60
  64.8 6.2 %collective-permute-start.9 = (bf16[64,1024]{1,0:T(8,128)(2,1)S(1)}, bf16[64,1024]{1,0:T(8,128)(2,1)S(1)}, u32[]{:S(2)}, u32[]{:S(2)}) collective-permute-start(bf16[64,1024]{1,0:T(8,128)(2,1)S(1)} %collective-permute-done.6.refs_1_), channel_id=1, source_target_pairs={{0,14},{2,4},{4,2},{6,8},{8,6},{10,12},{12,10},{14,0},{1,15},{3,5}... | collective-permute-start | bytes 393224 | tf_op jit(solution)/shard_map/ppermute | solution.py:60
  67.3 5.4 %collective-permute-start.8 = (bf16[64,1024]{1,0:T(8,128)(2,1)S(1)}, bf16[64,1024]{1,0:T(8,128)(2,1)S(1)}, u32[]{:S(2)}, u32[]{:S(2)}) collective-permute-start(bf16[64,1024]{1,0:T(8,128)(2,1)S(1)} %collective-permute-done.7.refs_7_), channel_id=1, source_target_pairs={{0,2},{2,0},{4,6},{6,4},{8,10},{10,8},{12,14},{14,12},{1,3},{3,1},... | collective-permute-start | bytes 393224 | tf_op jit(solution)/shard_map/ppermute | solution.py:58
  71.0 5.0 %collective-permute-start.10 = (bf16[64,1024]{1,0:T(8,128)(2,1)S(1)}, bf16[64,1024]{1,0:T(8,128)(2,1)S(1)}, u32[]{:S(2)}, u32[]{:S(2)}) collective-permute-start(bf16[64,1024]{1,0:T(8,128)(2,1)S(1)} %collective-permute-done.9.refs_6_), channel_id=1, source_target_pairs={{0,2},{2,0},{4,6},{6,4},{8,10},{10,8},{12,14},{14,12},{1,3},{3,1},... | collective-permute-start | bytes 393224 | tf_op jit(solution)/shard_map/ppermute | solution.py:58
  71.0 12.0 %collective-permute-start.14 = (bf16[128,1024]{1,0:T(8,128)(2,1)S(1)}, bf16[128,1024]{1,0:T(8,128)(2,1)S(1)}, u32[]{:S(2)}, u32[]{:S(2)}) collective-permute-start(bf16[128,1024]{1,0:T(8,128)(2,1)S(1)} %pad_maximum_fusion), channel_id=1, source_target_pairs={{0,16},{16,0},{1,17},{17,1},{2,18},{18,2},{3,19},{19,3},{4,20},{20... | collective-permute-start | bytes 786440 | tf_op jit(solution)/shard_map/ppermute | solution.py:47
  72.7 6.2 %collective-permute-start.11 = (bf16[64,1024]{1,0:T(8,128)(2,1)S(1)}, bf16[64,1024]{1,0:T(8,128)(2,1)S(1)}, u32[]{:S(2)}, u32[]{:S(2)}) collective-permute-start(bf16[64,1024]{1,0:T(8,128)(2,1)S(1)} %collective-permute-done.8.refs_2_), channel_id=1, source_target_pairs={{0,14},{2,4},{4,2},{6,8},{8,6},{10,12},{12,10},{14,0},{1,15},{3,5}... | collective-permute-start | bytes 393224 | tf_op jit(solution)/shard_map/ppermute | solution.py:60
  75.9 6.4 %collective-permute-start.13 = (bf16[64,1024]{1,0:T(8,128)(2,1)S(1)}, bf16[64,1024]{1,0:T(8,128)(2,1)S(1)}, u32[]{:S(2)}, u32[]{:S(2)}) collective-permute-start(bf16[64,1024]{1,0:T(8,128)(2,1)S(1)} %pad_maximum_fusion.4.refs_0_), channel_id=1, source_target_pairs={{0,16},{16,0},{1,17},{17,1},{2,18},{18,2},{3,19},{19,3},{4,20},{20... | collective-permute-start | bytes 393224 | tf_op jit(solution)/shard_map/ppermute | solution.py:47
  78.9 12.7 %collective-permute-start.15 = (bf16[128,1024]{1,0:T(8,128)(2,1)}, bf16[128,1024]{1,0:T(8,128)(2,1)}, u32[]{:S(2)}, u32[]{:S(2)}) collective-permute-start(bf16[128,1024]{1,0:T(8,128)(2,1)} %pad_maximum_fusion.1), channel_id=1, source_target_pairs={{0,16},{16,0},{1,17},{17,1},{2,18},{18,2},{3,19},{19,3},{4,20},{20... | collective-permute-start | bytes 786440 | tf_op jit(solution)/shard_map/ppermute | solution.py:47
  82.3 0.7 copy-start.3
  83.0 10.2 %collective-permute-start.16 = (bf16[128,1024]{1,0:T(8,128)(2,1)}, bf16[128,1024]{1,0:T(8,128)(2,1)}, u32[]{:S(2)}, u32[]{:S(2)}) collective-permute-start(bf16[128,1024]{1,0:T(8,128)(2,1)} %pad_maximum_fusion.2), channel_id=1, source_target_pairs={{0,16},{16,0},{1,17},{17,1},{2,18},{18,2},{3,19},{19,3},{4,20},{20... | collective-permute-start | bytes 786440 | tf_op jit(solution)/shard_map/ppermute | solution.py:47
  83.0 0.7 copy-start
  83.7 5.8 %collective-permute-start.12 = (bf16[64,1024]{1,0:T(8,128)(2,1)S(1)}, bf16[64,1024]{1,0:T(8,128)(2,1)}, u32[]{:S(2)}, u32[]{:S(2)}) collective-permute-start(bf16[64,1024]{1,0:T(8,128)(2,1)S(1)} %collective-permute-done.11.refs_5_), channel_id=1, source_target_pairs={{0,2},{2,0},{4,6},{6,4},{8,10},{10,8},{12,14},{14,12},{1,3},{3,1},... | collective-permute-start | bytes 393224 | tf_op jit(solution)/shard_map/ppermute | solution.py:58
  89.5 5.3 %collective-permute-start.17 = (bf16[64,1024]{1,0:T(8,128)(2,1)}, bf16[64,1024]{1,0:T(8,128)(2,1)}, u32[]{:S(2)}, u32[]{:S(2)}) collective-permute-start(bf16[64,1024]{1,0:T(8,128)(2,1)} %collective-permute-done.12.refs_4_), channel_id=1, source_target_pairs={{0,16},{16,0},{1,17},{17,1},{2,18},{18,2},{3,19},{19,3},{4,20},{20... | collective-permute-start | bytes 393224 | tf_op jit(solution)/shard_map/ppermute | solution.py:47
  94.8 1.0 copy-start.1
  95.7 0.9 copy-start.4
  100.7 3.6 %copy-start.6 = (bf16[512,1024]{1,0:T(8,128)(2,1)}, bf16[512,1024]{1,0:T(8,128)(2,1)S(1)}, u32[]{:S(2)}) copy-start(bf16[512,1024]{1,0:T(8,128)(2,1)S(1)} %get-tuple-element.13) | copy-start | bytes 3145732
  102.2 11.7 %collective-permute-start.19 = (bf16[512,512]{1,0:T(8,128)(2,1)}, bf16[512,512]{1,0:T(8,128)(2,1)}, u32[]{:S(2)}, u32[]{:S(2)}) collective-permute-start(bf16[512,512]{1,0:T(8,128)(2,1)} %convolution_convert_fusion), channel_id=1, source_target_pairs={{0,16},{16,0},{1,17},{17,1},{2,18},{18,2},{3,19},{19,3},{4,20},{20... | collective-permute-start | bytes 1572872 | tf_op jit(solution)/shard_map/ppermute | solution.py:47
  104.4 1.0 copy-start.2
  105.3 0.9 copy-start.5
  106.2 4.0 %copy-start.7 = (bf16[512,1024]{1,0:T(8,128)(2,1)S(1)}, bf16[512,1024]{1,0:T(8,128)(2,1)}, u32[]{:S(2)}) copy-start(bf16[512,1024]{1,0:T(8,128)(2,1)} %copy-done.6) | copy-start | bytes 3145732
  134.8 17.0 %all-to-all-start.2 = ((bf16[8,64,512]{2,1,0:T(8,128)(2,1)}), bf16[8,64,512]{2,1,0:T(8,128)(2,1)S(1)}, u32[]{:S(2)}, u32[]{:S(2)}) async-start(bf16[8,64,512]{2,1,0:T(8,128)(2,1)} %broadcast_in_dim.9), calls=%async_computation.2 | async-start | bytes 1048576 | tf_op jit(solution)/shard_map/all_to_all | solution.py:52
  151.8 5.7 %collective-permute-start.21 = (bf16[512,512]{1,0:T(8,128)(2,1)S(1)}, bf16[512,512]{1,0:T(8,128)(2,1)S(1)}, u32[]{:S(2)}, u32[]{:S(2)}) collective-permute-start(bf16[512,512]{1,0:T(8,128)(2,1)S(1)} %bitcast.34), channel_id=1, source_target_pairs={{0,1},{1,0},{2,3},{3,2},{4,5},{5,4},{6,7},{7,6},{8,9},{9,8},{10,11... | collective-permute-start | bytes 1572872 | tf_op jit(solution)/shard_map/ppermute | solution.py:47
  156.1 14.4 %collective-permute-start.20 = (bf16[512,512]{1,0:T(8,128)(2,1)S(1)}, bf16[512,512]{1,0:T(8,128)(2,1)S(1)}, u32[]{:S(2)}, u32[]{:S(2)}) collective-permute-start(bf16[512,512]{1,0:T(8,128)(2,1)S(1)} %bitcast.35), channel_id=1, source_target_pairs={{0,16},{16,0},{1,17},{17,1},{2,18},{18,2},{3,19},{19,3},{4,20},{20... | collective-permute-start | bytes 1572872 | tf_op jit(solution)/shard_map/ppermute | solution.py:47
  170.5 1.9 collective-permute-start.22
